TPU v7x, 32 devices: a whole 2x2x4 slice. The times are simulated.
32 devices in a mesh: dp: 2 (over x), space: 16 (over z, y, core).
Axes of the slice: x: 2, y: 2, z: 4, core: 2. Of those that a mesh axis runs over, the one named last changes fastest.
Arguments:
- volumes: bfloat16 [2, 4, 128, 128, 128], P('dp', None, 'space'), may hold values from -6 to 6
- kernel_one: bfloat16 [16, 4, 3, 3, 3], replicated, may hold values from -0.625 to 0.625
- kernel_two: bfloat16 [32, 16, 3, 3, 3], replicated, may hold values from -0.3125 to 0.3125
- cotangent: bfloat16 [2, 32, 32, 1024], P('dp', None, None, 'space'), may hold values from -6 to 6
Outputs:
- output_two: bfloat16 [2, 32, 32, 1024], P('dp', None, None, 'space')
- grad_one: float32 [16, 4, 3, 3, 3], replicated
- grad_two: float32 [32, 16, 3, 3, 3], replicated
All inputs are finite; a program needn't handle non-finite values.
Results may differ from a plain program's by a relative error of at most 0.004.
The roundings to bfloat16 on the way count: a program that leaves them out, or rounds other values in their place, can miss the bound.
Values may be sent and summed in bfloat16 or wider, within the bound.
No kernel may reach another device: no remote copies, remote signals or barrier semaphores. Data moves between devices by JAX's collectives and lax.ppermute only.
A program may use at most 256 MiB of HBM per device.

v0:
```python
import functools
import math

import jax
import jax.numpy as jnp
from jax import lax
from jax.experimental import pallas as pl
from jax.experimental.pallas import tpu as pltpu
from jax.sharding import PartitionSpec as P

f32 = jnp.float32
bf16 = jnp.bfloat16

SLOPE = 0.3
BLOCKS = 4
HB = 32
CIN, C1, C2 = 4, 16, 32
W0, W1, W2 = 32, 16, 8
ROWS = BLOCKS * HB
LA, LH, LZ = W0 * CIN, W1 * C1, W2 * C2
WIDE = BLOCKS * LZ
TAPS = [(kd, kh) for kd in range(3) for kh in range(3)]
INPUT_ROWS = {(0, 0): 4, (0, 1): 0, (0, 2): 1, (1, 0): 1, (1, 1): 2, (1, 2): 3}


def dot(a, b):
    return jnp.dot(a, b, preferred_element_type=f32)


def dot_nt(a, b):
    return lax.dot_general(a, b, (((1,), (1,)), ((), ())), preferred_element_type=f32)


def dot_tn(a, b):
    return lax.dot_general(a, b, (((0,), (0,)), ((), ())), preferred_element_type=f32)


def exact_nt(a, b):
    return lax.dot_general(
        a, b, (((1,), (1,)), ((), ())), precision=lax.Precision.HIGHEST, preferred_element_type=f32
    )


def iotas(shape):
    return lax.broadcasted_iota(jnp.int32, shape, 0), lax.broadcasted_iota(jnp.int32, shape, 1)


def one_hot(mask):
    return jnp.where(mask, 1.0, 0.0).astype(bf16)


def width_order():
    r, q = iotas((CIN * 128, CIN * 128))
    return one_hot(r == (q % CIN) * 128 + (q // LA) * W0 + (q // CIN) % W0)


def height_order():
    r, q = iotas((5 * HB, 4 * HB))
    return one_hot(q == 4 * (r % HB) + jnp.where(r // HB == 4, -1, r // HB))


def channel_order():
    r, q = iotas((WIDE, WIDE))
    cells = BLOCKS * W2
    return one_hot(r == (q % cells) * C2 + q // cells)


def arrange_planes(planes, count, put):
    x = jnp.concatenate([planes(c) for c in range(CIN)], axis=1)
    y = dot(x, width_order()).astype(bf16)
    order = height_order()
    none = jnp.zeros((HB, LA), bf16)
    for d in range(count):
        z = dot(order, y[d * 128 : (d + 1) * 128]).astype(bf16)
        for v in range(5):
            here = [z[v * HB : (v + 1) * HB, b * LA : (b + 1) * LA] for b in range(BLOCKS)]
            own = jnp.concatenate(here, axis=0)
            before = jnp.concatenate([none] + here[:-1], axis=0)
            put(d, v, own, before)


def band(taps, rows, cin, cols, cout, put):
    r, q = iotas((rows, cols))
    w, o = r // cin, q // cout
    rel = w - 2 * o + 1
    last = (w == rows // cin - 1) & (o == 0)
    for tap in range(9):
        e = [taps(3 * tap + kw) for kw in range(3)]
        own = jnp.where(rel == 0, e[0], jnp.where(rel == 1, e[1], jnp.where(rel == 2, e[2], 0.0)))
        put(tap, own.astype(bf16), jnp.where(last, e[0], 0.0).astype(bf16))


def band_back(taps, rows, cout, cols, cin, put):
    r, q = iotas((rows, cols))
    w, o = q // cin, r // cout
    rel = w - 2 * o + 1
    last = (w == cols // cin - 1) & (o == 0)
    for tap in range(9):
        e = [taps(3 * tap + kw) for kw in range(3)]
        own = jnp.where(rel == 0, e[0], jnp.where(rel == 1, e[1], jnp.where(rel == 2, e[2], 0.0)))
        put(tap, own.astype(bf16), jnp.where(last, e[0], 0.0).astype(bf16))


def spread(k, cols):
    c, q = iotas((k.shape[1], cols))
    return dot(k, one_hot(q % k.shape[1] == c))


def prepare_kernel(vol_ref, k1_ref, k2_ref, k2t_ref, a_ref, t1_ref, t2_ref, t2b_ref, order_ref):
    count = a_ref.shape[0]

    def put_a(d, v, own, before):
        a_ref[d, v, :, :LA] = own
        a_ref[d, v, :, LA:] = before

    arrange_planes(lambda c: vol_ref[c].reshape(count * 128, 128), count, put_a)

    def puts(ref, half):
        def put(tap, own, other):
            ref[2 * half * tap : 2 * half * tap + half] = own
            ref[2 * half * tap + half : 2 * half * (tap + 1)] = other

        return put

    def tiled(k, each, times):
        return lambda t: jnp.concatenate([k[each * t : each * (t + 1)]] * times, axis=0)

    band(tiled(spread(k1_ref[...], LH), 16, LA // 16), LA, CIN, LH, C1, puts(t1_ref, LA))
    band(tiled(spread(k2_ref[...], LZ), C1, W1), LH, C1, LZ, C2, puts(t2_ref, LH))
    band_back(tiled(spread(k2t_ref[...], LH), C2, W2), LZ, C2, LH, C1, puts(t2b_ref, LZ))
    order_ref[...] = channel_order()


def shifted_down(x, keep):
    return jnp.where(keep, pltpu.roll(x.astype(f32), 1, 0), 0.0).astype(bf16)


def row_choice(d2, hl, depth):
    r, q = iotas((d2 * HB, hl * depth))
    plane, h2 = r // HB, r % HB
    return one_hot(q == (h2 % hl) * depth + (h2 // hl) * d2 + plane)


def forward_kernel(low_ref, a_ref, t1_ref, t2_ref, order_ref, cot_ref, alow_ref, hh_ref, send_ref, delta_ref):
    planes = hh_ref.shape[0]
    d2n = delta_ref.shape[0]
    depth = cot_ref.shape[0]
    hl = cot_ref.shape[1] // WIDE

    def put_a(d, v, own, before):
        alow_ref[d, v, :, :LA] = own
        alow_ref[d, v, :, LA:] = before

    arrange_planes(lambda c: low_ref[c].reshape(3 * 128, 128), 3, put_a)

    def rows_of(plane, v):
        return alow_ref[plane, v] if plane < 3 else a_ref[plane - 3, v]

    r, _ = iotas((planes * ROWS, LH))
    keep = r % HB != 0
    none = jnp.zeros((HB, LH), bf16)
    for p in range(2):
        cols = [
            jnp.concatenate([rows_of(2 * j + kd, INPUT_ROWS[p, kh]) for j in range(planes)], axis=0)
            for kd, kh in TAPS
        ]
        linear = dot(jnp.concatenate(cols, axis=1), t1_ref[...])
        hidden = jnp.where(linear > 0, linear, SLOPE * linear).astype(bf16)
        variants = [(1, hidden)] if p == 0 else [(2, hidden), (0, shifted_down(hidden, keep))]
        for v, x in variants:
            for j in range(planes):
                own = x[j * ROWS : (j + 1) * ROWS]
                hh_ref[j, v, :, :LH] = own
                hh_ref[j, v, :, LH:] = jnp.concatenate([none, own[:-HB]], axis=0)

    cols = [jnp.concatenate([hh_ref[2 * d + kd, kh] for d in range(d2n)], axis=0) for kd, kh in TAPS]
    linear = dot(jnp.concatenate(cols, axis=1), t2_ref[...])
    out = jnp.where(linear > 0, linear, SLOPE * linear).astype(bf16)

    def wide(x):
        return jnp.concatenate(
            [
                jnp.concatenate([x[d * ROWS + b * HB : d * ROWS + (b + 1) * HB] for b in range(BLOCKS)], axis=1)
                for d in range(d2n)
            ],
            axis=0,
        )

    choice = row_choice(d2n, hl, depth)
    by_channel = dot(wide(out), order_ref[...]).astype(bf16)
    sent = dot_tn(choice, by_channel).astype(bf16)
    for h in range(hl):
        send_ref[:, h * WIDE : (h + 1) * WIDE] = sent[h * depth : (h + 1) * depth]

    got = jnp.concatenate([cot_ref[:, h * WIDE : (h + 1) * WIDE] for h in range(hl)], axis=0)
    chosen = dot(choice, got).astype(bf16)
    cot = dot_nt(chosen, order_ref[...])
    for d in range(d2n):
        for b in range(BLOCKS):
            z = linear[d * ROWS + b * HB : d * ROWS + (b + 1) * HB]
            c = cot[d * HB : (d + 1) * HB, b * LZ : (b + 1) * LZ]
            delta_ref[d, b * HB : (b + 1) * HB] = (c * jnp.where(z > 0, 1.0, SLOPE)).astype(bf16)


def diagonals(g, first, cells, cout, cin):
    lanes = 2 * cells * cin
    _, q = iotas((cout, lanes))
    w = q // cin
    ahead = jnp.zeros((cout, lanes), f32)
    behind = jnp.where(w == 2 * cells - 1, g[:cout, first + lanes : first + 2 * lanes], 0.0)
    for o in range(cells):
        x = g[o * cout : (o + 1) * cout, first : first + lanes]
        ahead = jnp.where(w // 2 == o, x, ahead)
        if o:
            behind = jnp.where(w == 2 * o - 1, x, behind)
    return ahead, behind


def width_sums(g, cells, cout, cin):
    lanes = 2 * cells * cin
    both = [diagonals(g, 2 * lanes * tap, cells, cout, cin) for tap in range(9)]
    ahead = jnp.concatenate([x for x, _ in both], axis=0)
    behind = jnp.concatenate([x for _, x in both], axis=0)
    r, q = iotas((2 * cin, lanes))
    pick = jnp.where((q // cin % 2 == r // cin) & (q % cin == r % cin), 1.0, 0.0)
    pad = max(cin, 8)
    r, q = iotas((pad, lanes))
    every = jnp.where(q % cin == r, 1.0, 0.0)
    return exact_nt(pick, ahead), exact_nt(every, behind)


def second_gradient_kernel(hh_ref, delta_ref, out_ref):
    d2n = delta_ref.shape[0]
    delta = jnp.concatenate([delta_ref[d] for d in range(d2n)], axis=0)
    cols = [jnp.concatenate([hh_ref[2 * d + kd, kh] for d in range(d2n)], axis=0) for kd, kh in TAPS]
    g = dot_tn(delta, jnp.concatenate(cols, axis=1))
    ahead, behind = width_sums(g, W2, C2, C1)
    out_ref[: 2 * C1] = ahead
    out_ref[2 * C1 :] = behind


def first_gradient_kernel(hh_ref, delta_ref, next_ref, t2b_ref, alow_ref, a_ref, out_ref, dv_ref):
    d2n = delta_ref.shape[0]
    d1n = 2 * d2n
    r, _ = iotas((ROWS, LZ))
    keep = r % HB != HB - 1
    none = jnp.zeros((HB, LZ), bf16)
    for d in range(d2n + 1):
        x = delta_ref[d] if d < d2n else next_ref[...]
        up = jnp.where(keep, pltpu.roll(x.astype(f32), ROWS - 1, 0), 0.0).astype(bf16)
        for v, y in enumerate((x, up)):
            dv_ref[d, v, :, :LZ] = y
            dv_ref[d, v, :, LZ:] = jnp.concatenate([y[HB:], none], axis=0)

    def pulled(first, kd, kh):
        v = 1 if kh == 0 else 0
        lhs = jnp.concatenate([dv_ref[d + first, v] for d in range(d2n)], axis=0)
        tap = 3 * kd + kh
        return lhs, t2b_ref[2 * LZ * tap : 2 * LZ * (tap + 1)]

    def rows_of(plane, v):
        return alow_ref[plane, v] if plane < 3 else a_ref[plane - 3, v]

    deltas, cols = [], []
    for p in range(2):
        heights = (1,) if p == 0 else (2, 0)
        for even in range(2):
            depths = ((0, 2), (1, 0)) if even else ((0, 1),)
            terms = [pulled(first, kd, kh) for first, kd in depths for kh in heights]
            back = dot(
                jnp.concatenate([lhs for lhs, _ in terms], axis=1),
                jnp.concatenate([rhs for _, rhs in terms], axis=0),
            )
            planes = [2 * d + 1 + even for d in range(d2n)]
            hidden = jnp.concatenate([hh_ref[j, 2 if p else 1, :, :LH] for j in planes], axis=0)
            deltas.append((back * jnp.where(hidden.astype(f32) > 0, 1.0, SLOPE)).astype(bf16))
            cols.append(
                jnp.concatenate(
                    [
                        jnp.concatenate([rows_of(2 * j + kd, INPUT_ROWS[p, kh]) for j in planes], axis=0)
                        for kd, kh in TAPS
                    ],
                    axis=1,
                )
            )
    g = dot_tn(jnp.concatenate(deltas, axis=0), jnp.concatenate(cols, axis=0))
    ahead, behind = width_sums(g, W1, C1, CIN)
    out_ref[: 2 * CIN] = ahead
    out_ref[2 * CIN :] = behind


def gather_kernel(cot_ref, out_ref):
    channels, depth, cells = cot_ref.shape
    hl = cells // 32
    r, q = iotas((cells, hl * 128))
    for first in range(0, channels, 4):
        total = None
        for i in range(4):
            move = one_hot((q // 128 == r // 32) & (q % 128 == i * 32 + r % 32))
            part = dot(cot_ref[first + i], move)
            total = part if total is None else total + part
        for h in range(hl):
            at = h * WIDE + first * 32
            out_ref[:, at : at + 128] = total[:, h * 128 : (h + 1) * 128].astype(bf16)


def scatter_kernel(got_ref, out_ref):
    channels, depth, cells = out_ref.shape
    hl = cells // 32
    r, q = iotas((hl * 128, cells))
    for first in range(0, channels, 4):
        x = jnp.concatenate(
            [got_ref[:, h * WIDE + first * 32 : h * WIDE + first * 32 + 128] for h in range(hl)], axis=1
        )
        for i in range(4):
            move = one_hot((r // 128 == q // 32) & (r % 128 == i * 32 + q % 32))
            out_ref[first + i] = dot(x, move).astype(bf16)


def call(kernel, name, outs, *args, scratch=()):
    return pl.pallas_call(
        kernel,
        name=name,
        out_shape=[jax.ShapeDtypeStruct(shape, dtype) for shape, dtype in outs],
        scratch_shapes=list(scratch),
        compiler_params=pltpu.CompilerParams(vmem_limit_bytes=56 << 20),
    )(*args)


def passed_along(block, distance):
    devices = range(lax.axis_size("space"))
    return lax.ppermute(block, "space", [(i - distance, i) for i in devices if i - distance in devices])


def total_of(terms):
    count = lax.axis_size("dp") * lax.axis_size("space")
    step = 1
    while step < count:
        terms = terms + lax.ppermute(terms, ("dp", "space"), [(i, i ^ step) for i in range(count)])
        step *= 2
    return terms


def exchanged(rows):
    depth, lanes = rows.shape
    devices = lax.axis_size("space")
    blocks = rows.reshape(devices, depth // devices, lanes)
    return lax.all_to_all(blocks, "space", 0, 0, tiled=True).reshape(depth, lanes)


def local(volumes, kernel_one, kernel_two, cotangent):
    _, _, planes, height, _ = volumes.shape
    d1n, d2n = planes // 2, planes // 4
    _, _, depth, cells = cotangent.shape
    vol, cot = volumes[0], cotangent[0]

    low = passed_along(vol[:, -3:], 1)
    (cot_rows,) = call(gather_kernel, "gather", [((depth, cells * C2), bf16)], cot)
    cot_here = exchanged(cot_rows)

    k1 = kernel_one.transpose(2, 3, 4, 1, 0).reshape(27, 1, CIN, C1)
    k1 = jnp.broadcast_to(k1, (27, 16 // CIN, CIN, C1)).reshape(27 * 16, C1)
    k2 = kernel_two.transpose(2, 3, 4, 1, 0).reshape(27 * C1, C2)
    k2t = kernel_two.transpose(2, 3, 4, 0, 1).reshape(27 * C2, C1)
    a, t1, t2, t2b, order = call(
        prepare_kernel,
        "prepare",
        [
            ((planes, 5, ROWS, 2 * LA), bf16),
            ((9 * 2 * LA, LH), bf16),
            ((9 * 2 * LH, LZ), bf16),
            ((9 * 2 * LZ, LH), bf16),
            ((WIDE, WIDE), bf16),
        ],
        vol,
        k1,
        k2,
        k2t,
    )
    a_low, hh, send, delta = call(
        forward_kernel,
        "forward",
        [
            ((3, 5, ROWS, 2 * LA), bf16),
            ((d1n + 1, 3, ROWS, 2 * LH), bf16),
            ((depth, cells * C2), bf16),
            ((d2n, ROWS, LZ), bf16),
        ],
        low,
        a,
        t1,
        t2,
        order,
        cot_here,
    )
    delta_next = passed_along(delta[0], -1)
    got = exchanged(send)
    (term_two,) = call(second_gradient_kernel, "second_gradient", [((3 * C1, 9 * C2), f32)], hh, delta)
    (term_one,) = call(
        first_gradient_kernel,
        "first_gradient",
        [((16, 9 * C1), f32)],
        hh,
        delta,
        delta_next,
        t2b,
        a_low,
        a,
        scratch=[pltpu.VMEM((d2n + 1, 2, ROWS, 2 * LZ), bf16)],
    )
    terms = jnp.concatenate([term_two, jnp.pad(term_one, ((0, 0), (0, 9 * (C2 - C1))))], axis=0)
    (out,) = call(scatter_kernel, "scatter", [((C2, depth, cells), bf16)], got)
    totals = total_of(terms)

    count = volumes.shape[0] * lax.axis_size("dp")
    factor = 1.0 / math.sqrt(count * depth * (height // 4) ** 2)
    two = jnp.roll(totals[: 3 * C1].reshape(3, C1, 3, 3, C2), 1, axis=0) * factor
    one = totals[3 * C1 : 3 * C1 + 3 * CIN, : 9 * C1].reshape(3, CIN, 3, 3, C1)
    one = jnp.roll(one, 1, axis=0) * factor
    return (
        out[None],
        one.transpose(4, 1, 2, 3, 0),
        two.transpose(4, 1, 2, 3, 0),
    )


def solution(mesh):
    placed = (P("dp", None, "space", None, None), P(), P(), P("dp", None, None, "space"))
    return jax.shard_map(
        local,
        mesh=mesh,
        in_specs=placed,
        out_specs=(P("dp", None, None, "space"), P(), P()),
        check_vma=False,
    )
```

profile of v0, /device:TPU:0, one launch (start us, length us, event | category | flops | bytes accessed | tf_op | source)
XLA Modules:
  0.0 83.3 jit_solution(660852210279156947)
XLA Ops:
  0.6 1.0 %slice.50 = bf16[4,3,128,128]{3,2,1,0:T(8,128)(2,1)S(1)} slice(bf16[4,8,128,128]{3,2,1,0:T(8,128)(2,1)} %bitcast.18), slice={[0:4], [5:8], [0:128], [0:128]} | slice | bytes 786432 | tf_op jit(solution)/shard_map/slice | solution.py:357
  1.7 2.4 %collective-permute-start = (bf16[4,3,128,128]{3,2,1,0:T(8,128)(2,1)S(1)}, bf16[4,3,128,128]{3,2,1,0:T(8,128)(2,1)S(1)}, u32[]{:S(2)}, u32[]{:S(2)}) collective-permute-start(bf16[4,3,128,128]{3,2,1,0:T(8,128)(2,1)S(1)} %slice.50), channel_id=1, source_target_pairs={{0,1},{1,2},{2,3},{3,4},{4,5},{5,6},{6,7},{7,8},{8,9},{9,10},{10,1... | collective-permute-start | bytes 1179656 | tf_op jit(solution)/shard_map/ppermute | solution.py:332
  4.1 1.9 %gather.1 = bf16[32,2048]{1,0:T(8,128)(2,1)} custom-call(bf16[32,32,64]{2,1,0:T(8,128)(2,1)} %bitcast.24), custom_call_target="tpu_custom_call" | custom-call | tf_op jit(solution)/shard_map/gather/pallas_call | solution.py:321
  6.0 1.7 %reshape.38 = bf16[16,2,2048]{2,1,0:T(2,128)(2,1)} reshape(bf16[32,2048]{1,0:T(8,128)(2,1)} %gather.1) | data formatting | bytes 262144 | tf_op jit(solution)/shard_map/reshape | solution.py:347
  7.6 7.2 %all-to-all-start = ((bf16[16,2,2048]{2,1,0:T(2,128)(2,1)}), bf16[16,2,2048]{2,1,0:T(2,128)(2,1)S(1)}, u32[]{:S(2)}, u32[]{:S(2)}) async-start(bf16[16,2,2048]{2,1,0:T(2,128)(2,1)} %reshape.38), calls=%async_computation | async-start | bytes 262144 | tf_op jit(solution)/shard_map/all_to_all | solution.py:348
  14.8 1.7 %copy.12 = bf16[3,3,3,32,16]{4,3,2,1,0:T(8,128)(2,1)} copy(bf16[3,3,3,32,16]{3,4,2,1,0:T(8,128)(2,1)} %bitcast.22) | data formatting | bytes 55296 | tf_op jit(solution)/shard_map/transpose | solution.py:364
  16.5 1.4 %broadcast_in_dim.11 = bf16[27,4,4,16]{3,2,1,0:T(4,128)(2,1)} broadcast(bf16[27,4,16]{2,1,0:T(4,128)(2,1)} %bitcast.26), dimensions={0,2,3} | broadcast | bytes 17280 | tf_op jit(solution)/shard_map/broadcast_in_dim | solution.py:362
  17.9 7.9 %prepare.1 = (bf16[8,5,128,256]{3,2,1,0:T(8,128)(2,1)}, bf16[2304,256]{1,0:T(8,128)(2,1)}, bf16[4608,256]{1,0:T(8,128)(2,1)}, bf16[4608,256]{1,0:T(8,128)(2,1)}, bf16[1024,1024]{1,0:T(8,128)(2,1)}) custom-call(bf16[4,8,128,128]{3,2,1,0:T(8,128)(2,1)} %bitcast.19, bf16[432,16]{1,0:T(8,128)(2,1)} %bitcast.21, bf16[432,32]{1,0:T(8,128)(2,1)} %bitcast.23, ...), custom_call_target="tpu_custom_call" | custom-call | tf_op jit(solution)/shard_map/prepare/pallas_call | solution.py:321
  25.9 0.0 all-to-all-done
  25.9 0.7 reshape.39.cot_ref
  26.6 0.0 collective-permute-done.low_ref
  26.6 0.0 copy-start.1
  26.6 0.7 copy-done.1
  27.3 9.5 %forward.1 = (bf16[3,5,128,256]{3,2,1,0:T(8,128)(2,1)}, bf16[5,3,128,512]{3,2,1,0:T(8,128)(2,1)}, bf16[32,2048]{1,0:T(8,128)(2,1)}, bf16[2,128,256]{2,1,0:T(8,128)(2,1)}) custom-call(bf16[4,3,128,128]{3,2,1,0:T(8,128)(2,1)} %copy-done.1, bf16[8,5,128,256]{3,2,1,0:T(8,128)(2,1)} %get-tuple-element.12.a_ref, bf16[2304,256]{1,0:T(8,128)(2,1)} %get-tuple-element.13.t1_ref, ...), custom_call_target="tpu_custom_call" | custom-call | tf_op jit(solution)/shard_map/forward/pallas_call | solution.py:321
  36.9 0.8 %slice_bitcast_fusion = bf16[128,256]{1,0:T(8,128)(2,1)S(1)} fusion(bf16[2,128,256]{2,1,0:T(8,128)(2,1)} %get-tuple-element.18.delta_ref), kind=kLoop, calls=%fused_computation.6 | loop fusion | bytes 131072 | tf_op jit(solution)/shard_map/squeeze | solution.py:396
  37.7 1.3 %collective-permute-start.1 = (bf16[128,256]{1,0:T(8,128)(2,1)S(1)}, bf16[128,256]{1,0:T(8,128)(2,1)S(1)}, u32[]{:S(2)}, u32[]{:S(2)}) collective-permute-start(bf16[128,256]{1,0:T(8,128)(2,1)S(1)} %slice_bitcast_fusion), channel_id=1, source_target_pairs={{1,0},{2,1},{3,2},{4,3},{5,4},{6,5},{7,6},{8,7},{9,8},{10,9},{11,1... | collective-permute-start | bytes 196616 | tf_op jit(solution)/shard_map/ppermute | solution.py:332
  39.0 3.6 %second_gradient.1 = f32[48,288]{1,0:T(8,128)} custom-call(bf16[5,3,128,512]{3,2,1,0:T(8,128)(2,1)} %get-tuple-element.17.hh_ref, bf16[2,128,256]{2,1,0:T(8,128)(2,1)} %get-tuple-element.18.delta_ref), custom_call_target="tpu_custom_call" | custom-call | tf_op jit(solution)/shard_map/second_gradient/pallas_call | solution.py:321
  42.6 0.0 collective-permute-done.1.next_ref
  42.6 0.0 copy-start.3
  42.6 0.6 copy-done.3
  43.3 0.0 copy-start
  43.3 0.0 copy-start.2
  43.3 6.6 %first_gradient.1 = f32[16,144]{1,0:T(8,128)} custom-call(bf16[5,3,128,512]{3,2,1,0:T(8,128)(2,1)} %get-tuple-element.17.hh_ref, bf16[2,128,256]{2,1,0:T(8,128)(2,1)} %get-tuple-element.18.delta_ref, bf16[128,256]{1,0:T(8,128)(2,1)} %copy-done.3, bf16[4608,256]{1,0:T(8,128)(2,1)} %get-tuple-element.19.t2b_ref, ...), custom_call_target="tpu_custom_call" | custom-call | tf_op jit(solution)/shard_map/first_gradient/pallas_call | solution.py:321
  49.9 0.0 copy-done
  49.9 0.7 select_maximum_fusion
  50.6 1.1 %collective-permute-start.2 = (f32[64,288]{1,0:T(8,128)S(1)}, f32[64,288]{1,0:T(8,128)S(1)}, u32[]{:S(2)}, u32[]{:S(2)}) collective-permute-start(f32[64,288]{1,0:T(8,128)S(1)} %select_maximum_fusion), channel_id=1, source_target_pairs={{0,1},{1,0},{2,3},{3,2},{4,5},{5,4},{6,7},{7,6},{8,9},{9,8},{10,11... | collective-permute-start | bytes 221192 | tf_op jit(solution)/shard_map/ppermute | solution.py:339
  51.7 0.9 %collective-permute-done.2 = f32[64,288]{1,0:T(8,128)S(1)} collective-permute-done((f32[64,288]{1,0:T(8,128)S(1)}, f32[64,288]{1,0:T(8,128)S(1)}, u32[]{:S(2)}, u32[]{:S(2)}) %collective-permute-start.2) | collective-permute-done | bytes 73760 | tf_op jit(solution)/shard_map/ppermute | solution.py:339
  52.7 0.7 fusion.2
  53.4 2.6 %collective-permute-start.3 = (f32[64,288]{1,0:T(8,128)S(1)}, f32[64,288]{1,0:T(8,128)S(1)}, u32[]{:S(2)}, u32[]{:S(2)}) collective-permute-start(f32[64,288]{1,0:T(8,128)S(1)} %fusion.2), channel_id=1, source_target_pairs={{0,2},{1,3},{2,0},{3,1},{4,6},{5,7},{6,4},{7,5},{8,10},{9,11},{10,... | collective-permute-start | bytes 221192 | tf_op jit(solution)/shard_map/ppermute | solution.py:339
  56.0 0.0 copy-done.2
  56.0 0.8 reshape.40
  56.8 5.1 %all-to-all-start.1 = ((bf16[16,2,2048]{2,1,0:T(2,128)(2,1)}), bf16[16,2,2048]{2,1,0:T(2,128)(2,1)S(1)}, u32[]{:S(2)}, u32[]{:S(2)}) async-start(bf16[16,2,2048]{2,1,0:T(2,128)(2,1)} %reshape.40), calls=%async_computation.1 | async-start | bytes 262144 | tf_op jit(solution)/shard_map/all_to_all | solution.py:348
  61.9 0.0 collective-permute-done.3
  61.9 2.0 %collective-permute-start.4 = (f32[64,288]{1,0:T(8,128)S(1)}, f32[64,288]{1,0:T(8,128)S(1)}, u32[]{:S(2)}, u32[]{:S(2)}) collective-permute-start(f32[64,288]{1,0:T(8,128)S(1)} %add.18), channel_id=1, source_target_pairs={{0,4},{1,5},{2,6},{3,7},{4,0},{5,1},{6,2},{7,3},{8,12},{9,13},{10,... | collective-permute-start | bytes 221192 | tf_op jit(solution)/shard_map/ppermute | solution.py:339
  63.9 5.3 %collective-permute-done.4 = f32[64,288]{1,0:T(8,128)S(1)} collective-permute-done((f32[64,288]{1,0:T(8,128)S(1)}, f32[64,288]{1,0:T(8,128)S(1)}, u32[]{:S(2)}, u32[]{:S(2)}) %collective-permute-start.4) | collective-permute-done | bytes 73760 | tf_op jit(solution)/shard_map/ppermute | solution.py:339
  69.2 2.4 %collective-permute-start.5 = (f32[64,288]{1,0:T(8,128)S(1)}, f32[64,288]{1,0:T(8,128)S(1)}, u32[]{:S(2)}, u32[]{:S(2)}) collective-permute-start(f32[64,288]{1,0:T(8,128)S(1)} %add.19), channel_id=1, source_target_pairs={{0,8},{1,9},{2,10},{3,11},{4,12},{5,13},{6,14},{7,15},{8,0},{9,1},... | collective-permute-start | bytes 221192 | tf_op jit(solution)/shard_map/ppermute | solution.py:339
  71.7 5.0 %collective-permute-done.5 = f32[64,288]{1,0:T(8,128)S(1)} collective-permute-done((f32[64,288]{1,0:T(8,128)S(1)}, f32[64,288]{1,0:T(8,128)S(1)}, u32[]{:S(2)}, u32[]{:S(2)}) %collective-permute-start.5) | collective-permute-done | bytes 73760 | tf_op jit(solution)/shard_map/ppermute | solution.py:339
  76.7 1.6 %collective-permute-start.6 = (f32[64,288]{1,0:T(8,128)S(1)}, f32[64,288]{1,0:T(8,128)S(1)}, u32[]{:S(2)}, u32[]{:S(2)}) collective-permute-start(f32[64,288]{1,0:T(8,128)S(1)} %add.20), channel_id=1, source_target_pairs={{0,16},{1,17},{2,18},{3,19},{4,20},{5,21},{6,22},{7,23},{8,24},{9,... | collective-permute-start | bytes 221192 | tf_op jit(solution)/shard_map/ppermute | solution.py:339
  78.2 0.0 all-to-all-done.1
  78.2 0.7 reshape.41.got_ref
  78.9 2.1 %scatter.1 = bf16[32,32,64]{2,1,0:T(8,128)(2,1)} custom-call(bf16[32,2048]{1,0:T(8,128)(2,1)} %reshape.41.got_ref), custom_call_target="tpu_custom_call" | custom-call | tf_op jit(solution)/shard_map/scatter/pallas_call | solution.py:321
  81.1 0.3 collective-permute-done.6
  81.4 0.1 slice.43
  81.5 0.1 slice.45
  81.6 0.6 copy.13
  82.3 0.1 slice.47
  82.4 0.1 slice.49
  82.5 0.1 fusion
  82.6 0.7 copy.14
  (9 shorter events, 0.1 us)
Async XLA Ops:
  1.7 24.9 %collective-permute-start = (bf16[4,3,128,128]{3,2,1,0:T(8,128)(2,1)S(1)}, bf16[4,3,128,128]{3,2,1,0:T(8,128)(2,1)S(1)}, u32[]{:S(2)}, u32[]{:S(2)}) collective-permute-start(bf16[4,3,128,128]{3,2,1,0:T(8,128)(2,1)S(1)} %slice.50), channel_id=1, source_target_pairs={{0,1},{1,2},{2,3},{3,4},{4,5},{5,6},{6,7},{7,8},{8,9},{9,10},{10,1... | collective-permute-start | bytes 1179656 | tf_op jit(solution)/shard_map/ppermute | solution.py:332
  7.6 18.3 %all-to-all-start = ((bf16[16,2,2048]{2,1,0:T(2,128)(2,1)}), bf16[16,2,2048]{2,1,0:T(2,128)(2,1)S(1)}, u32[]{:S(2)}, u32[]{:S(2)}) async-start(bf16[16,2,2048]{2,1,0:T(2,128)(2,1)} %reshape.38), calls=%async_computation | async-start | bytes 262144 | tf_op jit(solution)/shard_map/all_to_all | solution.py:348
  26.6 0.7 copy-start.1
  37.7 4.9 %collective-permute-start.1 = (bf16[128,256]{1,0:T(8,128)(2,1)S(1)}, bf16[128,256]{1,0:T(8,128)(2,1)S(1)}, u32[]{:S(2)}, u32[]{:S(2)}) collective-permute-start(bf16[128,256]{1,0:T(8,128)(2,1)S(1)} %slice_bitcast_fusion), channel_id=1, source_target_pairs={{1,0},{2,1},{3,2},{4,3},{5,4},{6,5},{7,6},{8,7},{9,8},{10,9},{11,1... | collective-permute-start | bytes 196616 | tf_op jit(solution)/shard_map/ppermute | solution.py:332
  42.6 0.6 copy-start.3
  43.3 6.6 %copy-start = (f32[48,288]{1,0:T(8,128)S(1)}, f32[48,288]{1,0:T(8,128)}, u32[]{:S(2)}) copy-start(f32[48,288]{1,0:T(8,128)} %second_gradient.1) | copy-start | bytes 165892
  43.3 12.8 %copy-start.2 = (bf16[32,2048]{1,0:T(8,128)(2,1)S(1)}, bf16[32,2048]{1,0:T(8,128)(2,1)}, u32[]{:S(2)}) copy-start(bf16[32,2048]{1,0:T(8,128)(2,1)} %get-tuple-element.16) | copy-start | bytes 393220
  50.6 2.1 %collective-permute-start.2 = (f32[64,288]{1,0:T(8,128)S(1)}, f32[64,288]{1,0:T(8,128)S(1)}, u32[]{:S(2)}, u32[]{:S(2)}) collective-permute-start(f32[64,288]{1,0:T(8,128)S(1)} %select_maximum_fusion), channel_id=1, source_target_pairs={{0,1},{1,0},{2,3},{3,2},{4,5},{5,4},{6,7},{7,6},{8,9},{9,8},{10,11... | collective-permute-start | bytes 221192 | tf_op jit(solution)/shard_map/ppermute | solution.py:339
  53.4 8.5 %collective-permute-start.3 = (f32[64,288]{1,0:T(8,128)S(1)}, f32[64,288]{1,0:T(8,128)S(1)}, u32[]{:S(2)}, u32[]{:S(2)}) collective-permute-start(f32[64,288]{1,0:T(8,128)S(1)} %fusion.2), channel_id=1, source_target_pairs={{0,2},{1,3},{2,0},{3,1},{4,6},{5,7},{6,4},{7,5},{8,10},{9,11},{10,... | collective-permute-start | bytes 221192 | tf_op jit(solution)/shard_map/ppermute | solution.py:339
  56.8 21.5 %all-to-all-start.1 = ((bf16[16,2,2048]{2,1,0:T(2,128)(2,1)}), bf16[16,2,2048]{2,1,0:T(2,128)(2,1)S(1)}, u32[]{:S(2)}, u32[]{:S(2)}) async-start(bf16[16,2,2048]{2,1,0:T(2,128)(2,1)} %reshape.40), calls=%async_computation.1 | async-start | bytes 262144 | tf_op jit(solution)/shard_map/all_to_all | solution.py:348
  61.9 7.3 %collective-permute-start.4 = (f32[64,288]{1,0:T(8,128)S(1)}, f32[64,288]{1,0:T(8,128)S(1)}, u32[]{:S(2)}, u32[]{:S(2)}) collective-permute-start(f32[64,288]{1,0:T(8,128)S(1)} %add.18), channel_id=1, source_target_pairs={{0,4},{1,5},{2,6},{3,7},{4,0},{5,1},{6,2},{7,3},{8,12},{9,13},{10,... | collective-permute-start | bytes 221192 | tf_op jit(solution)/shard_map/ppermute | solution.py:339
  69.2 7.4 %collective-permute-start.5 = (f32[64,288]{1,0:T(8,128)S(1)}, f32[64,288]{1,0:T(8,128)S(1)}, u32[]{:S(2)}, u32[]{:S(2)}) collective-permute-start(f32[64,288]{1,0:T(8,128)S(1)} %add.19), channel_id=1, source_target_pairs={{0,8},{1,9},{2,10},{3,11},{4,12},{5,13},{6,14},{7,15},{8,0},{9,1},... | collective-permute-start | bytes 221192 | tf_op jit(solution)/shard_map/ppermute | solution.py:339
  76.7 4.7 %collective-permute-start.6 = (f32[64,288]{1,0:T(8,128)S(1)}, f32[64,288]{1,0:T(8,128)S(1)}, u32[]{:S(2)}, u32[]{:S(2)}) collective-permute-start(f32[64,288]{1,0:T(8,128)S(1)} %add.20), channel_id=1, source_target_pairs={{0,16},{1,17},{2,18},{3,19},{4,20},{5,21},{6,22},{7,23},{8,24},{9,... | collective-permute-start | bytes 221192 | tf_op jit(solution)/shard_map/ppermute | solution.py:339
where the time goes:
time: 84 us; the launch traced here: 83.3 us
  Pallas kernels  31.7 us (38%)
  starting transfers between devices  25.7 us (31%)
  local copies, waits for them, and re-layouts  12 us (14%)
  waiting for transfers between devices  11.6 us (14%)
  other arithmetic  1.63 us (2%)
    pallas_call x6, Pallas kernels, call(): pl.pallas_call(kernel, name=name, out_shape=[jax.ShapeDtypeStruct(shape,...  31.7 us
    all_to_all x2, starting transfers between devices, exchanged(): lax.all_to_all(blocks, 'space', 0, 0, tiled=True).reshape(depth, lanes)  12.3 us
    ppermute x5, waiting for transfers between devices, total_of(): lax.ppermute(terms, ('dp', 'space'), [(i, i ^ step) for i in range(count)])  11.6 us
    ppermute x5, starting transfers between devices, total_of(): lax.ppermute(terms, ('dp', 'space'), [(i, i ^ step) for i in range(count)])  9.7 us
    ppermute x2, starting transfers between devices, passed_along(): lax.ppermute(block, 'space', [(i - distance, i) for i in devices if i - d...  3.66 us
    unnamed x10, local copies, waits for them, and re-layouts  2.72 us
    reshape x2, local copies, waits for them, and re-layouts, exchanged(): blocks = rows.reshape(devices, depth // devices, lanes)  2.42 us
    transpose x1, local copies, waits for them, and re-layouts, local(): k2t = kernel_two.transpose(2, 3, 4, 0, 1).reshape(27 * C2, C1)  1.71 us
  transfers between devices with their start and end apart: 9, of which 4 were waited for; matrix products, arithmetic and copies ran while one was open for 8% of the time, Pallas kernels for 19%

commit v1 on v0

v1 whole, which is shorter than its diff:
```python
import functools
import math

import jax
import jax.numpy as jnp
from jax import lax
from jax.experimental import pallas as pl
from jax.experimental.pallas import tpu as pltpu
from jax.sharding import PartitionSpec as P

f32 = jnp.float32
bf16 = jnp.bfloat16

SLOPE = 0.3
BLOCKS = 4
HB = 32
CIN, C1, C2 = 4, 16, 32
W0, W1, W2 = 32, 16, 8
ROWS = BLOCKS * HB
LA, LH, LZ = W0 * CIN, W1 * C1, W2 * C2
WIDE = BLOCKS * LZ
TAPS = [(kd, kh) for kd in range(3) for kh in range(3)]
INPUT_ROWS = {(0, 0): 4, (0, 1): 0, (0, 2): 1, (1, 0): 1, (1, 1): 2, (1, 2): 3}


def dot(a, b):
    return jnp.dot(a, b, preferred_element_type=f32)


def dot_nt(a, b):
    return lax.dot_general(a, b, (((1,), (1,)), ((), ())), preferred_element_type=f32)


def dot_tn(a, b):
    return lax.dot_general(a, b, (((0,), (0,)), ((), ())), preferred_element_type=f32)


def exact_nt(a, b):
    return lax.dot_general(
        a, b, (((1,), (1,)), ((), ())), precision=lax.Precision.HIGHEST, preferred_element_type=f32
    )


def iotas(shape):
    return lax.broadcasted_iota(jnp.int32, shape, 0), lax.broadcasted_iota(jnp.int32, shape, 1)


def one_hot(mask):
    return jnp.where(mask, 1.0, 0.0).astype(bf16)


def width_order():
    r, q = iotas((CIN * 128, CIN * 128))
    return one_hot(r == (q % CIN) * 128 + (q // LA) * W0 + (q // CIN) % W0)


def height_order():
    r, q = iotas((5 * HB, 4 * HB))
    return one_hot(q == 4 * (r % HB) + jnp.where(r // HB == 4, -1, r // HB))


def channel_order():
    r, q = iotas((WIDE, WIDE))
    cells = BLOCKS * W2
    return one_hot(r == (q % cells) * C2 + q // cells)


def arrange_planes(planes, count, put):
    x = jnp.concatenate([planes(c) for c in range(CIN)], axis=1)
    y = dot(x, width_order()).astype(bf16)
    order = height_order()
    for d in range(count):
        z = dot(order, y[d * 128 : (d + 1) * 128]).astype(bf16)
        for v in range(5):
            put(d, v, [z[v * HB : (v + 1) * HB, b * LA : (b + 1) * LA] for b in range(BLOCKS)])


def with_before(x):
    return jnp.concatenate([x, jnp.concatenate([jnp.zeros_like(x[:HB]), x[:-HB]], axis=0)], axis=1)


def band(taps, rows, cin, cols, cout, put):
    r, q = iotas((rows, cols))
    w, o = r // cin, q // cout
    rel = w - 2 * o + 1
    last = (w == rows // cin - 1) & (o == 0)
    for tap in range(9):
        e = [taps(3 * tap + kw) for kw in range(3)]
        own = jnp.where(rel == 0, e[0], jnp.where(rel == 1, e[1], jnp.where(rel == 2, e[2], 0.0)))
        put(tap, own.astype(bf16), jnp.where(last, e[0], 0.0).astype(bf16))


def band_back(taps, rows, cout, cols, cin, put):
    r, q = iotas((rows, cols))
    w, o = q // cin, r // cout
    rel = w - 2 * o + 1
    last = (w == cols // cin - 1) & (o == 0)
    for tap in range(9):
        e = [taps(3 * tap + kw) for kw in range(3)]
        own = jnp.where(rel == 0, e[0], jnp.where(rel == 1, e[1], jnp.where(rel == 2, e[2], 0.0)))
        put(tap, own.astype(bf16), jnp.where(last, e[0], 0.0).astype(bf16))


def spread(k, cols):
    c, q = iotas((k.shape[1], cols))
    return dot(k, one_hot(q % k.shape[1] == c))


def spread_back(k2):
    r, q = iotas((C2, C2))
    flipped = dot_nt(one_hot(r == q), k2).astype(bf16)
    flipped = jnp.concatenate([flipped, jnp.zeros((C2, 512 - 27 * C1), bf16)], axis=1)
    stacked = jnp.concatenate([flipped[:, 128 * i : 128 * (i + 1)] for i in range(4)], axis=0)
    r, q = iotas((128, LH))
    parts = [dot(stacked, one_hot((r // C1 == g) & (q % C1 == r % C1))) for g in range(8)]
    return lambda t: parts[t % 8][C2 * (t // 8) : C2 * (t // 8 + 1)]


def shifted_down(x, keep):
    return jnp.where(keep, pltpu.roll(x.astype(f32), 1, 0), 0.0).astype(bf16)


def travel_order(r, depth, d2n, hl):
    groups = hl * C2 // 4
    return (r // d2n) % groups, r // (groups * d2n) * d2n + r % d2n


def by_height(r, d2n):
    group, plane, h2 = r // (d2n * HB), (r // HB) % d2n, r % HB
    return (h2 * (C2 // 4) + group) * d2n + plane


def puts(ref, half):
    def put(tap, own, other):
        ref[2 * half * tap : 2 * half * tap + half] = own
        ref[2 * half * tap + half : 2 * half * (tap + 1)] = other

    return put


def tiled(each, times):
    return lambda t: jnp.concatenate([each(t)] * times, axis=0)


def forward_kernel(
    vol_ref, low_ref, k1_ref, k2_ref, order_ref, a_ref, hh_ref, send_ref, slope_ref, own_ref, t1_ref, t2_ref, sem
):
    count = vol_ref.shape[1]
    planes = hh_ref.shape[0]
    d2n = slope_ref.shape[0]
    copy = pltpu.make_async_copy(vol_ref, own_ref, sem)
    copy.start()

    def put_from(first):
        def put(d, v, blocks):
            for b, x in enumerate(blocks):
                a_ref[first + d, v, b * HB : (b + 1) * HB] = x

        return put

    arrange_planes(lambda c: low_ref[c].reshape(3 * 128, 128), 3, put_from(0))
    k1 = jnp.concatenate([k1_ref[t].astype(f32) for t in range(27) for _ in range(16 // CIN)], axis=0)
    k1 = spread(k1.astype(bf16), LH)
    band(tiled(lambda t: k1[16 * t : 16 * (t + 1)], LA // 16), LA, CIN, LH, C1, puts(t1_ref, LA))
    k2 = spread(k2_ref[...], LZ)
    band(tiled(lambda t: k2[C1 * t : C1 * (t + 1)], W1), LH, C1, LZ, C2, puts(t2_ref, LH))
    copy.wait()
    arrange_planes(lambda c: own_ref[c].reshape(count * 128, 128), count, put_from(3))

    r, _ = iotas((planes * ROWS, LH))
    keep = r % HB != 0
    for p in range(2):
        cols = [
            jnp.concatenate([with_before(a_ref[2 * j + kd, INPUT_ROWS[p, kh]]) for j in range(planes)], axis=0)
            for kd, kh in TAPS
        ]
        linear = dot(jnp.concatenate(cols, axis=1), t1_ref[...])
        hidden = jnp.where(linear > 0, linear, SLOPE * linear).astype(bf16)
        variants = [(1, hidden)] if p == 0 else [(2, hidden), (0, shifted_down(hidden, keep))]
        for v, x in variants:
            for j in range(planes):
                hh_ref[j, v] = x[j * ROWS : (j + 1) * ROWS]

    linear = dot(second_layer_columns(hh_ref, d2n), t2_ref[...])
    out = jnp.where(linear > 0, linear, SLOPE * linear).astype(bf16)
    positive = jnp.where(linear > 0, 1.0, 0.0).astype(bf16)
    for d in range(d2n):
        slope_ref[d] = positive[d * ROWS : (d + 1) * ROWS]
    wide = jnp.concatenate(
        [
            jnp.concatenate([out[d * ROWS + b * HB : d * ROWS + (b + 1) * HB] for b in range(BLOCKS)], axis=1)
            for d in range(d2n)
        ],
        axis=0,
    )
    groups = C2 // 4
    by_channel = dot(wide, order_ref[...]).astype(bf16)
    stacked = jnp.concatenate([by_channel[:, 128 * g : 128 * (g + 1)] for g in range(groups)], axis=0)
    r, q = iotas((stacked.shape[0], stacked.shape[0]))
    send_ref[...] = dot(one_hot(r == by_height(q, d2n)), stacked).astype(bf16)


def second_layer_columns(hh_ref, d2n):
    cols = [jnp.concatenate([with_before(hh_ref[2 * d + kd, kh]) for d in range(d2n)], axis=0) for kd, kh in TAPS]
    return jnp.concatenate(cols, axis=1)


def delta_kernel(cot_ref, slope_ref, delta_ref):
    d2n = delta_ref.shape[0]
    count = cot_ref.shape[0]
    r, q = iotas((count, count))
    got = dot(one_hot(q == by_height(r, d2n)), cot_ref[...])
    for d in range(d2n):
        for b in range(BLOCKS):
            at = [((2 * b + i) * d2n + d) * HB for i in range(2)]
            c = jnp.concatenate([got[i : i + HB] for i in at], axis=1)
            slope = jnp.where(slope_ref[d, b * HB : (b + 1) * HB].astype(f32) > 0, 1.0, SLOPE)
            delta_ref[d, b * HB : (b + 1) * HB] = (c * slope).astype(bf16)


def diagonals(g, first, cells, cout, cin):
    lanes = 2 * cells * cin
    _, q = iotas((cout, lanes))
    w = q // cin
    ahead = jnp.zeros((cout, lanes), f32)
    behind = jnp.where(w == 2 * cells - 1, g[:cout, first + lanes : first + 2 * lanes], 0.0)
    for o in range(cells):
        x = g[o * cout : (o + 1) * cout, first : first + lanes]
        ahead = jnp.where(w // 2 == o, x, ahead)
        if o:
            behind = jnp.where(w == 2 * o - 1, x, behind)
    return ahead, behind


def width_sums(g, cells, cout, cin, place):
    lanes = 2 * cells * cin
    both = [diagonals(g, 2 * lanes * tap, cells, cout, cin) for tap in range(9)]
    ahead, behind = place([x for x, _ in both]), place([x for _, x in both])
    r, q = iotas((2 * cin, lanes))
    pick = jnp.where((q // cin % 2 == r // cin) & (q % cin == r % cin), 1.0, 0.0)
    r, q = iotas((max(cin, 8), lanes))
    every = jnp.where(q % cin == r, 1.0, 0.0)
    return [jnp.concatenate([exact_nt(pick, x), exact_nt(every, y)], axis=0) for x, y in zip(ahead, behind)]


def second_gradient_kernel(hh_ref, delta_ref, k2_ref, out_ref, t2b_ref):
    d2n = delta_ref.shape[0]
    band_back(tiled(spread_back(k2_ref[...]), W2), LZ, C2, LH, C1, puts(t2b_ref, LZ))
    delta = jnp.concatenate([delta_ref[d] for d in range(d2n)], axis=0)
    g = dot_tn(delta, second_layer_columns(hh_ref, d2n))
    none = [jnp.zeros((3 * C2, LH), f32)]
    (sums,) = width_sums(g, W2, C2, C1, lambda taps: [jnp.concatenate(taps + none, axis=0)])
    out_ref[...] = sums


def first_gradient_kernel(hh_ref, delta_ref, next_ref, t2b_ref, a_ref, two_ref, out_ref, dv_ref):
    d2n = delta_ref.shape[0]
    r, _ = iotas((ROWS, LZ))
    keep = r % HB != HB - 1
    none = jnp.zeros((HB, LZ), bf16)
    for d in range(d2n + 1):
        x = delta_ref[d] if d < d2n else next_ref[...]
        up = jnp.where(keep, pltpu.roll(x.astype(f32), ROWS - 1, 0), 0.0).astype(bf16)
        for v, y in enumerate((x, up)):
            dv_ref[d, v, :, :LZ] = y
            dv_ref[d, v, :, LZ:] = jnp.concatenate([y[HB:], none], axis=0)

    def pulled(first, kd, kh):
        v = 1 if kh == 0 else 0
        lhs = jnp.concatenate([dv_ref[d + first, v] for d in range(d2n)], axis=0)
        tap = 3 * kd + kh
        return lhs, t2b_ref[2 * LZ * tap : 2 * LZ * (tap + 1)]

    deltas, cols = [], []
    for p in range(2):
        heights = (1,) if p == 0 else (2, 0)
        for even in range(2):
            depths = ((0, 2), (1, 0)) if even else ((0, 1),)
            terms = [pulled(first, kd, kh) for first, kd in depths for kh in heights]
            back = dot(
                jnp.concatenate([lhs for lhs, _ in terms], axis=1),
                jnp.concatenate([rhs for _, rhs in terms], axis=0),
            )
            planes = [2 * d + 1 + even for d in range(d2n)]
            hidden = jnp.concatenate([hh_ref[j, 2 if p else 1] for j in planes], axis=0)
            deltas.append((back * jnp.where(hidden.astype(f32) > 0, 1.0, SLOPE)).astype(bf16))
            cols.append(
                jnp.concatenate(
                    [
                        jnp.concatenate([with_before(a_ref[2 * j + kd, INPUT_ROWS[p, kh]]) for j in planes], axis=0)
                        for kd, kh in TAPS
                    ],
                    axis=1,
                )
            )
    g = dot_tn(jnp.concatenate(deltas, axis=0), jnp.concatenate(cols, axis=0))
    before, after = [jnp.zeros((C2, LA), f32)], [jnp.zeros((128 - C2 - 3 * C1, LA), f32)]

    def place(taps):
        return [jnp.concatenate(before + taps[i : i + 3] + after, axis=0) for i in range(0, 9, 3)]

    sums = jnp.concatenate(width_sums(g, W1, C1, CIN, place), axis=0)
    out_ref[: 3 * C1] = two_ref[:, :128]
    out_ref[3 * C1 : 6 * C1] = two_ref[:, 128:256]
    out_ref[6 * C1 :] = two_ref[:, 256:] + sums


def scale_kernel(factor, sum_ref, one_ref, two_ref):
    place = (2, 0, 1)
    for tap in range(9):
        for kw in range(3):
            r, q = 3 * C1 * (tap // 4) + C1 * place[kw], C2 * (tap % 4)
            two_ref[3 * tap + kw] = sum_ref[r : r + C1, q : q + C2] * factor
            r, q = 6 * C1 + C1 * (tap // 3) + CIN * place[kw], C2 + C1 * (tap % 3)
            one_ref[3 * tap + kw] = sum_ref[r : r + CIN, q : q + C1] * factor


def gather_kernel(vol_ref, cot_ref, low_ref, out_ref, order_ref, own_ref, sems):
    planes = vol_ref.shape[1]
    d2n = planes // 4
    copies = [
        pltpu.make_async_copy(cot_ref, own_ref, sems.at[0]),
        pltpu.make_async_copy(vol_ref.at[:, planes - 3 :], low_ref, sems.at[1]),
    ]
    for copy in copies:
        copy.start()
    channels, depth, cells = cot_ref.shape
    hl = cells // 32
    order_ref[...] = channel_order()
    r, q = iotas((cells, hl * 128))
    moves = [one_hot((q // 128 == r // 32) & (q % 128 == i * 32 + r % 32)) for i in range(4)]
    copies[0].wait()
    groups = []
    for first in range(0, channels, 4):
        parts = [dot(own_ref[first + i], moves[i]) for i in range(4)]
        groups.append(((parts[0] + parts[1]) + (parts[2] + parts[3])).astype(bf16))
    x = jnp.concatenate(
        [jnp.concatenate([g[:, h * 128 : (h + 1) * 128] for g in groups], axis=1) for h in range(hl)], axis=0
    )
    x = dot_nt(x, order_ref[...]).astype(bf16)
    rows = [x[h * depth : (h + 1) * depth, 128 * g : 128 * (g + 1)] for h in range(hl) for g in range(8)]
    count = len(rows) * depth
    r, q = iotas((count, count))
    row, plane = travel_order(r, depth, d2n, hl)
    out_ref[...] = dot(one_hot(q == row * depth + plane), jnp.concatenate(rows, axis=0)).astype(bf16)
    copies[1].wait()


def scatter_kernel(d2n, got_ref, out_ref):
    channels, depth, cells = out_ref.shape
    hl = cells // 32
    count = got_ref.shape[0]
    r, q = iotas((count, count))
    row, plane = travel_order(q, depth, d2n, hl)
    got = dot(one_hot(r == row * depth + plane), got_ref[...]).astype(bf16)
    r, q = iotas((hl * 128, cells))
    moves = [one_hot((r // 128 == q // 32) & (r % 128 == i * 32 + q % 32)) for i in range(4)]
    groups = channels // 4
    for g in range(groups):
        x = jnp.concatenate(
            [got[(h * groups + g) * depth : (h * groups + g + 1) * depth] for h in range(hl)], axis=1
        )
        for i in range(4):
            out_ref[4 * g + i] = dot(x, moves[i]).astype(bf16)


def call(kernel, name, outs, *args, scratch=(), apart=()):
    return pl.pallas_call(
        kernel,
        name=name,
        in_specs=[pl.BlockSpec(memory_space=pltpu.HBM if i in apart else pltpu.VMEM) for i in range(len(args))],
        out_specs=[pl.BlockSpec(memory_space=pltpu.VMEM) for _ in outs],
        out_shape=[jax.ShapeDtypeStruct(shape, dtype) for shape, dtype in outs],
        scratch_shapes=list(scratch),
        compiler_params=pltpu.CompilerParams(vmem_limit_bytes=32 << 20),
    )(*args)


def passed_along(block, distance):
    devices = range(lax.axis_size("space"))
    return lax.ppermute(block, "space", [(i - distance, i) for i in devices if i - distance in devices])


def with_partner(block, bit):
    count = lax.axis_size("dp") * lax.axis_size("space")
    return lax.ppermute(block, ("dp", "space"), [(i, i ^ bit) for i in range(count)])


def total_and_exchange(terms, rows):
    devices = lax.axis_size("space")
    here = lax.axis_index("space")
    count = rows.shape[0] // devices
    blocks = rows.reshape(devices, count, 128)
    half = terms.shape[0] // 2
    first, second = rows.shape[0] // 2, rows.shape[0] // 2 + half
    even = here % 2 == 0
    bit = 1
    while bit < devices:
        mine = (here // bit) % 2 == 0
        pairs = blocks.reshape(devices // (2 * bit), 2, bit, count, 128)
        kept = jnp.where(mine, pairs[:, 0], pairs[:, 1])
        sent = jnp.where(mine, pairs[:, 1], pairs[:, 0]).reshape(first, 128)
        high = lax.reduce_precision(terms, 8, 7)
        rest = lax.reduce_precision(terms - high, 8, 7)
        if bit == 1:
            stay = jnp.where(even, terms[:half], terms[half:])
            high, rest = (jnp.where(even, x[half:], x[:half]) for x in (high, rest))
        else:
            stay = high + rest
        got = with_partner(jnp.concatenate([sent, high.astype(bf16), rest.astype(bf16)], axis=0), bit)
        terms = stay + (got[first:second].astype(f32) + got[second:].astype(f32))
        came = got[:first].reshape(kept.shape)
        blocks = jnp.where(mine, jnp.stack([kept, came], 1), jnp.stack([came, kept], 1))
        bit *= 2
    while bit < devices * lax.axis_size("dp"):
        terms = terms + with_partner(terms, bit)
        bit *= 2
    other = with_partner(terms, 1)
    terms = jnp.where(even, jnp.concatenate([terms, other], 0), jnp.concatenate([other, terms], 0))
    return terms, blocks.reshape(rows.shape)


def exchanged(rows):
    devices = lax.axis_size("space")
    blocks = rows.reshape(devices, rows.shape[0] // devices, 128)
    return lax.all_to_all(blocks, "space", 0, 0, tiled=True).reshape(rows.shape)


def local(volumes, kernel_one, kernel_two, cotangent):
    _, _, planes, height, width = volumes.shape
    d1n, d2n = planes // 2, planes // 4
    _, _, depth, cells = cotangent.shape
    vol, cot = volumes[0], cotangent[0]
    travelling = depth * (cells // 32) * (C2 // 4)

    low, cot_rows, order = call(
        gather_kernel,
        "gather",
        [((CIN, 3, height, width), bf16), ((travelling, 128), bf16), ((WIDE, WIDE), bf16)],
        vol,
        cot,
        scratch=[pltpu.VMEM(cot.shape, bf16), pltpu.SemaphoreType.DMA((2,))],
        apart=(0, 1),
    )
    low = passed_along(low, 1)
    cot_here = exchanged(cot_rows)

    k1 = kernel_one.transpose(2, 3, 4, 1, 0).reshape(27, CIN, C1)
    k2 = kernel_two.transpose(2, 3, 4, 1, 0).reshape(27 * C1, C2)
    a, hh, send, slope = call(
        forward_kernel,
        "forward",
        [
            ((planes + 3, 5, ROWS, LA), bf16),
            ((d1n + 1, 3, ROWS, LH), bf16),
            ((travelling, 128), bf16),
            ((d2n, ROWS, LZ), bf16),
        ],
        vol,
        low,
        k1,
        k2,
        order,
        scratch=[
            pltpu.VMEM(vol.shape, bf16),
            pltpu.VMEM((9 * 2 * LA, LH), bf16),
            pltpu.VMEM((9 * 2 * LH, LZ), bf16),
            pltpu.SemaphoreType.DMA,
        ],
        apart=(0,),
    )
    (delta,) = call(delta_kernel, "delta", [((d2n, ROWS, LZ), bf16)], cot_here, slope)
    delta_next = passed_along(delta[0], -1)
    term_two, t2b = call(
        second_gradient_kernel,
        "second_gradient",
        [((3 * C1, 384), f32), ((9 * 2 * LZ, LH), bf16)],
        hh,
        delta,
        k2,
    )
    (terms,) = call(
        first_gradient_kernel,
        "first_gradient",
        [((9 * C1, 128), f32)],
        hh,
        delta,
        delta_next,
        t2b,
        a,
        term_two,
        scratch=[pltpu.VMEM((d2n + 1, 2, ROWS, 2 * LZ), bf16)],
    )
    terms, got = total_and_exchange(terms, send)
    (out,) = call(functools.partial(scatter_kernel, d2n), "scatter", [((C2, depth, cells), bf16)], got)
    count = volumes.shape[0] * lax.axis_size("dp")
    factor = 1.0 / math.sqrt(count * depth * (height // 4) ** 2)
    one, two = call(
        functools.partial(scale_kernel, factor),
        "scale",
        [((27, CIN, C1), f32), ((27, C1, C2), f32)],
        terms,
    )
    return (
        out[None],
        one.reshape(3, 3, 3, CIN, C1).transpose(4, 3, 0, 1, 2),
        two.reshape(3, 3, 3, C1, C2).transpose(4, 3, 0, 1, 2),
    )


def solution(mesh):
    placed = (P("dp", None, "space", None, None), P(), P(), P("dp", None, None, "space"))
    return jax.shard_map(
        local,
        mesh=mesh,
        in_specs=placed,
        out_specs=(P("dp", None, None, "space"), P(), P()),
        check_vma=False,
    )
```

time: 84 us -> 60.6 us (0.72)
  Pallas kernels: 31.7 us -> 15.6 us
  local copies, waits for them, and re-layouts: 12 us -> 8.05 us
  starting transfers between devices: 25.7 us -> 22.4 us
  other arithmetic: 1.63 us -> 0.34 us
  waiting for transfers between devices: 11.6 us -> 12.8 us
    pallas_call x6 -> x7, Pallas kernels: 31.7 us -> 15.6 us  [call(): pl.pallas_call(kernel, name=name, in_specs=[pl.BlockSpec(memory_space=plt...]
    unnamed x10 -> x20, local copies, waits for them, and re-layouts: 2.72 us -> 8 us
    all_to_all x2 -> x1, starting transfers between devices: 12.3 us -> 7.2 us  [exchanged(): return lax.all_to_all(blocks, 'space', 0, 0, tiled=True).reshape(rows.shape)]
    reshape x4 -> x0, local copies, waits for them, and re-layouts: 3.83 us -> none  [the longest x2 2.42 us: exchanged(): blocks = rows.reshape(devices, depth // devices, lanes)]
    transpose x1 -> x0, local copies, waits for them, and re-layouts: 1.71 us -> none  [local(): k2t = kernel_two.transpose(2, 3, 4, 0, 1).reshape(27 * C2, C1)]
    ppermute x5 -> x6, starting transfers between devices: 9.7 us -> 11.2 us  [with_partner(): lax.ppermute(block, ('dp', 'space'), [(i, i ^ bit) for i in range(count)])]
    slice x9 -> x4, local copies, waits for them, and re-layouts: 1.44 us -> 0.02 us  [total_and_exchange(): came = got[:first].reshape(kept.shape)]
    broadcast_in_dim x1 -> x0, local copies, waits for them, and re-layouts: 1.41 us -> none  [local(): k1 = jnp.broadcast_to(k1, (27, 16 // CIN, CIN, C1)).reshape(27 * 16, C1)]
  transfers between devices with their start and end apart: 9 -> 9, of which waited for: 4 -> 5; matrix products, arithmetic and copies ran while one was open for 8% -> 0% of each run, Pallas kernels for 19% -> 15%
where the time goes in v1:
time: 60.6 us; the launch traced here: 60.2 us
  starting transfers between devices  22.4 us (37%)
  Pallas kernels  15.6 us (26%)
  waiting for transfers between devices  12.8 us (21%)
  local copies, waits for them, and re-layouts  8.05 us (13%)
  between operations  0.94 us (2%)
    pallas_call x7, Pallas kernels, call(): pl.pallas_call(kernel, name=name, in_specs=[pl.BlockSpec(memory_space=plt...  15.6 us
    ppermute x6, waiting for transfers between devices, with_partner(): lax.ppermute(block, ('dp', 'space'), [(i, i ^ bit) for i in range(count)])  12.8 us
    ppermute x6, starting transfers between devices, with_partner(): lax.ppermute(block, ('dp', 'space'), [(i, i ^ bit) for i in range(count)])  11.2 us
    unnamed x20, local copies, waits for them, and re-layouts  8 us
    all_to_all x1, starting transfers between devices, exchanged(): return lax.all_to_all(blocks, 'space', 0, 0, tiled=True).reshape(rows.shape)  7.2 us
    ppermute x2, starting transfers between devices, passed_along(): lax.ppermute(block, 'space', [(i - distance, i) for i in devices if i - d...  3.97 us
  transfers between devices with their start and end apart: 9, of which 5 were waited for; matrix products, arithmetic and copies ran while one was open for 0% of the time, Pallas kernels for 15%

profile of v1, /device:TPU:0, one launch (start us, length us, event | category | flops | bytes accessed | tf_op | source)
XLA Modules:
  0.0 60.2 jit_solution(7827160575360851013)
XLA Ops:
  0.6 0.0 copy-start
  0.6 1.2 %copy-done = bf16[1,4,8,128,128]{4,3,2,1,0:T(8,128)(2,1)S(1)} copy-done((bf16[1,4,8,128,128]{4,3,2,1,0:T(8,128)(2,1)S(1)}, bf16[1,4,8,128,128]{4,3,2,1,0:T(8,128)(2,1)}, u32[]{:S(2)}) %copy-start) | copy-done | bytes 1048600
  1.9 0.0 copy-start.8
  1.9 0.9 %copy-done.8 = bf16[1,32,32,64]{3,2,1,0:T(8,128)(2,1)S(1)} copy-done((bf16[1,32,32,64]{3,2,1,0:T(8,128)(2,1)S(1)}, bf16[1,32,32,64]{3,2,1,0:T(8,128)(2,1)}, u32[]{:S(2)}) %copy-start.8) | copy-done | bytes 131096
  2.8 0.0 copy-start.1
  2.8 2.4 %gather.1 = (bf16[4,3,128,128]{3,2,1,0:T(8,128)(2,1)S(1)}, bf16[512,128]{1,0:T(8,128)(2,1)}, bf16[1024,1024]{1,0:T(8,128)(2,1)S(1)}) custom-call(bf16[4,8,128,128]{3,2,1,0:T(8,128)(2,1)S(1)} %bitcast.46, bf16[32,32,64]{2,1,0:T(8,128)(2,1)S(1)} %bitcast.52), custom_call_target="tpu_custom_call" | custom-call | tf_op jit(solution)/shard_map/gather/pallas_call | solution.py:368
  5.2 0.0 copy-start.2
  5.2 1.4 %copy-done.2 = bf16[1024,1024]{1,0:T(8,128)(2,1)} copy-done((bf16[1024,1024]{1,0:T(8,128)(2,1)}, bf16[1024,1024]{1,0:T(8,128)(2,1)S(1)}, u32[]{:S(2)}) %copy-start.2) | copy-done | bytes 2097176
  6.6 2.4 %collective-permute-start = (bf16[4,3,128,128]{3,2,1,0:T(8,128)(2,1)S(1)}, bf16[4,3,128,128]{3,2,1,0:T(8,128)(2,1)S(1)}, u32[]{:S(2)}, u32[]{:S(2)}) collective-permute-start(bf16[4,3,128,128]{3,2,1,0:T(8,128)(2,1)S(1)} %get-tuple-element.14), channel_id=1, source_target_pairs={{0,1},{1,2},{2,3},{3,4},{4,5},{5,6},{6,7},{7,8},{8,9},{9,10},{10,1... | collective-permute-start | bytes 1179656 | tf_op jit(solution)/shard_map/ppermute | solution.py:381
  8.9 7.2 %all-to-all-start = ((bf16[16,32,128]{2,1,0:T(8,128)(2,1)}), bf16[16,32,128]{2,1,0:T(8,128)(2,1)S(1)}, u32[]{:S(2)}, u32[]{:S(2)}) async-start(bf16[16,32,128]{2,1,0:T(8,128)(2,1)} %bitcast.9), calls=%async_computation | async-start | bytes 262144 | tf_op jit(solution)/shard_map/all_to_all | solution.py:426
  16.2 0.0 collective-permute-done.low_ref
  16.2 0.0 copy-done.1
  16.2 0.0 copy-start.3
  16.2 1.6 %copy-done.3 = bf16[1024,1024]{1,0:T(8,128)(2,1)S(1)} copy-done((bf16[1024,1024]{1,0:T(8,128)(2,1)S(1)}, bf16[1024,1024]{1,0:T(8,128)(2,1)}, u32[]{:S(2)}) %copy-start.3) | copy-done | bytes 2097176
  17.8 0.0 copy-start.6
  17.8 0.9 %copy-done.6 = bf16[32,16,3,3,3]{0,1,4,3,2:T(8,128)(2,1)S(1)} copy-done((bf16[32,16,3,3,3]{0,1,4,3,2:T(8,128)(2,1)S(1)}, bf16[32,16,3,3,3]{0,1,4,3,2:T(8,128)(2,1)}, u32[]{:S(2)}) %copy-start.6) | copy-done | bytes 27672
  18.7 0.0 copy-start.9
  18.7 0.7 %copy-done.9 = bf16[16,4,3,3,3]{0,1,4,3,2:T(4,128)(2,1)S(1)} copy-done((bf16[16,4,3,3,3]{0,1,4,3,2:T(4,128)(2,1)S(1)}, bf16[16,4,3,3,3]{0,1,4,3,2:T(4,128)(2,1)}, u32[]{:S(2)}) %copy-start.9) | copy-done | bytes 3480
  19.4 0.0 copy-start.7
  19.4 5.6 %forward.1 = (bf16[11,5,128,128]{3,2,1,0:T(8,128)(2,1)S(1)}, bf16[5,3,128,256]{3,2,1,0:T(8,128)(2,1)S(1)}, bf16[512,128]{1,0:T(8,128)(2,1)S(1)}, bf16[2,128,256]{2,1,0:T(8,128)(2,1)S(1)}) custom-call(bf16[4,8,128,128]{3,2,1,0:T(8,128)(2,1)S(1)} %bitcast.47, bf16[4,3,128,128]{3,2,1,0:T(8,128)(2,1)S(1)} %collective-permute-done.low_ref, ...), custom_call_target="tpu_custom_call" | custom-call | tf_op jit(solution)/shard_map/forward/pallas_call | solution.py:368
  25.0 0.0 copy-start.4
  25.0 1.2 %copy-done.4 = bf16[11,5,128,128]{3,2,1,0:T(8,128)(2,1)} copy-done((bf16[11,5,128,128]{3,2,1,0:T(8,128)(2,1)}, bf16[11,5,128,128]{3,2,1,0:T(8,128)(2,1)S(1)}, u32[]{:S(2)}) %copy-start.4) | copy-done | bytes 1802264
  26.2 0.0 all-to-all-done
  26.2 0.0 copy-start.5
  26.2 0.3 delta.1.delta_ref
  26.6 1.6 %collective-permute-start.1 = (bf16[128,256]{1,0:T(8,128)(2,1)S(1)}, bf16[128,256]{1,0:T(8,128)(2,1)S(1)}, u32[]{:S(2)}, u32[]{:S(2)}) collective-permute-start(bf16[128,256]{1,0:T(8,128)(2,1)S(1)} %slice_bitcast_fusion), channel_id=1, source_target_pairs={{1,0},{2,1},{3,2},{4,3},{5,4},{6,5},{7,6},{8,7},{9,8},{10,9},{11,1... | collective-permute-start | bytes 196616 | tf_op jit(solution)/shard_map/ppermute | solution.py:381
  28.2 0.0 copy-done.7
  28.2 2.1 %second_gradient.1 = (f32[48,384]{1,0:T(8,128)S(1)}, bf16[4608,256]{1,0:T(8,128)(2,1)S(1)}) custom-call(bf16[5,3,128,256]{3,2,1,0:T(8,128)(2,1)S(1)} %get-tuple-element.17.hh_ref, bf16[2,128,256]{2,1,0:T(8,128)(2,1)S(1)} %delta.1.delta_ref, bf16[432,32]{1,0:T(8,128)(2,1)S(1)} %bitcast.51), custom_call_target="tpu_custom_call" | custom-call | tf_op jit(solution)/shard_map/second_gradient/pallas_call | solution.py:368
  30.3 0.0 collective-permute-done.1.next_ref
  30.3 0.0 copy-done.5
  30.3 2.7 %first_gradient.1 = f32[144,128]{1,0:T(8,128)S(1)} custom-call(bf16[5,3,128,256]{3,2,1,0:T(8,128)(2,1)S(1)} %get-tuple-element.17.hh_ref, bf16[2,128,256]{2,1,0:T(8,128)(2,1)S(1)} %delta.1.delta_ref, bf16[128,256]{1,0:T(8,128)(2,1)S(1)} %collective-permute-done.1.next_ref, bf16[4608,256]{1,0:T(8,128)(2,1)S(1)} %get-tuple-element.20.t2b_ref, ...), custom_call_target="tpu_custom_call" | custom-call | tf_op jit(solution)/shard_map/first_gradient/pallas_call | solution.py:368
  33.1 2.8 %collective-permute-start.2 = (bf16[400,128]{1,0:T(8,128)(2,1)S(1)}, bf16[400,128]{1,0:T(8,128)(2,1)S(1)}, u32[]{:S(2)}, u32[]{:S(2)}) collective-permute-start(bf16[400,128]{1,0:T(8,128)(2,1)S(1)} %pad_maximum_fusion), channel_id=1, source_target_pairs={{0,1},{1,0},{2,3},{3,2},{4,5},{5,4},{6,7},{7,6},{8,9},{9,8},{10,11... | collective-permute-start | bytes 307208 | tf_op jit(solution)/shard_map/ppermute | solution.py:386
  36.0 0.9 %collective-permute-done.2 = bf16[400,128]{1,0:T(8,128)(2,1)S(1)} collective-permute-done((bf16[400,128]{1,0:T(8,128)(2,1)S(1)}, bf16[400,128]{1,0:T(8,128)(2,1)S(1)}, u32[]{:S(2)}, u32[]{:S(2)}) %collective-permute-start.2) | collective-permute-done | bytes 102432 | tf_op jit(solution)/shard_map/ppermute | solution.py:386
  37.1 2.5 %collective-permute-start.3 = (bf16[400,128]{1,0:T(8,128)(2,1)S(1)}, bf16[400,128]{1,0:T(8,128)(2,1)S(1)}, u32[]{:S(2)}, u32[]{:S(2)}) collective-permute-start(bf16[400,128]{1,0:T(8,128)(2,1)S(1)} %pad_maximum_fusion.1), channel_id=1, source_target_pairs={{0,2},{1,3},{2,0},{3,1},{4,6},{5,7},{6,4},{7,5},{8,10},{9,11},{10,... | collective-permute-start | bytes 307208 | tf_op jit(solution)/shard_map/ppermute | solution.py:386
  39.5 3.4 %collective-permute-done.3 = bf16[400,128]{1,0:T(8,128)(2,1)S(1)} collective-permute-done((bf16[400,128]{1,0:T(8,128)(2,1)S(1)}, bf16[400,128]{1,0:T(8,128)(2,1)S(1)}, u32[]{:S(2)}, u32[]{:S(2)}) %collective-permute-start.3) | collective-permute-done | bytes 102432 | tf_op jit(solution)/shard_map/ppermute | solution.py:386
  43.1 1.6 %collective-permute-start.4 = (bf16[400,128]{1,0:T(8,128)(2,1)S(1)}, bf16[400,128]{1,0:T(8,128)(2,1)S(1)}, u32[]{:S(2)}, u32[]{:S(2)}) collective-permute-start(bf16[400,128]{1,0:T(8,128)(2,1)S(1)} %pad_maximum_fusion.2), channel_id=1, source_target_pairs={{0,4},{1,5},{2,6},{3,7},{4,0},{5,1},{6,2},{7,3},{8,12},{9,13},{10,... | collective-permute-start | bytes 307208 | tf_op jit(solution)/shard_map/ppermute | solution.py:386
  44.7 3.1 %collective-permute-done.4 = bf16[400,128]{1,0:T(8,128)(2,1)S(1)} collective-permute-done((bf16[400,128]{1,0:T(8,128)(2,1)S(1)}, bf16[400,128]{1,0:T(8,128)(2,1)S(1)}, u32[]{:S(2)}, u32[]{:S(2)}) %collective-permute-start.4) | collective-permute-done | bytes 102432 | tf_op jit(solution)/shard_map/ppermute | solution.py:386
  47.9 2.7 %collective-permute-start.5 = (bf16[400,128]{1,0:T(8,128)(2,1)S(1)}, bf16[400,128]{1,0:T(8,128)(2,1)S(1)}, u32[]{:S(2)}, u32[]{:S(2)}) collective-permute-start(bf16[400,128]{1,0:T(8,128)(2,1)S(1)} %pad_maximum_fusion.3), channel_id=1, source_target_pairs={{0,8},{1,9},{2,10},{3,11},{4,12},{5,13},{6,14},{7,15},{8,0},{9,1},... | collective-permute-start | bytes 307208 | tf_op jit(solution)/shard_map/ppermute | solution.py:386
  50.6 3.0 %collective-permute-done.5 = bf16[400,128]{1,0:T(8,128)(2,1)S(1)} collective-permute-done((bf16[400,128]{1,0:T(8,128)(2,1)S(1)}, bf16[400,128]{1,0:T(8,128)(2,1)S(1)}, u32[]{:S(2)}, u32[]{:S(2)}) %collective-permute-start.5) | collective-permute-done | bytes 102432 | tf_op jit(solution)/shard_map/ppermute | solution.py:386
  53.6 1.6 %collective-permute-start.6 = (f32[72,128]{1,0:T(8,128)S(1)}, f32[72,128]{1,0:T(8,128)S(1)}, u32[]{:S(2)}, u32[]{:S(2)}) collective-permute-start(f32[72,128]{1,0:T(8,128)S(1)} %fusion.8), channel_id=1, source_target_pairs={{0,16},{1,17},{2,18},{3,19},{4,20},{5,21},{6,22},{7,23},{8,24},{9,... | collective-permute-start | bytes 110600 | tf_op jit(solution)/shard_map/ppermute | solution.py:386
  55.1 2.4 %collective-permute-done.6 = f32[72,128]{1,0:T(8,128)S(1)} collective-permute-done((f32[72,128]{1,0:T(8,128)S(1)}, f32[72,128]{1,0:T(8,128)S(1)}, u32[]{:S(2)}, u32[]{:S(2)}) %collective-permute-start.6) | collective-permute-done | bytes 36896 | tf_op jit(solution)/shard_map/ppermute | solution.py:386
  57.6 0.0 collective-permute-start.7
  57.6 1.7 %scatter.1 = bf16[32,32,64]{2,1,0:T(8,128)(2,1)} custom-call(bf16[512,128]{1,0:T(8,128)(2,1)S(1)} %bitcast.49), custom_call_target="tpu_custom_call" | custom-call | tf_op jit(solution)/shard_map/scatter/pallas_call | solution.py:368
  59.3 0.0 collective-permute-done.7
  59.3 0.8 %scale.1 = (f32[27,4,16]{2,1,0:T(4,128)}, f32[27,16,32]{2,1,0:T(8,128)}) custom-call(f32[144,128]{1,0:T(8,128)S(1)} %maximum_select_fusion.4.sum_ref), custom_call_target="tpu_custom_call" | custom-call | tf_op jit(solution)/shard_map/scale/pallas_call | solution.py:368
  (29 shorter events, 0.4 us)
Async XLA Ops:
  0.6 1.2 %copy-start = (bf16[1,4,8,128,128]{4,3,2,1,0:T(8,128)(2,1)S(1)}, bf16[1,4,8,128,128]{4,3,2,1,0:T(8,128)(2,1)}, u32[]{:S(2)}) copy-start(bf16[1,4,8,128,128]{4,3,2,1,0:T(8,128)(2,1)} %param.4) | copy-start | bytes 3145732
  1.9 0.9 %copy-start.8 = (bf16[1,32,32,64]{3,2,1,0:T(8,128)(2,1)S(1)}, bf16[1,32,32,64]{3,2,1,0:T(8,128)(2,1)}, u32[]{:S(2)}) copy-start(bf16[1,32,32,64]{3,2,1,0:T(8,128)(2,1)} %param.7) | copy-start | bytes 393220
  2.8 13.4 %copy-start.1 = (bf16[1,4,8,128,128]{4,3,2,1,0:T(8,128)(2,1)S(1)}, bf16[1,4,8,128,128]{4,3,2,1,0:T(8,128)(2,1)}, u32[]{:S(2)}) copy-start(bf16[1,4,8,128,128]{4,3,2,1,0:T(8,128)(2,1)} %param.4) | copy-start | bytes 3145732
  5.2 1.4 %copy-start.2 = (bf16[1024,1024]{1,0:T(8,128)(2,1)}, bf16[1024,1024]{1,0:T(8,128)(2,1)S(1)}, u32[]{:S(2)}) copy-start(bf16[1024,1024]{1,0:T(8,128)(2,1)S(1)} %get-tuple-element.15.order_ref) | copy-start | bytes 6291460
  6.6 9.6 %collective-permute-start = (bf16[4,3,128,128]{3,2,1,0:T(8,128)(2,1)S(1)}, bf16[4,3,128,128]{3,2,1,0:T(8,128)(2,1)S(1)}, u32[]{:S(2)}, u32[]{:S(2)}) collective-permute-start(bf16[4,3,128,128]{3,2,1,0:T(8,128)(2,1)S(1)} %get-tuple-element.14), channel_id=1, source_target_pairs={{0,1},{1,2},{2,3},{3,4},{4,5},{5,6},{6,7},{7,8},{8,9},{9,10},{10,1... | collective-permute-start | bytes 1179656 | tf_op jit(solution)/shard_map/ppermute | solution.py:381
  8.9 17.3 %all-to-all-start = ((bf16[16,32,128]{2,1,0:T(8,128)(2,1)}), bf16[16,32,128]{2,1,0:T(8,128)(2,1)S(1)}, u32[]{:S(2)}, u32[]{:S(2)}) async-start(bf16[16,32,128]{2,1,0:T(8,128)(2,1)} %bitcast.9), calls=%async_computation | async-start | bytes 262144 | tf_op jit(solution)/shard_map/all_to_all | solution.py:426
  16.2 1.6 %copy-start.3 = (bf16[1024,1024]{1,0:T(8,128)(2,1)S(1)}, bf16[1024,1024]{1,0:T(8,128)(2,1)}, u32[]{:S(2)}) copy-start(bf16[1024,1024]{1,0:T(8,128)(2,1)} %copy-done.2) | copy-start | bytes 6291460
  17.8 0.9 %copy-start.6 = (bf16[32,16,3,3,3]{0,1,4,3,2:T(8,128)(2,1)S(1)}, bf16[32,16,3,3,3]{0,1,4,3,2:T(8,128)(2,1)}, u32[]{:S(2)}) copy-start(bf16[32,16,3,3,3]{0,1,4,3,2:T(8,128)(2,1)} %param.6) | copy-start | bytes 82948
  18.7 0.7 %copy-start.9 = (bf16[16,4,3,3,3]{0,1,4,3,2:T(4,128)(2,1)S(1)}, bf16[16,4,3,3,3]{0,1,4,3,2:T(4,128)(2,1)}, u32[]{:S(2)}) copy-start(bf16[16,4,3,3,3]{0,1,4,3,2:T(4,128)(2,1)} %param.5) | copy-start | bytes 10372
  19.4 8.8 %copy-start.7 = (bf16[32,16,3,3,3]{0,1,4,3,2:T(8,128)(2,1)S(1)}, bf16[32,16,3,3,3]{0,1,4,3,2:T(8,128)(2,1)}, u32[]{:S(2)}) copy-start(bf16[32,16,3,3,3]{0,1,4,3,2:T(8,128)(2,1)} %param.6) | copy-start | bytes 82948
  25.0 1.3 %copy-start.4 = (bf16[11,5,128,128]{3,2,1,0:T(8,128)(2,1)}, bf16[11,5,128,128]{3,2,1,0:T(8,128)(2,1)S(1)}, u32[]{:S(2)}) copy-start(bf16[11,5,128,128]{3,2,1,0:T(8,128)(2,1)S(1)} %get-tuple-element.21.a_ref) | copy-start | bytes 5406724
  26.2 4.1 %copy-start.5 = (bf16[11,5,128,128]{3,2,1,0:T(8,128)(2,1)S(1)}, bf16[11,5,128,128]{3,2,1,0:T(8,128)(2,1)}, u32[]{:S(2)}) copy-start(bf16[11,5,128,128]{3,2,1,0:T(8,128)(2,1)} %copy-done.4) | copy-start | bytes 5406724
  26.6 3.7 %collective-permute-start.1 = (bf16[128,256]{1,0:T(8,128)(2,1)S(1)}, bf16[128,256]{1,0:T(8,128)(2,1)S(1)}, u32[]{:S(2)}, u32[]{:S(2)}) collective-permute-start(bf16[128,256]{1,0:T(8,128)(2,1)S(1)} %slice_bitcast_fusion), channel_id=1, source_target_pairs={{1,0},{2,1},{3,2},{4,3},{5,4},{6,5},{7,6},{8,7},{9,8},{10,9},{11,1... | collective-permute-start | bytes 196616 | tf_op jit(solution)/shard_map/ppermute | solution.py:381
  33.1 3.8 %collective-permute-start.2 = (bf16[400,128]{1,0:T(8,128)(2,1)S(1)}, bf16[400,128]{1,0:T(8,128)(2,1)S(1)}, u32[]{:S(2)}, u32[]{:S(2)}) collective-permute-start(bf16[400,128]{1,0:T(8,128)(2,1)S(1)} %pad_maximum_fusion), channel_id=1, source_target_pairs={{0,1},{1,0},{2,3},{3,2},{4,5},{5,4},{6,7},{7,6},{8,9},{9,8},{10,11... | collective-permute-start | bytes 307208 | tf_op jit(solution)/shard_map/ppermute | solution.py:386
  37.1 5.9 %collective-permute-start.3 = (bf16[400,128]{1,0:T(8,128)(2,1)S(1)}, bf16[400,128]{1,0:T(8,128)(2,1)S(1)}, u32[]{:S(2)}, u32[]{:S(2)}) collective-permute-start(bf16[400,128]{1,0:T(8,128)(2,1)S(1)} %pad_maximum_fusion.1), channel_id=1, source_target_pairs={{0,2},{1,3},{2,0},{3,1},{4,6},{5,7},{6,4},{7,5},{8,10},{9,11},{10,... | collective-permute-start | bytes 307208 | tf_op jit(solution)/shard_map/ppermute | solution.py:386
  43.1 4.7 %collective-permute-start.4 = (bf16[400,128]{1,0:T(8,128)(2,1)S(1)}, bf16[400,128]{1,0:T(8,128)(2,1)S(1)}, u32[]{:S(2)}, u32[]{:S(2)}) collective-permute-start(bf16[400,128]{1,0:T(8,128)(2,1)S(1)} %pad_maximum_fusion.2), channel_id=1, source_target_pairs={{0,4},{1,5},{2,6},{3,7},{4,0},{5,1},{6,2},{7,3},{8,12},{9,13},{10,... | collective-permute-start | bytes 307208 | tf_op jit(solution)/shard_map/ppermute | solution.py:386
  47.9 5.6 %collective-permute-start.5 = (bf16[400,128]{1,0:T(8,128)(2,1)S(1)}, bf16[400,128]{1,0:T(8,128)(2,1)S(1)}, u32[]{:S(2)}, u32[]{:S(2)}) collective-permute-start(bf16[400,128]{1,0:T(8,128)(2,1)S(1)} %pad_maximum_fusion.3), channel_id=1, source_target_pairs={{0,8},{1,9},{2,10},{3,11},{4,12},{5,13},{6,14},{7,15},{8,0},{9,1},... | collective-permute-start | bytes 307208 | tf_op jit(solution)/shard_map/ppermute | solution.py:386
  53.6 4.0 %collective-permute-start.6 = (f32[72,128]{1,0:T(8,128)S(1)}, f32[72,128]{1,0:T(8,128)S(1)}, u32[]{:S(2)}, u32[]{:S(2)}) collective-permute-start(f32[72,128]{1,0:T(8,128)S(1)} %fusion.8), channel_id=1, source_target_pairs={{0,16},{1,17},{2,18},{3,19},{4,20},{5,21},{6,22},{7,23},{8,24},{9,... | collective-permute-start | bytes 110600 | tf_op jit(solution)/shard_map/ppermute | solution.py:386
  57.6 1.7 %collective-permute-start.7 = (f32[72,128]{1,0:T(8,128)S(1)}, f32[72,128]{1,0:T(8,128)S(1)}, u32[]{:S(2)}, u32[]{:S(2)}) collective-permute-start(f32[72,128]{1,0:T(8,128)S(1)} %add.69), channel_id=1, source_target_pairs={{0,1},{1,0},{2,3},{3,2},{4,5},{5,4},{6,7},{7,6},{8,9},{9,8},{10,11... | collective-permute-start | bytes 110600 | tf_op jit(solution)/shard_map/ppermute | solution.py:386

commit v2 on v1

--- a/solution.py
+++ b/solution.py
@@ -42,7 +42,8 @@
 
 
 def iotas(shape):
-    return lax.broadcasted_iota(jnp.int32, shape, 0), lax.broadcasted_iota(jnp.int32, shape, 1)
+    rows, lanes = shape
+    return lax.broadcasted_iota(jnp.int32, (rows, 1), 0), lax.broadcasted_iota(jnp.int32, (1, lanes), 1)
 
 
 def one_hot(mask):
@@ -143,13 +144,12 @@
 
 
 def forward_kernel(
-    vol_ref, low_ref, k1_ref, k2_ref, order_ref, a_ref, hh_ref, send_ref, slope_ref, own_ref, t1_ref, t2_ref, sem
+    vol_ref, low_ref, k1_ref, k2_ref, a_hbm, hh_ref, send_ref, slope_ref, a_ref, t1_ref, t2_ref, sem
 ):
     count = vol_ref.shape[1]
     planes = hh_ref.shape[0]
     d2n = slope_ref.shape[0]
-    copy = pltpu.make_async_copy(vol_ref, own_ref, sem)
-    copy.start()
+    copy = pltpu.make_async_copy(a_ref, a_hbm, sem)
 
     def put_from(first):
         def put(d, v, blocks):
@@ -158,14 +158,14 @@
 
         return put
 
-    arrange_planes(lambda c: low_ref[c].reshape(3 * 128, 128), 3, put_from(0))
     k1 = jnp.concatenate([k1_ref[t].astype(f32) for t in range(27) for _ in range(16 // CIN)], axis=0)
     k1 = spread(k1.astype(bf16), LH)
     band(tiled(lambda t: k1[16 * t : 16 * (t + 1)], LA // 16), LA, CIN, LH, C1, puts(t1_ref, LA))
     k2 = spread(k2_ref[...], LZ)
     band(tiled(lambda t: k2[C1 * t : C1 * (t + 1)], W1), LH, C1, LZ, C2, puts(t2_ref, LH))
-    copy.wait()
-    arrange_planes(lambda c: own_ref[c].reshape(count * 128, 128), count, put_from(3))
+    arrange_planes(lambda c: low_ref[c].reshape(3 * 128, 128), 3, put_from(0))
+    arrange_planes(lambda c: vol_ref[c].reshape(count * 128, 128), count, put_from(3))
+    copy.start()
 
     r, _ = iotas((planes * ROWS, LH))
     keep = r % HB != 0
@@ -194,10 +194,11 @@
         axis=0,
     )
     groups = C2 // 4
-    by_channel = dot(wide, order_ref[...]).astype(bf16)
+    by_channel = dot(wide, channel_order()).astype(bf16)
     stacked = jnp.concatenate([by_channel[:, 128 * g : 128 * (g + 1)] for g in range(groups)], axis=0)
     r, q = iotas((stacked.shape[0], stacked.shape[0]))
     send_ref[...] = dot(one_hot(r == by_height(q, d2n)), stacked).astype(bf16)
+    copy.wait()
 
 
 def second_layer_columns(hh_ref, d2n):
@@ -207,13 +208,15 @@
 
 def delta_kernel(cot_ref, slope_ref, delta_ref):
     d2n = delta_ref.shape[0]
-    count = cot_ref.shape[0]
-    r, q = iotas((count, count))
-    got = dot(one_hot(q == by_height(r, d2n)), cot_ref[...])
+    devices, lines, _ = cot_ref.shape
+    hl = lines // d2n
+    r, q = iotas((d2n * HB, devices * lines))
+    plane, h2 = r // HB, r % HB
+    order = one_hot(q == h2 // hl * lines + h2 % hl * d2n + plane)
+    got = dot(order, jnp.concatenate([cot_ref[i] for i in range(devices)], axis=0))
     for d in range(d2n):
         for b in range(BLOCKS):
-            at = [((2 * b + i) * d2n + d) * HB for i in range(2)]
-            c = jnp.concatenate([got[i : i + HB] for i in at], axis=1)
+            c = got[d * HB : (d + 1) * HB, b * LZ : (b + 1) * LZ]
             slope = jnp.where(slope_ref[d, b * HB : (b + 1) * HB].astype(f32) > 0, 1.0, SLOPE)
             delta_ref[d, b * HB : (b + 1) * HB] = (c * slope).astype(bf16)
 
@@ -243,14 +246,17 @@
     return [jnp.concatenate([exact_nt(pick, x), exact_nt(every, y)], axis=0) for x, y in zip(ahead, behind)]
 
 
-def second_gradient_kernel(hh_ref, delta_ref, k2_ref, out_ref, t2b_ref):
+def second_gradient_kernel(hh_ref, delta_ref, k2_ref, a_hbm, out_ref, t2b_ref, a_ref, sem):
+    copy = pltpu.make_async_copy(a_hbm, a_ref, sem)
+    copy.start()
     d2n = delta_ref.shape[0]
-    band_back(tiled(spread_back(k2_ref[...]), W2), LZ, C2, LH, C1, puts(t2b_ref, LZ))
     delta = jnp.concatenate([delta_ref[d] for d in range(d2n)], axis=0)
     g = dot_tn(delta, second_layer_columns(hh_ref, d2n))
     none = [jnp.zeros((3 * C2, LH), f32)]
     (sums,) = width_sums(g, W2, C2, C1, lambda taps: [jnp.concatenate(taps + none, axis=0)])
     out_ref[...] = sums
+    band_back(tiled(spread_back(k2_ref[...]), W2), LZ, C2, LH, C1, puts(t2b_ref, LZ))
+    copy.wait()
 
 
 def first_gradient_kernel(hh_ref, delta_ref, next_ref, t2b_ref, a_ref, two_ref, out_ref, dv_ref):
@@ -271,7 +277,7 @@
         tap = 3 * kd + kh
         return lhs, t2b_ref[2 * LZ * tap : 2 * LZ * (tap + 1)]
 
-    deltas, cols = [], []
+    deltas, planes = [], []
     for p in range(2):
         heights = (1,) if p == 0 else (2, 0)
         for even in range(2):
@@ -281,19 +287,15 @@
                 jnp.concatenate([lhs for lhs, _ in terms], axis=1),
                 jnp.concatenate([rhs for _, rhs in terms], axis=0),
             )
-            planes = [2 * d + 1 + even for d in range(d2n)]
-            hidden = jnp.concatenate([hh_ref[j, 2 if p else 1] for j in planes], axis=0)
+            here = [(p, 2 * d + 1 + even) for d in range(d2n)]
+            hidden = jnp.concatenate([hh_ref[j, 2 if p else 1] for _, j in here], axis=0)
             deltas.append((back * jnp.where(hidden.astype(f32) > 0, 1.0, SLOPE)).astype(bf16))
-            cols.append(
-                jnp.concatenate(
-                    [
-                        jnp.concatenate([with_before(a_ref[2 * j + kd, INPUT_ROWS[p, kh]]) for j in planes], axis=0)
-                        for kd, kh in TAPS
-                    ],
-                    axis=1,
-                )
-            )
-    g = dot_tn(jnp.concatenate(deltas, axis=0), jnp.concatenate(cols, axis=0))
+            planes += here
+    cols = [
+        jnp.concatenate([with_before(a_ref[2 * j + kd, INPUT_ROWS[p, kh]]) for p, j in planes], axis=0)
+        for kd, kh in TAPS
+    ]
+    g = dot_tn(jnp.concatenate(deltas, axis=0), jnp.concatenate(cols, axis=1))
     before, after = [jnp.zeros((C2, LA), f32)], [jnp.zeros((128 - C2 - 3 * C1, LA), f32)]
 
     def place(taps):
@@ -315,35 +317,45 @@
             one_ref[3 * tap + kw] = sum_ref[r : r + CIN, q : q + C1] * factor
 
 
-def gather_kernel(vol_ref, cot_ref, low_ref, out_ref, order_ref, own_ref, sems):
-    planes = vol_ref.shape[1]
-    d2n = planes // 4
+def gather_kernel(
+    vol_hbm, cot_hbm, k1_hbm, k2_hbm, vol_ref, out_ref, k1_ref, k2_ref, cot_ref, order_ref, sems
+):
+    d2n = vol_ref.shape[1] // 4
     copies = [
-        pltpu.make_async_copy(cot_ref, own_ref, sems.at[0]),
-        pltpu.make_async_copy(vol_ref.at[:, planes - 3 :], low_ref, sems.at[1]),
+        pltpu.make_async_copy(x, y, sems.at[i])
+        for i, (x, y) in enumerate(
+            [(cot_hbm, cot_ref), (vol_hbm, vol_ref), (k1_hbm, k1_ref), (k2_hbm, k2_ref)]
+        )
     ]
     for copy in copies:
         copy.start()
     channels, depth, cells = cot_ref.shape
     hl = cells // 32
-    order_ref[...] = channel_order()
+    r, q = iotas((WIDE, WIDE))
+    order_ref[...] = one_hot(q == (r % (BLOCKS * W2)) * C2 + r // (BLOCKS * W2))
     r, q = iotas((cells, hl * 128))
     moves = [one_hot((q // 128 == r // 32) & (q % 128 == i * 32 + r % 32)) for i in range(4)]
     copies[0].wait()
-    groups = []
-    for first in range(0, channels, 4):
-        parts = [dot(own_ref[first + i], moves[i]) for i in range(4)]
-        groups.append(((parts[0] + parts[1]) + (parts[2] + parts[3])).astype(bf16))
+    parts = [
+        dot(jnp.concatenate([cot_ref[first + i] for first in range(0, channels, 4)], axis=0), moves[i])
+        for i in range(4)
+    ]
+    together = ((parts[0] + parts[1]) + (parts[2] + parts[3])).astype(bf16)
+    groups = [together[i * depth : (i + 1) * depth] for i in range(channels // 4)]
     x = jnp.concatenate(
         [jnp.concatenate([g[:, h * 128 : (h + 1) * 128] for g in groups], axis=1) for h in range(hl)], axis=0
     )
-    x = dot_nt(x, order_ref[...]).astype(bf16)
-    rows = [x[h * depth : (h + 1) * depth, 128 * g : 128 * (g + 1)] for h in range(hl) for g in range(8)]
-    count = len(rows) * depth
-    r, q = iotas((count, count))
-    row, plane = travel_order(r, depth, d2n, hl)
-    out_ref[...] = dot(one_hot(q == row * depth + plane), jnp.concatenate(rows, axis=0)).astype(bf16)
-    copies[1].wait()
+    x = dot(x, order_ref[...]).astype(bf16)
+    for device in range(out_ref.shape[0]):
+        for h in range(hl):
+            at = h * depth + device * d2n
+            out_ref[device, h * d2n : (h + 1) * d2n] = x[at : at + d2n]
+    for copy in copies[1:]:
+        copy.wait()
+
+
+def last_planes_kernel(vol_ref, low_ref):
+    low_ref[...] = vol_ref[:, vol_ref.shape[1] - 3 :]
 
 
 def scatter_kernel(d2n, got_ref, out_ref):
@@ -364,16 +376,21 @@
             out_ref[4 * g + i] = dot(x, moves[i]).astype(bf16)
 
 
-def call(kernel, name, outs, *args, scratch=(), apart=()):
+def call(kernel, name, outs, *args, scratch=(), apart=(), apart_out=()):
     return pl.pallas_call(
         kernel,
         name=name,
         in_specs=[pl.BlockSpec(memory_space=pltpu.HBM if i in apart else pltpu.VMEM) for i in range(len(args))],
-        out_specs=[pl.BlockSpec(memory_space=pltpu.VMEM) for _ in outs],
-        out_shape=[jax.ShapeDtypeStruct(shape, dtype) for shape, dtype in outs],
+        out_specs=[
+            pl.BlockSpec(memory_space=pltpu.HBM if i in apart_out else pltpu.VMEM) for i in range(len(outs))
+        ],
+        out_shape=[
+            pltpu.HBM(shape, dtype) if i in apart_out else jax.ShapeDtypeStruct(shape, dtype)
+            for i, (shape, dtype) in enumerate(outs)
+        ],
         scratch_shapes=list(scratch),
         compiler_params=pltpu.CompilerParams(vmem_limit_bytes=32 << 20),
-    )(*args)
+    )(*[pltpu.with_memory_space_constraint(x, pltpu.HBM) if i in apart else x for i, x in enumerate(args)])
 
 
 def passed_along(block, distance):
@@ -415,15 +432,13 @@
     while bit < devices * lax.axis_size("dp"):
         terms = terms + with_partner(terms, bit)
         bit *= 2
-    other = with_partner(terms, 1)
-    terms = jnp.where(even, jnp.concatenate([terms, other], 0), jnp.concatenate([other, terms], 0))
     return terms, blocks.reshape(rows.shape)
 
 
-def exchanged(rows):
-    devices = lax.axis_size("space")
-    blocks = rows.reshape(devices, rows.shape[0] // devices, 128)
-    return lax.all_to_all(blocks, "space", 0, 0, tiled=True).reshape(rows.shape)
+def rejoined(half):
+    other = with_partner(half, 1)
+    even = lax.axis_index("space") % 2 == 0
+    return jnp.where(even, jnp.concatenate([half, other], 0), jnp.concatenate([other, half], 0))
 
 
 def local(volumes, kernel_one, kernel_two, cotangent):
@@ -431,22 +446,30 @@
     d1n, d2n = planes // 2, planes // 4
     _, _, depth, cells = cotangent.shape
     vol, cot = volumes[0], cotangent[0]
+    devices = lax.axis_size("space")
     travelling = depth * (cells // 32) * (C2 // 4)
 
-    low, cot_rows, order = call(
+    k1 = kernel_one.transpose(2, 3, 4, 1, 0).reshape(27, CIN, C1)
+    k2 = kernel_two.transpose(2, 3, 4, 1, 0).reshape(27 * C1, C2)
+    vol, cot_rows, k1, k2 = call(
         gather_kernel,
         "gather",
-        [((CIN, 3, height, width), bf16), ((travelling, 128), bf16), ((WIDE, WIDE), bf16)],
+        [(vol.shape, bf16), ((devices, depth // devices * (cells // 32), WIDE), bf16), (k1.shape, bf16), (k2.shape, bf16)],
         vol,
         cot,
-        scratch=[pltpu.VMEM(cot.shape, bf16), pltpu.SemaphoreType.DMA((2,))],
-        apart=(0, 1),
-    )
+        k1,
+        k2,
+        scratch=[
+            pltpu.VMEM(cot.shape, bf16),
+            pltpu.VMEM((WIDE, WIDE), bf16),
+            pltpu.SemaphoreType.DMA((4,)),
+        ],
+        apart=(0, 1, 2, 3),
+    )
+    (low,) = call(last_planes_kernel, "last_planes", [((CIN, 3, height, width), bf16)], vol)
     low = passed_along(low, 1)
-    cot_here = exchanged(cot_rows)
-
-    k1 = kernel_one.transpose(2, 3, 4, 1, 0).reshape(27, CIN, C1)
-    k2 = kernel_two.transpose(2, 3, 4, 1, 0).reshape(27 * C1, C2)
+    cot_here = lax.all_to_all(cot_rows, "space", 0, 0, tiled=True)
+
     a, hh, send, slope = call(
         forward_kernel,
         "forward",
@@ -460,24 +483,26 @@
         low,
         k1,
         k2,
-        order,
         scratch=[
-            pltpu.VMEM(vol.shape, bf16),
+            pltpu.VMEM((planes + 3, 5, ROWS, LA), bf16),
             pltpu.VMEM((9 * 2 * LA, LH), bf16),
             pltpu.VMEM((9 * 2 * LH, LZ), bf16),
             pltpu.SemaphoreType.DMA,
         ],
-        apart=(0,),
+        apart_out=(0,),
     )
     (delta,) = call(delta_kernel, "delta", [((d2n, ROWS, LZ), bf16)], cot_here, slope)
     delta_next = passed_along(delta[0], -1)
-    term_two, t2b = call(
+    term_two, t2b, a = call(
         second_gradient_kernel,
         "second_gradient",
-        [((3 * C1, 384), f32), ((9 * 2 * LZ, LH), bf16)],
+        [((3 * C1, 384), f32), ((9 * 2 * LZ, LH), bf16), (a.shape, bf16)],
         hh,
         delta,
         k2,
+        a,
+        scratch=[pltpu.SemaphoreType.DMA],
+        apart=(3,),
     )
     (terms,) = call(
         first_gradient_kernel,
@@ -491,8 +516,10 @@
         term_two,
         scratch=[pltpu.VMEM((d2n + 1, 2, ROWS, 2 * LZ), bf16)],
     )
-    terms, got = total_and_exchange(terms, send)
+    half, got = total_and_exchange(terms, send)
     (out,) = call(functools.partial(scatter_kernel, d2n), "scatter", [((C2, depth, cells), bf16)], got)
+    half, out = lax.optimization_barrier((half, out))
+    terms = rejoined(half)
     count = volumes.shape[0] * lax.axis_size("dp")
     factor = 1.0 / math.sqrt(count * depth * (height // 4) ** 2)
     one, two = call(

time: 60.6 us -> 53.1 us (0.88)
  local copies, waits for them, and re-layouts: 8.05 us -> 0.04 us
  waiting for transfers between devices: 12.8 us -> 17.1 us
  starting transfers between devices: 22.4 us -> 19.1 us
    unnamed x20 -> x0, local copies, waits for them, and re-layouts: 8 us -> none
    ppermute x6, starting transfers between devices: 11.2 us -> 8.19 us  [with_partner(): lax.ppermute(block, ('dp', 'space'), [(i, i ^ bit) for i in range(count)])]
    all_to_all x1, waiting for transfers between devices: 0.01 us -> 2.59 us  [local(): cot_here = lax.all_to_all(cot_rows, 'space', 0, 0, tiled=True)]
    ppermute x6, waiting for transfers between devices: 12.8 us -> 14.5 us  [with_partner(): lax.ppermute(block, ('dp', 'space'), [(i, i ^ bit) for i in range(count)])]
    pallas_call x7 -> x8, Pallas kernels: 15.6 us -> 15.4 us  [call(): pl.pallas_call(kernel, name=name, in_specs=[pl.BlockSpec(memory_space=plt...]
  transfers between devices with their start and end apart: 9 -> 9, of which waited for: 5 -> 7; matrix products, arithmetic and copies ran while one was open for 0% -> 0% of each run, Pallas kernels for 15% -> 17%
where the time goes in v2:
time: 53.1 us; the launch traced here: 52.8 us
  starting transfers between devices  19.1 us (36%)
  waiting for transfers between devices  17.1 us (32%)
  Pallas kernels  15.4 us (29%)
  between operations  0.88 us (2%)
    pallas_call x8, Pallas kernels, call(): pl.pallas_call(kernel, name=name, in_specs=[pl.BlockSpec(memory_space=plt...  15.4 us
    ppermute x6, waiting for transfers between devices, with_partner(): lax.ppermute(block, ('dp', 'space'), [(i, i ^ bit) for i in range(count)])  14.5 us
    ppermute x6, starting transfers between devices, with_partner(): lax.ppermute(block, ('dp', 'space'), [(i, i ^ bit) for i in range(count)])  8.19 us
    all_to_all x1, starting transfers between devices, local(): cot_here = lax.all_to_all(cot_rows, 'space', 0, 0, tiled=True)  7.21 us
    ppermute x2, starting transfers between devices, passed_along(): lax.ppermute(block, 'space', [(i - distance, i) for i in devices if i - d...  3.67 us
    all_to_all x1, waiting for transfers between devices, local(): cot_here = lax.all_to_all(cot_rows, 'space', 0, 0, tiled=True)  2.59 us
  transfers between devices with their start and end apart: 9, of which 7 were waited for; matrix products, arithmetic and copies ran while one was open for 0% of the time, Pallas kernels for 17%

profile of v2, /device:TPU:0, one launch (start us, length us, event | category | flops | bytes accessed | tf_op | source)
XLA Modules:
  0.0 52.8 jit_solution(894260669890207665)
XLA Ops:
  0.6 2.6 %gather.1 = (bf16[4,8,128,128]{3,2,1,0:T(8,128)(2,1)S(1)}, bf16[16,4,1024]{2,1,0:T(4,128)(2,1)}, bf16[27,4,16]{2,1,0:T(4,128)(2,1)S(1)}, bf16[432,32]{1,0:T(8,128)(2,1)S(1)}) custom-call(bf16[4,8,128,128]{3,2,1,0:T(8,128)(2,1)} %bitcast.46, bf16[32,32,64]{2,1,0:T(8,128)(2,1)} %bitcast.49, bf16[27,4,16]{2,1,0:T(4,128)(2,1)} %bitcast.61, bf16[432,32]{1,0:T(8,128)(2,1)} %bitcast.60), custom_call_target="tpu_custom_call" | custom-call | tf_op jit(solution)/shard_map/gather/pallas_call | solution.py:380
  3.2 2.4 %collective-permute-start = (bf16[4,3,128,128]{3,2,1,0:T(8,128)(2,1)S(1)}, bf16[4,3,128,128]{3,2,1,0:T(8,128)(2,1)S(1)}, u32[]{:S(2)}, u32[]{:S(2)}) collective-permute-start(bf16[4,3,128,128]{3,2,1,0:T(8,128)(2,1)S(1)} %last_planes.1), channel_id=1, source_target_pairs={{0,1},{1,2},{2,3},{3,4},{4,5},{5,6},{6,7},{7,8},{8,9},{9,10},{10,1... | collective-permute-start | bytes 1179656 | tf_op jit(solution)/shard_map/ppermute | solution.py:398
  5.6 7.2 %all-to-all-start = ((bf16[16,4,1024]{2,1,0:T(4,128)(2,1)}), bf16[16,4,1024]{2,1,0:T(4,128)(2,1)S(1)}, u32[]{:S(2)}, u32[]{:S(2)}) async-start(bf16[16,4,1024]{2,1,0:T(4,128)(2,1)} %get-tuple-element.22), calls=%async_computation | async-start | bytes 262144 | tf_op jit(solution)/shard_map/all_to_all | solution.py:471
  12.9 0.0 collective-permute-done.low_ref
  12.9 5.3 %forward.1 = (bf16[11,5,128,128]{3,2,1,0:T(8,128)(2,1)}, bf16[5,3,128,256]{3,2,1,0:T(8,128)(2,1)S(1)}, bf16[512,128]{1,0:T(8,128)(2,1)S(1)}, bf16[2,128,256]{2,1,0:T(8,128)(2,1)S(1)}) custom-call(bf16[4,8,128,128]{3,2,1,0:T(8,128)(2,1)S(1)} %get-tuple-element.18.vol_ref, bf16[4,3,128,128]{3,2,1,0:T(8,128)(2,1)S(1)} %collective-permute-done.low_ref, ...), custom_call_target="tpu_custom_call" | custom-call | tf_op jit(solution)/shard_map/forward/pallas_call | solution.py:380
  18.2 2.6 %all-to-all-done.cot_ref = bf16[16,4,1024]{2,1,0:T(4,128)(2,1)S(1)} async-done(((bf16[16,4,1024]{2,1,0:T(4,128)(2,1)}), bf16[16,4,1024]{2,1,0:T(4,128)(2,1)S(1)}, u32[]{:S(2)}, u32[]{:S(2)}) %all-to-all-start) | async-done | bytes 131104 | tf_op jit(solution)/shard_map/all_to_all | solution.py:471
  20.8 0.2 delta.1.delta_ref
  21.0 1.3 %collective-permute-start.1 = (bf16[128,256]{1,0:T(8,128)(2,1)S(1)}, bf16[128,256]{1,0:T(8,128)(2,1)S(1)}, u32[]{:S(2)}, u32[]{:S(2)}) collective-permute-start(bf16[128,256]{1,0:T(8,128)(2,1)S(1)} %slice_bitcast_fusion.2), channel_id=1, source_target_pairs={{1,0},{2,1},{3,2},{4,3},{5,4},{6,5},{7,6},{8,7},{9,8},{10,9},{11,1... | collective-permute-start | bytes 196616 | tf_op jit(solution)/shard_map/ppermute | solution.py:398
  22.3 2.1 %second_gradient.1 = (f32[48,384]{1,0:T(8,128)S(1)}, bf16[4608,256]{1,0:T(8,128)(2,1)S(1)}, bf16[11,5,128,128]{3,2,1,0:T(8,128)(2,1)S(1)}) custom-call(bf16[5,3,128,256]{3,2,1,0:T(8,128)(2,1)S(1)} %get-tuple-element.21.hh_ref, bf16[2,128,256]{2,1,0:T(8,128)(2,1)S(1)} %delta.1.delta_ref, bf16[432,32]{1,0:T(8,128)(2,1)S(1)} %get-tuple-element.20.k2_ref, ...), custom_call_target="tpu_custom_call" | custom-call | tf_op jit(solution)/shard_map/second_gradient/pallas_call | solution.py:380
  24.4 0.0 collective-permute-done.1.next_ref
  24.4 2.7 %first_gradient.1 = f32[144,128]{1,0:T(8,128)S(1)} custom-call(bf16[5,3,128,256]{3,2,1,0:T(8,128)(2,1)S(1)} %get-tuple-element.21.hh_ref, bf16[2,128,256]{2,1,0:T(8,128)(2,1)S(1)} %delta.1.delta_ref, bf16[128,256]{1,0:T(8,128)(2,1)S(1)} %collective-permute-done.1.next_ref, bf16[4608,256]{1,0:T(8,128)(2,1)S(1)} %get-tuple-element.25.t2b_ref, ...), custom_call_target="tpu_custom_call" | custom-call | tf_op jit(solution)/shard_map/first_gradient/pallas_call | solution.py:380
  27.2 1.5 %collective-permute-start.2 = (bf16[400,128]{1,0:T(8,128)(2,1)S(1)}, bf16[400,128]{1,0:T(8,128)(2,1)S(1)}, u32[]{:S(2)}, u32[]{:S(2)}) collective-permute-start(bf16[400,128]{1,0:T(8,128)(2,1)S(1)} %pad_maximum_fusion), channel_id=1, source_target_pairs={{0,1},{1,0},{2,3},{3,2},{4,5},{5,4},{6,7},{7,6},{8,9},{9,8},{10,11... | collective-permute-start | bytes 307208 | tf_op jit(solution)/shard_map/ppermute | solution.py:403
  28.8 0.9 %collective-permute-done.2 = bf16[400,128]{1,0:T(8,128)(2,1)S(1)} collective-permute-done((bf16[400,128]{1,0:T(8,128)(2,1)S(1)}, bf16[400,128]{1,0:T(8,128)(2,1)S(1)}, u32[]{:S(2)}, u32[]{:S(2)}) %collective-permute-start.2) | collective-permute-done | bytes 102432 | tf_op jit(solution)/shard_map/ppermute | solution.py:403
  29.8 1.7 %collective-permute-start.3 = (bf16[400,128]{1,0:T(8,128)(2,1)S(1)}, bf16[400,128]{1,0:T(8,128)(2,1)S(1)}, u32[]{:S(2)}, u32[]{:S(2)}) collective-permute-start(bf16[400,128]{1,0:T(8,128)(2,1)S(1)} %pad_maximum_fusion.1), channel_id=1, source_target_pairs={{0,2},{1,3},{2,0},{3,1},{4,6},{5,7},{6,4},{7,5},{8,10},{9,11},{10,... | collective-permute-start | bytes 307208 | tf_op jit(solution)/shard_map/ppermute | solution.py:403
  31.5 3.5 %collective-permute-done.3 = bf16[400,128]{1,0:T(8,128)(2,1)S(1)} collective-permute-done((bf16[400,128]{1,0:T(8,128)(2,1)S(1)}, bf16[400,128]{1,0:T(8,128)(2,1)S(1)}, u32[]{:S(2)}, u32[]{:S(2)}) %collective-permute-start.3) | collective-permute-done | bytes 102432 | tf_op jit(solution)/shard_map/ppermute | solution.py:403
  35.2 1.2 %collective-permute-start.4 = (bf16[400,128]{1,0:T(8,128)(2,1)S(1)}, bf16[400,128]{1,0:T(8,128)(2,1)S(1)}, u32[]{:S(2)}, u32[]{:S(2)}) collective-permute-start(bf16[400,128]{1,0:T(8,128)(2,1)S(1)} %pad_maximum_fusion.2), channel_id=1, source_target_pairs={{0,4},{1,5},{2,6},{3,7},{4,0},{5,1},{6,2},{7,3},{8,12},{9,13},{10,... | collective-permute-start | bytes 307208 | tf_op jit(solution)/shard_map/ppermute | solution.py:403
  36.4 3.5 %collective-permute-done.4 = bf16[400,128]{1,0:T(8,128)(2,1)S(1)} collective-permute-done((bf16[400,128]{1,0:T(8,128)(2,1)S(1)}, bf16[400,128]{1,0:T(8,128)(2,1)S(1)}, u32[]{:S(2)}, u32[]{:S(2)}) %collective-permute-start.4) | collective-permute-done | bytes 102432 | tf_op jit(solution)/shard_map/ppermute | solution.py:403
  40.0 2.2 %collective-permute-start.5 = (bf16[400,128]{1,0:T(8,128)(2,1)S(1)}, bf16[400,128]{1,0:T(8,128)(2,1)S(1)}, u32[]{:S(2)}, u32[]{:S(2)}) collective-permute-start(bf16[400,128]{1,0:T(8,128)(2,1)S(1)} %pad_maximum_fusion.3), channel_id=1, source_target_pairs={{0,8},{1,9},{2,10},{3,11},{4,12},{5,13},{6,14},{7,15},{8,0},{9,1},... | collective-permute-start | bytes 307208 | tf_op jit(solution)/shard_map/ppermute | solution.py:403
  42.2 4.5 %collective-permute-done.5 = bf16[400,128]{1,0:T(8,128)(2,1)S(1)} collective-permute-done((bf16[400,128]{1,0:T(8,128)(2,1)S(1)}, bf16[400,128]{1,0:T(8,128)(2,1)S(1)}, u32[]{:S(2)}, u32[]{:S(2)}) %collective-permute-start.5) | collective-permute-done | bytes 102432 | tf_op jit(solution)/shard_map/ppermute | solution.py:403
  46.8 1.6 %collective-permute-start.6 = (f32[72,128]{1,0:T(8,128)S(1)}, f32[72,128]{1,0:T(8,128)S(1)}, u32[]{:S(2)}, u32[]{:S(2)}) collective-permute-start(f32[72,128]{1,0:T(8,128)S(1)} %fusion.8), channel_id=1, source_target_pairs={{0,16},{1,17},{2,18},{3,19},{4,20},{5,21},{6,22},{7,23},{8,24},{9,... | collective-permute-start | bytes 110600 | tf_op jit(solution)/shard_map/ppermute | solution.py:403
  48.3 1.7 %scatter.1 = bf16[32,32,64]{2,1,0:T(8,128)(2,1)} custom-call(bf16[512,128]{1,0:T(8,128)(2,1)S(1)} %bitcast.44), custom_call_target="tpu_custom_call" | custom-call | tf_op jit(solution)/shard_map/scatter/pallas_call | solution.py:380
  50.0 0.8 %collective-permute-done.6 = f32[72,128]{1,0:T(8,128)S(1)} collective-permute-done((f32[72,128]{1,0:T(8,128)S(1)}, f32[72,128]{1,0:T(8,128)S(1)}, u32[]{:S(2)}, u32[]{:S(2)}) %collective-permute-start.6) | collective-permute-done | bytes 36896 | tf_op jit(solution)/shard_map/ppermute | solution.py:403
  50.8 0.0 collective-permute-start.7
  50.8 1.2 %collective-permute-done.7 = f32[72,128]{1,0:T(8,128)S(1)} collective-permute-done((f32[72,128]{1,0:T(8,128)S(1)}, f32[72,128]{1,0:T(8,128)S(1)}, u32[]{:S(2)}, u32[]{:S(2)}) %collective-permute-start.7) | collective-permute-done | bytes 36896 | tf_op jit(solution)/shard_map/ppermute | solution.py:403
  52.0 0.8 %scale.1 = (f32[27,4,16]{2,1,0:T(4,128)}, f32[27,16,32]{2,1,0:T(8,128)}) custom-call(f32[144,128]{1,0:T(8,128)S(1)} %maximum_select_fusion.4.sum_ref), custom_call_target="tpu_custom_call" | custom-call | tf_op jit(solution)/shard_map/scale/pallas_call | solution.py:380
  (30 shorter events, 0.4 us)
Async XLA Ops:
  3.2 9.6 %collective-permute-start = (bf16[4,3,128,128]{3,2,1,0:T(8,128)(2,1)S(1)}, bf16[4,3,128,128]{3,2,1,0:T(8,128)(2,1)S(1)}, u32[]{:S(2)}, u32[]{:S(2)}) collective-permute-start(bf16[4,3,128,128]{3,2,1,0:T(8,128)(2,1)S(1)} %last_planes.1), channel_id=1, source_target_pairs={{0,1},{1,2},{2,3},{3,4},{4,5},{5,6},{6,7},{7,8},{8,9},{9,10},{10,1... | collective-permute-start | bytes 1179656 | tf_op jit(solution)/shard_map/ppermute | solution.py:398
  5.6 15.2 %all-to-all-start = ((bf16[16,4,1024]{2,1,0:T(4,128)(2,1)}), bf16[16,4,1024]{2,1,0:T(4,128)(2,1)S(1)}, u32[]{:S(2)}, u32[]{:S(2)}) async-start(bf16[16,4,1024]{2,1,0:T(4,128)(2,1)} %get-tuple-element.22), calls=%async_computation | async-start | bytes 262144 | tf_op jit(solution)/shard_map/all_to_all | solution.py:471
  21.0 3.4 %collective-permute-start.1 = (bf16[128,256]{1,0:T(8,128)(2,1)S(1)}, bf16[128,256]{1,0:T(8,128)(2,1)S(1)}, u32[]{:S(2)}, u32[]{:S(2)}) collective-permute-start(bf16[128,256]{1,0:T(8,128)(2,1)S(1)} %slice_bitcast_fusion.2), channel_id=1, source_target_pairs={{1,0},{2,1},{3,2},{4,3},{5,4},{6,5},{7,6},{8,7},{9,8},{10,9},{11,1... | collective-permute-start | bytes 196616 | tf_op jit(solution)/shard_map/ppermute | solution.py:398
  27.2 2.5 %collective-permute-start.2 = (bf16[400,128]{1,0:T(8,128)(2,1)S(1)}, bf16[400,128]{1,0:T(8,128)(2,1)S(1)}, u32[]{:S(2)}, u32[]{:S(2)}) collective-permute-start(bf16[400,128]{1,0:T(8,128)(2,1)S(1)} %pad_maximum_fusion), channel_id=1, source_target_pairs={{0,1},{1,0},{2,3},{3,2},{4,5},{5,4},{6,7},{7,6},{8,9},{9,8},{10,11... | collective-permute-start | bytes 307208 | tf_op jit(solution)/shard_map/ppermute | solution.py:403
  29.8 5.2 %collective-permute-start.3 = (bf16[400,128]{1,0:T(8,128)(2,1)S(1)}, bf16[400,128]{1,0:T(8,128)(2,1)S(1)}, u32[]{:S(2)}, u32[]{:S(2)}) collective-permute-start(bf16[400,128]{1,0:T(8,128)(2,1)S(1)} %pad_maximum_fusion.1), channel_id=1, source_target_pairs={{0,2},{1,3},{2,0},{3,1},{4,6},{5,7},{6,4},{7,5},{8,10},{9,11},{10,... | collective-permute-start | bytes 307208 | tf_op jit(solution)/shard_map/ppermute | solution.py:403
  35.2 4.7 %collective-permute-start.4 = (bf16[400,128]{1,0:T(8,128)(2,1)S(1)}, bf16[400,128]{1,0:T(8,128)(2,1)S(1)}, u32[]{:S(2)}, u32[]{:S(2)}) collective-permute-start(bf16[400,128]{1,0:T(8,128)(2,1)S(1)} %pad_maximum_fusion.2), channel_id=1, source_target_pairs={{0,4},{1,5},{2,6},{3,7},{4,0},{5,1},{6,2},{7,3},{8,12},{9,13},{10,... | collective-permute-start | bytes 307208 | tf_op jit(solution)/shard_map/ppermute | solution.py:403
  40.0 6.7 %collective-permute-start.5 = (bf16[400,128]{1,0:T(8,128)(2,1)S(1)}, bf16[400,128]{1,0:T(8,128)(2,1)S(1)}, u32[]{:S(2)}, u32[]{:S(2)}) collective-permute-start(bf16[400,128]{1,0:T(8,128)(2,1)S(1)} %pad_maximum_fusion.3), channel_id=1, source_target_pairs={{0,8},{1,9},{2,10},{3,11},{4,12},{5,13},{6,14},{7,15},{8,0},{9,1},... | collective-permute-start | bytes 307208 | tf_op jit(solution)/shard_map/ppermute | solution.py:403
  46.8 4.0 %collective-permute-start.6 = (f32[72,128]{1,0:T(8,128)S(1)}, f32[72,128]{1,0:T(8,128)S(1)}, u32[]{:S(2)}, u32[]{:S(2)}) collective-permute-start(f32[72,128]{1,0:T(8,128)S(1)} %fusion.8), channel_id=1, source_target_pairs={{0,16},{1,17},{2,18},{3,19},{4,20},{5,21},{6,22},{7,23},{8,24},{9,... | collective-permute-start | bytes 110600 | tf_op jit(solution)/shard_map/ppermute | solution.py:403
  50.8 1.2 %collective-permute-start.7 = (f32[72,128]{1,0:T(8,128)S(1)}, f32[72,128]{1,0:T(8,128)S(1)}, u32[]{:S(2)}, u32[]{:S(2)}) collective-permute-start(f32[72,128]{1,0:T(8,128)S(1)} %add.70), channel_id=1, source_target_pairs={{0,1},{1,0},{2,3},{3,2},{4,5},{5,4},{6,7},{7,6},{8,9},{9,8},{10,11... | collective-permute-start | bytes 110600 | tf_op jit(solution)/shard_map/ppermute | solution.py:403

commit v3 on v2

--- a/solution.py
+++ b/solution.py
@@ -18,6 +18,7 @@
 W0, W1, W2 = 32, 16, 8
 ROWS = BLOCKS * HB
 LA, LH, LZ = W0 * CIN, W1 * C1, W2 * C2
+EDGE = LA // BLOCKS
 WIDE = BLOCKS * LZ
 TAPS = [(kd, kh) for kd in range(3) for kh in range(3)]
 INPUT_ROWS = {(0, 0): 4, (0, 1): 0, (0, 2): 1, (1, 0): 1, (1, 1): 2, (1, 2): 3}
@@ -51,8 +52,10 @@
 
 
 def width_order():
-    r, q = iotas((CIN * 128, CIN * 128))
-    return one_hot(r == (q % CIN) * 128 + (q // LA) * W0 + (q // CIN) % W0)
+    r, q = iotas((CIN * 128, (CIN + 1) * 128))
+    own = (q % CIN) * 128 + (q // LA) * W0 + (q // CIN) % W0
+    edge = (q % CIN) * 128 + (q % LA) // EDGE * W0 - 1
+    return one_hot(r == jnp.where(q < CIN * 128, own, jnp.where(q % LA < EDGE, -1, edge)))
 
 
 def height_order():
@@ -73,11 +76,30 @@
     for d in range(count):
         z = dot(order, y[d * 128 : (d + 1) * 128]).astype(bf16)
         for v in range(5):
-            put(d, v, [z[v * HB : (v + 1) * HB, b * LA : (b + 1) * LA] for b in range(BLOCKS)])
+            put(d, v, [z[v * HB : (v + 1) * HB, b * LA : (b + 1) * LA] for b in range(BLOCKS + 1)])
 
 
 def with_before(x):
     return jnp.concatenate([x, jnp.concatenate([jnp.zeros_like(x[:HB]), x[:-HB]], axis=0)], axis=1)
+
+
+def first_layer_columns(a_ref, planes):
+    _, q = iotas((HB, LA))
+    times = [one_hot(q // CIN % 8 == t) for t in range(8)]
+    blocks = [one_hot(q // EDGE == b) for b in range(BLOCKS)]
+    cols = [[] for _ in range(11)]
+    for p, j in planes:
+        x = [a_ref[2 * j + kd, INPUT_ROWS[p, kh]] for kd, kh in TAPS]
+        edges = [y[ROWS:] for y in x]
+        eight = edges[0] * times[0]
+        for t in range(1, 8):
+            eight = eight + edges[t] * times[t]
+        x = [y[:ROWS] for y in x]
+        for y in (eight, edges[8] * times[0]):
+            x.append(jnp.concatenate([y * m for m in blocks], axis=0))
+        for col, y in zip(cols, x):
+            col.append(y)
+    return jnp.concatenate([jnp.concatenate(col, axis=0) for col in cols], axis=1)
 
 
 def band(taps, rows, cin, cols, cout, put):
@@ -160,7 +182,14 @@
 
     k1 = jnp.concatenate([k1_ref[t].astype(f32) for t in range(27) for _ in range(16 // CIN)], axis=0)
     k1 = spread(k1.astype(bf16), LH)
-    band(tiled(lambda t: k1[16 * t : 16 * (t + 1)], LA // 16), LA, CIN, LH, C1, puts(t1_ref, LA))
+    def put_own(tap, own, _):
+        t1_ref[LA * tap : LA * (tap + 1)] = own
+
+    band(tiled(lambda t: k1[16 * t : 16 * (t + 1)], LA // 16), LA, CIN, LH, C1, put_own)
+    _, q = iotas((LA, LH))
+    for i, taps in enumerate((range(8), [8] * 8)):
+        edge = jnp.concatenate([k1[48 * t : 48 * t + CIN] for _ in range(BLOCKS) for t in taps], axis=0)
+        t1_ref[LA * (9 + i) : LA * (10 + i)] = jnp.where(q < C1, edge, 0.0).astype(bf16)
     k2 = spread(k2_ref[...], LZ)
     band(tiled(lambda t: k2[C1 * t : C1 * (t + 1)], W1), LH, C1, LZ, C2, puts(t2_ref, LH))
     arrange_planes(lambda c: low_ref[c].reshape(3 * 128, 128), 3, put_from(0))
@@ -170,11 +199,7 @@
     r, _ = iotas((planes * ROWS, LH))
     keep = r % HB != 0
     for p in range(2):
-        cols = [
-            jnp.concatenate([with_before(a_ref[2 * j + kd, INPUT_ROWS[p, kh]]) for j in range(planes)], axis=0)
-            for kd, kh in TAPS
-        ]
-        linear = dot(jnp.concatenate(cols, axis=1), t1_ref[...])
+        linear = dot(first_layer_columns(a_ref, [(p, j) for j in range(planes)]), t1_ref[...])
         hidden = jnp.where(linear > 0, linear, SLOPE * linear).astype(bf16)
         variants = [(1, hidden)] if p == 0 else [(2, hidden), (0, shifted_down(hidden, keep))]
         for v, x in variants:
@@ -221,23 +246,23 @@
             delta_ref[d, b * HB : (b + 1) * HB] = (c * slope).astype(bf16)
 
 
-def diagonals(g, first, cells, cout, cin):
+def diagonals(x, before, cells, cout, cin):
     lanes = 2 * cells * cin
     _, q = iotas((cout, lanes))
     w = q // cin
     ahead = jnp.zeros((cout, lanes), f32)
-    behind = jnp.where(w == 2 * cells - 1, g[:cout, first + lanes : first + 2 * lanes], 0.0)
+    behind = jnp.zeros((cout, lanes), f32)
     for o in range(cells):
-        x = g[o * cout : (o + 1) * cout, first : first + lanes]
-        ahead = jnp.where(w // 2 == o, x, ahead)
+        y = x[o * cout : (o + 1) * cout]
+        ahead = jnp.where(w // 2 == o, y, ahead)
         if o:
-            behind = jnp.where(w == 2 * o - 1, x, behind)
-    return ahead, behind
-
-
-def width_sums(g, cells, cout, cin, place):
+            behind = jnp.where(w == 2 * o - 1, y, behind)
+    return ahead, behind + before
+
+
+def width_sums(own, before, cells, cout, cin, place):
     lanes = 2 * cells * cin
-    both = [diagonals(g, 2 * lanes * tap, cells, cout, cin) for tap in range(9)]
+    both = [diagonals(own(tap), before(tap), cells, cout, cin) for tap in range(9)]
     ahead, behind = place([x for x, _ in both]), place([x for _, x in both])
     r, q = iotas((2 * cin, lanes))
     pick = jnp.where((q // cin % 2 == r // cin) & (q % cin == r % cin), 1.0, 0.0)
@@ -253,7 +278,15 @@
     delta = jnp.concatenate([delta_ref[d] for d in range(d2n)], axis=0)
     g = dot_tn(delta, second_layer_columns(hh_ref, d2n))
     none = [jnp.zeros((3 * C2, LH), f32)]
-    (sums,) = width_sums(g, W2, C2, C1, lambda taps: [jnp.concatenate(taps + none, axis=0)])
+    _, q = iotas((C2, LH))
+    (sums,) = width_sums(
+        lambda tap: g[:, 2 * LH * tap : 2 * LH * tap + LH],
+        lambda tap: jnp.where(q // C1 == W1 - 1, g[:C2, 2 * LH * tap + LH : 2 * LH * (tap + 1)], 0.0),
+        W2,
+        C2,
+        C1,
+        lambda taps: [jnp.concatenate(taps + none, axis=0)],
+    )
     out_ref[...] = sums
     band_back(tiled(spread_back(k2_ref[...]), W2), LZ, C2, LH, C1, puts(t2b_ref, LZ))
     copy.wait()
@@ -291,17 +324,22 @@
             hidden = jnp.concatenate([hh_ref[j, 2 if p else 1] for _, j in here], axis=0)
             deltas.append((back * jnp.where(hidden.astype(f32) > 0, 1.0, SLOPE)).astype(bf16))
             planes += here
-    cols = [
-        jnp.concatenate([with_before(a_ref[2 * j + kd, INPUT_ROWS[p, kh]]) for p, j in planes], axis=0)
-        for kd, kh in TAPS
-    ]
-    g = dot_tn(jnp.concatenate(deltas, axis=0), jnp.concatenate(cols, axis=1))
+    g = dot_tn(jnp.concatenate(deltas, axis=0), first_layer_columns(a_ref, planes))
     before, after = [jnp.zeros((C2, LA), f32)], [jnp.zeros((128 - C2 - 3 * C1, LA), f32)]
 
     def place(taps):
         return [jnp.concatenate(before + taps[i : i + 3] + after, axis=0) for i in range(0, 9, 3)]
 
-    sums = jnp.concatenate(width_sums(g, W1, C1, CIN, place), axis=0)
+    _, q = iotas((C1, LA))
+    sums = width_sums(
+        lambda tap: g[:, LA * tap : LA * (tap + 1)],
+        lambda tap: jnp.where(q // CIN % 8 == tap % 8, g[:C1, LA * (9 + tap // 8) : LA * (10 + tap // 8)], 0.0),
+        W1,
+        C1,
+        CIN,
+        place,
+    )
+    sums = jnp.concatenate(sums, axis=0)
     out_ref[: 3 * C1] = two_ref[:, :128]
     out_ref[3 * C1 : 6 * C1] = two_ref[:, 128:256]
     out_ref[6 * C1 :] = two_ref[:, 256:] + sums
@@ -474,7 +512,7 @@
         forward_kernel,
         "forward",
         [
-            ((planes + 3, 5, ROWS, LA), bf16),
+            ((planes + 3, 5, ROWS + HB, LA), bf16),
             ((d1n + 1, 3, ROWS, LH), bf16),
             ((travelling, 128), bf16),
             ((d2n, ROWS, LZ), bf16),
@@ -484,8 +522,8 @@
         k1,
         k2,
         scratch=[
-            pltpu.VMEM((planes + 3, 5, ROWS, LA), bf16),
-            pltpu.VMEM((9 * 2 * LA, LH), bf16),
+            pltpu.VMEM((planes + 3, 5, ROWS + HB, LA), bf16),
+            pltpu.VMEM((11 * LA, LH), bf16),
             pltpu.VMEM((9 * 2 * LH, LZ), bf16),
             pltpu.SemaphoreType.DMA,
         ],

time: 53.1 us -> 52.7 us (level)
  waiting for transfers between devices: 17.1 us -> 16.1 us
  starting transfers between devices: 19.1 us -> 19.8 us
    ppermute x6, waiting for transfers between devices: 14.5 us -> 13.8 us  [with_partner(): lax.ppermute(block, ('dp', 'space'), [(i, i ^ bit) for i in range(count)])]
  transfers between devices with their start and end apart: 9 -> 9, of which waited for: 7 -> 7; matrix products, arithmetic and copies ran while one was open for 0% -> 0% of each run, Pallas kernels for 17% -> 18%
where the time goes in v3:
time: 52.7 us; the launch traced here: 52.5 us
  starting transfers between devices  19.8 us (38%)
  waiting for transfers between devices  16.1 us (31%)
  Pallas kernels  15.4 us (29%)
  between operations  0.89 us (2%)
    pallas_call x8, Pallas kernels, call(): pl.pallas_call(kernel, name=name, in_specs=[pl.BlockSpec(memory_space=plt...  15.4 us
    ppermute x6, waiting for transfers between devices, with_partner(): lax.ppermute(block, ('dp', 'space'), [(i, i ^ bit) for i in range(count)])  13.8 us
    ppermute x6, starting transfers between devices, with_partner(): lax.ppermute(block, ('dp', 'space'), [(i, i ^ bit) for i in range(count)])  8.7 us
    all_to_all x1, starting transfers between devices, local(): cot_here = lax.all_to_all(cot_rows, 'space', 0, 0, tiled=True)  7.21 us
    ppermute x2, starting transfers between devices, passed_along(): lax.ppermute(block, 'space', [(i - distance, i) for i in devices if i - d...  3.86 us
    all_to_all x1, waiting for transfers between devices, local(): cot_here = lax.all_to_all(cot_rows, 'space', 0, 0, tiled=True)  2.27 us
  transfers between devices with their start and end apart: 9, of which 7 were waited for; matrix products, arithmetic and copies ran while one was open for 0% of the time, Pallas kernels for 18%

profile of v3, /device:TPU:0, one launch (start us, length us, event | category | flops | bytes accessed | tf_op | source)
XLA Modules:
  0.0 52.5 jit_solution(4805462663301939353)
XLA Ops:
  0.6 2.6 %gather.1 = (bf16[4,8,128,128]{3,2,1,0:T(8,128)(2,1)S(1)}, bf16[16,4,1024]{2,1,0:T(4,128)(2,1)}, bf16[27,4,16]{2,1,0:T(4,128)(2,1)S(1)}, bf16[432,32]{1,0:T(8,128)(2,1)S(1)}) custom-call(bf16[4,8,128,128]{3,2,1,0:T(8,128)(2,1)} %bitcast.46, bf16[32,32,64]{2,1,0:T(8,128)(2,1)} %bitcast.49, bf16[27,4,16]{2,1,0:T(4,128)(2,1)} %bitcast.61, bf16[432,32]{1,0:T(8,128)(2,1)} %bitcast.60), custom_call_target="tpu_custom_call" | custom-call | tf_op jit(solution)/shard_map/gather/pallas_call | solution.py:418
  3.2 2.4 %collective-permute-start = (bf16[4,3,128,128]{3,2,1,0:T(8,128)(2,1)S(1)}, bf16[4,3,128,128]{3,2,1,0:T(8,128)(2,1)S(1)}, u32[]{:S(2)}, u32[]{:S(2)}) collective-permute-start(bf16[4,3,128,128]{3,2,1,0:T(8,128)(2,1)S(1)} %last_planes.1), channel_id=1, source_target_pairs={{0,1},{1,2},{2,3},{3,4},{4,5},{5,6},{6,7},{7,8},{8,9},{9,10},{10,1... | collective-permute-start | bytes 1179656 | tf_op jit(solution)/shard_map/ppermute | solution.py:436
  5.6 7.2 %all-to-all-start = ((bf16[16,4,1024]{2,1,0:T(4,128)(2,1)}), bf16[16,4,1024]{2,1,0:T(4,128)(2,1)S(1)}, u32[]{:S(2)}, u32[]{:S(2)}) async-start(bf16[16,4,1024]{2,1,0:T(4,128)(2,1)} %get-tuple-element.22), calls=%async_computation | async-start | bytes 262144 | tf_op jit(solution)/shard_map/all_to_all | solution.py:509
  12.9 0.0 collective-permute-done.low_ref
  12.9 5.6 %forward.1 = (bf16[11,5,160,128]{3,2,1,0:T(8,128)(2,1)}, bf16[5,3,128,256]{3,2,1,0:T(8,128)(2,1)S(1)}, bf16[512,128]{1,0:T(8,128)(2,1)S(1)}, bf16[2,128,256]{2,1,0:T(8,128)(2,1)S(1)}) custom-call(bf16[4,8,128,128]{3,2,1,0:T(8,128)(2,1)S(1)} %get-tuple-element.18.vol_ref, bf16[4,3,128,128]{3,2,1,0:T(8,128)(2,1)S(1)} %collective-permute-done.low_ref, ...), custom_call_target="tpu_custom_call" | custom-call | tf_op jit(solution)/shard_map/forward/pallas_call | solution.py:418
  18.5 2.3 %all-to-all-done.cot_ref = bf16[16,4,1024]{2,1,0:T(4,128)(2,1)S(1)} async-done(((bf16[16,4,1024]{2,1,0:T(4,128)(2,1)}), bf16[16,4,1024]{2,1,0:T(4,128)(2,1)S(1)}, u32[]{:S(2)}, u32[]{:S(2)}) %all-to-all-start) | async-done | bytes 131104 | tf_op jit(solution)/shard_map/all_to_all | solution.py:509
  20.8 0.2 delta.1.delta_ref
  21.0 1.5 %collective-permute-start.1 = (bf16[128,256]{1,0:T(8,128)(2,1)S(1)}, bf16[128,256]{1,0:T(8,128)(2,1)S(1)}, u32[]{:S(2)}, u32[]{:S(2)}) collective-permute-start(bf16[128,256]{1,0:T(8,128)(2,1)S(1)} %slice_bitcast_fusion.2), channel_id=1, source_target_pairs={{1,0},{2,1},{3,2},{4,3},{5,4},{6,5},{7,6},{8,7},{9,8},{10,9},{11,1... | collective-permute-start | bytes 196616 | tf_op jit(solution)/shard_map/ppermute | solution.py:436
  22.5 2.1 %second_gradient.1 = (f32[48,384]{1,0:T(8,128)S(1)}, bf16[4608,256]{1,0:T(8,128)(2,1)S(1)}, bf16[11,5,160,128]{3,2,1,0:T(8,128)(2,1)S(1)}) custom-call(bf16[5,3,128,256]{3,2,1,0:T(8,128)(2,1)S(1)} %get-tuple-element.21.hh_ref, bf16[2,128,256]{2,1,0:T(8,128)(2,1)S(1)} %delta.1.delta_ref, bf16[432,32]{1,0:T(8,128)(2,1)S(1)} %get-tuple-element.20.k2_ref, ...), custom_call_target="tpu_custom_call" | custom-call | tf_op jit(solution)/shard_map/second_gradient/pallas_call | solution.py:418
  24.6 0.0 collective-permute-done.1.next_ref
  24.6 2.4 %first_gradient.1 = f32[144,128]{1,0:T(8,128)S(1)} custom-call(bf16[5,3,128,256]{3,2,1,0:T(8,128)(2,1)S(1)} %get-tuple-element.21.hh_ref, bf16[2,128,256]{2,1,0:T(8,128)(2,1)S(1)} %delta.1.delta_ref, bf16[128,256]{1,0:T(8,128)(2,1)S(1)} %collective-permute-done.1.next_ref, bf16[4608,256]{1,0:T(8,128)(2,1)S(1)} %get-tuple-element.25.t2b_ref, ...), custom_call_target="tpu_custom_call" | custom-call | tf_op jit(solution)/shard_map/first_gradient/pallas_call | solution.py:418
  27.0 1.4 %collective-permute-start.2 = (bf16[400,128]{1,0:T(8,128)(2,1)S(1)}, bf16[400,128]{1,0:T(8,128)(2,1)S(1)}, u32[]{:S(2)}, u32[]{:S(2)}) collective-permute-start(bf16[400,128]{1,0:T(8,128)(2,1)S(1)} %pad_maximum_fusion), channel_id=1, source_target_pairs={{0,1},{1,0},{2,3},{3,2},{4,5},{5,4},{6,7},{7,6},{8,9},{9,8},{10,11... | collective-permute-start | bytes 307208 | tf_op jit(solution)/shard_map/ppermute | solution.py:441
  28.4 0.9 %collective-permute-done.2 = bf16[400,128]{1,0:T(8,128)(2,1)S(1)} collective-permute-done((bf16[400,128]{1,0:T(8,128)(2,1)S(1)}, bf16[400,128]{1,0:T(8,128)(2,1)S(1)}, u32[]{:S(2)}, u32[]{:S(2)}) %collective-permute-start.2) | collective-permute-done | bytes 102432 | tf_op jit(solution)/shard_map/ppermute | solution.py:441
  29.5 1.7 %collective-permute-start.3 = (bf16[400,128]{1,0:T(8,128)(2,1)S(1)}, bf16[400,128]{1,0:T(8,128)(2,1)S(1)}, u32[]{:S(2)}, u32[]{:S(2)}) collective-permute-start(bf16[400,128]{1,0:T(8,128)(2,1)S(1)} %pad_maximum_fusion.1), channel_id=1, source_target_pairs={{0,2},{1,3},{2,0},{3,1},{4,6},{5,7},{6,4},{7,5},{8,10},{9,11},{10,... | collective-permute-start | bytes 307208 | tf_op jit(solution)/shard_map/ppermute | solution.py:441
  31.2 3.5 %collective-permute-done.3 = bf16[400,128]{1,0:T(8,128)(2,1)S(1)} collective-permute-done((bf16[400,128]{1,0:T(8,128)(2,1)S(1)}, bf16[400,128]{1,0:T(8,128)(2,1)S(1)}, u32[]{:S(2)}, u32[]{:S(2)}) %collective-permute-start.3) | collective-permute-done | bytes 102432 | tf_op jit(solution)/shard_map/ppermute | solution.py:441
  34.8 1.5 %collective-permute-start.4 = (bf16[400,128]{1,0:T(8,128)(2,1)S(1)}, bf16[400,128]{1,0:T(8,128)(2,1)S(1)}, u32[]{:S(2)}, u32[]{:S(2)}) collective-permute-start(bf16[400,128]{1,0:T(8,128)(2,1)S(1)} %pad_maximum_fusion.2), channel_id=1, source_target_pairs={{0,4},{1,5},{2,6},{3,7},{4,0},{5,1},{6,2},{7,3},{8,12},{9,13},{10,... | collective-permute-start | bytes 307208 | tf_op jit(solution)/shard_map/ppermute | solution.py:441
  36.4 3.2 %collective-permute-done.4 = bf16[400,128]{1,0:T(8,128)(2,1)S(1)} collective-permute-done((bf16[400,128]{1,0:T(8,128)(2,1)S(1)}, bf16[400,128]{1,0:T(8,128)(2,1)S(1)}, u32[]{:S(2)}, u32[]{:S(2)}) %collective-permute-start.4) | collective-permute-done | bytes 102432 | tf_op jit(solution)/shard_map/ppermute | solution.py:441
  39.6 2.5 %collective-permute-start.5 = (bf16[400,128]{1,0:T(8,128)(2,1)S(1)}, bf16[400,128]{1,0:T(8,128)(2,1)S(1)}, u32[]{:S(2)}, u32[]{:S(2)}) collective-permute-start(bf16[400,128]{1,0:T(8,128)(2,1)S(1)} %pad_maximum_fusion.3), channel_id=1, source_target_pairs={{0,8},{1,9},{2,10},{3,11},{4,12},{5,13},{6,14},{7,15},{8,0},{9,1},... | collective-permute-start | bytes 307208 | tf_op jit(solution)/shard_map/ppermute | solution.py:441
  42.2 4.2 %collective-permute-done.5 = bf16[400,128]{1,0:T(8,128)(2,1)S(1)} collective-permute-done((bf16[400,128]{1,0:T(8,128)(2,1)S(1)}, bf16[400,128]{1,0:T(8,128)(2,1)S(1)}, u32[]{:S(2)}, u32[]{:S(2)}) %collective-permute-start.5) | collective-permute-done | bytes 102432 | tf_op jit(solution)/shard_map/ppermute | solution.py:441
  46.4 1.6 %collective-permute-start.6 = (f32[72,128]{1,0:T(8,128)S(1)}, f32[72,128]{1,0:T(8,128)S(1)}, u32[]{:S(2)}, u32[]{:S(2)}) collective-permute-start(f32[72,128]{1,0:T(8,128)S(1)} %fusion.8), channel_id=1, source_target_pairs={{0,16},{1,17},{2,18},{3,19},{4,20},{5,21},{6,22},{7,23},{8,24},{9,... | collective-permute-start | bytes 110600 | tf_op jit(solution)/shard_map/ppermute | solution.py:441
  48.0 1.7 %scatter.1 = bf16[32,32,64]{2,1,0:T(8,128)(2,1)} custom-call(bf16[512,128]{1,0:T(8,128)(2,1)S(1)} %bitcast.44), custom_call_target="tpu_custom_call" | custom-call | tf_op jit(solution)/shard_map/scatter/pallas_call | solution.py:418
  49.7 0.8 %collective-permute-done.6 = f32[72,128]{1,0:T(8,128)S(1)} collective-permute-done((f32[72,128]{1,0:T(8,128)S(1)}, f32[72,128]{1,0:T(8,128)S(1)}, u32[]{:S(2)}, u32[]{:S(2)}) %collective-permute-start.6) | collective-permute-done | bytes 36896 | tf_op jit(solution)/shard_map/ppermute | solution.py:441
  50.4 0.0 collective-permute-start.7
  50.4 1.2 %collective-permute-done.7 = f32[72,128]{1,0:T(8,128)S(1)} collective-permute-done((f32[72,128]{1,0:T(8,128)S(1)}, f32[72,128]{1,0:T(8,128)S(1)}, u32[]{:S(2)}, u32[]{:S(2)}) %collective-permute-start.7) | collective-permute-done | bytes 36896 | tf_op jit(solution)/shard_map/ppermute | solution.py:441
  51.7 0.8 %scale.1 = (f32[27,4,16]{2,1,0:T(4,128)}, f32[27,16,32]{2,1,0:T(8,128)}) custom-call(f32[144,128]{1,0:T(8,128)S(1)} %maximum_select_fusion.4.sum_ref), custom_call_target="tpu_custom_call" | custom-call | tf_op jit(solution)/shard_map/scale/pallas_call | solution.py:418
  (30 shorter events, 0.4 us)
Async XLA Ops:
  3.2 9.6 %collective-permute-start = (bf16[4,3,128,128]{3,2,1,0:T(8,128)(2,1)S(1)}, bf16[4,3,128,128]{3,2,1,0:T(8,128)(2,1)S(1)}, u32[]{:S(2)}, u32[]{:S(2)}) collective-permute-start(bf16[4,3,128,128]{3,2,1,0:T(8,128)(2,1)S(1)} %last_planes.1), channel_id=1, source_target_pairs={{0,1},{1,2},{2,3},{3,4},{4,5},{5,6},{6,7},{7,8},{8,9},{9,10},{10,1... | collective-permute-start | bytes 1179656 | tf_op jit(solution)/shard_map/ppermute | solution.py:436
  5.6 15.2 %all-to-all-start = ((bf16[16,4,1024]{2,1,0:T(4,128)(2,1)}), bf16[16,4,1024]{2,1,0:T(4,128)(2,1)S(1)}, u32[]{:S(2)}, u32[]{:S(2)}) async-start(bf16[16,4,1024]{2,1,0:T(4,128)(2,1)} %get-tuple-element.22), calls=%async_computation | async-start | bytes 262144 | tf_op jit(solution)/shard_map/all_to_all | solution.py:509
  21.0 3.6 %collective-permute-start.1 = (bf16[128,256]{1,0:T(8,128)(2,1)S(1)}, bf16[128,256]{1,0:T(8,128)(2,1)S(1)}, u32[]{:S(2)}, u32[]{:S(2)}) collective-permute-start(bf16[128,256]{1,0:T(8,128)(2,1)S(1)} %slice_bitcast_fusion.2), channel_id=1, source_target_pairs={{1,0},{2,1},{3,2},{4,3},{5,4},{6,5},{7,6},{8,7},{9,8},{10,9},{11,1... | collective-permute-start | bytes 196616 | tf_op jit(solution)/shard_map/ppermute | solution.py:436
  27.0 2.3 %collective-permute-start.2 = (bf16[400,128]{1,0:T(8,128)(2,1)S(1)}, bf16[400,128]{1,0:T(8,128)(2,1)S(1)}, u32[]{:S(2)}, u32[]{:S(2)}) collective-permute-start(bf16[400,128]{1,0:T(8,128)(2,1)S(1)} %pad_maximum_fusion), channel_id=1, source_target_pairs={{0,1},{1,0},{2,3},{3,2},{4,5},{5,4},{6,7},{7,6},{8,9},{9,8},{10,11... | collective-permute-start | bytes 307208 | tf_op jit(solution)/shard_map/ppermute | solution.py:441
  29.5 5.2 %collective-permute-start.3 = (bf16[400,128]{1,0:T(8,128)(2,1)S(1)}, bf16[400,128]{1,0:T(8,128)(2,1)S(1)}, u32[]{:S(2)}, u32[]{:S(2)}) collective-permute-start(bf16[400,128]{1,0:T(8,128)(2,1)S(1)} %pad_maximum_fusion.1), channel_id=1, source_target_pairs={{0,2},{1,3},{2,0},{3,1},{4,6},{5,7},{6,4},{7,5},{8,10},{9,11},{10,... | collective-permute-start | bytes 307208 | tf_op jit(solution)/shard_map/ppermute | solution.py:441
  34.8 4.7 %collective-permute-start.4 = (bf16[400,128]{1,0:T(8,128)(2,1)S(1)}, bf16[400,128]{1,0:T(8,128)(2,1)S(1)}, u32[]{:S(2)}, u32[]{:S(2)}) collective-permute-start(bf16[400,128]{1,0:T(8,128)(2,1)S(1)} %pad_maximum_fusion.2), channel_id=1, source_target_pairs={{0,4},{1,5},{2,6},{3,7},{4,0},{5,1},{6,2},{7,3},{8,12},{9,13},{10,... | collective-permute-start | bytes 307208 | tf_op jit(solution)/shard_map/ppermute | solution.py:441
  39.6 6.7 %collective-permute-start.5 = (bf16[400,128]{1,0:T(8,128)(2,1)S(1)}, bf16[400,128]{1,0:T(8,128)(2,1)S(1)}, u32[]{:S(2)}, u32[]{:S(2)}) collective-permute-start(bf16[400,128]{1,0:T(8,128)(2,1)S(1)} %pad_maximum_fusion.3), channel_id=1, source_target_pairs={{0,8},{1,9},{2,10},{3,11},{4,12},{5,13},{6,14},{7,15},{8,0},{9,1},... | collective-permute-start | bytes 307208 | tf_op jit(solution)/shard_map/ppermute | solution.py:441
  46.4 4.0 %collective-permute-start.6 = (f32[72,128]{1,0:T(8,128)S(1)}, f32[72,128]{1,0:T(8,128)S(1)}, u32[]{:S(2)}, u32[]{:S(2)}) collective-permute-start(f32[72,128]{1,0:T(8,128)S(1)} %fusion.8), channel_id=1, source_target_pairs={{0,16},{1,17},{2,18},{3,19},{4,20},{5,21},{6,22},{7,23},{8,24},{9,... | collective-permute-start | bytes 110600 | tf_op jit(solution)/shard_map/ppermute | solution.py:441
  50.4 1.2 %collective-permute-start.7 = (f32[72,128]{1,0:T(8,128)S(1)}, f32[72,128]{1,0:T(8,128)S(1)}, u32[]{:S(2)}, u32[]{:S(2)}) collective-permute-start(f32[72,128]{1,0:T(8,128)S(1)} %add.70), channel_id=1, source_target_pairs={{0,1},{1,0},{2,3},{3,2},{4,5},{5,4},{6,7},{7,6},{8,9},{9,8},{10,11... | collective-permute-start | bytes 110600 | tf_op jit(solution)/shard_map/ppermute | solution.py:441

commit v4 on v3

--- a/solution.py
+++ b/solution.py
@@ -467,16 +467,17 @@
         came = got[:first].reshape(kept.shape)
         blocks = jnp.where(mine, jnp.stack([kept, came], 1), jnp.stack([came, kept], 1))
         bit *= 2
-    while bit < devices * lax.axis_size("dp"):
+    while 2 * bit < devices * lax.axis_size("dp"):
         terms = terms + with_partner(terms, bit)
         bit *= 2
-    return terms, blocks.reshape(rows.shape)
-
-
-def rejoined(half):
-    other = with_partner(half, 1)
+    beyond = [with_partner(terms, mask) for mask in (bit, 1, bit ^ 1)]
+    return terms, beyond, blocks.reshape(rows.shape)
+
+
+def rejoined(terms, beyond):
+    mine, other = terms + beyond[0], beyond[1] + beyond[2]
     even = lax.axis_index("space") % 2 == 0
-    return jnp.where(even, jnp.concatenate([half, other], 0), jnp.concatenate([other, half], 0))
+    return jnp.where(even, jnp.concatenate([mine, other], 0), jnp.concatenate([other, mine], 0))
 
 
 def local(volumes, kernel_one, kernel_two, cotangent):
@@ -554,10 +555,9 @@
         term_two,
         scratch=[pltpu.VMEM((d2n + 1, 2, ROWS, 2 * LZ), bf16)],
     )
-    half, got = total_and_exchange(terms, send)
+    terms, beyond, got = total_and_exchange(terms, send)
     (out,) = call(functools.partial(scatter_kernel, d2n), "scatter", [((C2, depth, cells), bf16)], got)
-    half, out = lax.optimization_barrier((half, out))
-    terms = rejoined(half)
+    terms = rejoined(terms, beyond)
     count = volumes.shape[0] * lax.axis_size("dp")
     factor = 1.0 / math.sqrt(count * depth * (height // 4) ** 2)
     one, two = call(

time: 52.7 us -> 52.5 us (level)
  waiting for transfers between devices: 16.1 us -> 15.1 us
  starting transfers between devices: 19.8 us -> 20.4 us
    ppermute x6 -> x7, waiting for transfers between devices: 13.8 us -> 12.8 us  [with_partner(): lax.ppermute(block, ('dp', 'space'), [(i, i ^ bit) for i in range(count)])]
    ppermute x6 -> x7, starting transfers between devices: 8.7 us -> 9.34 us  [with_partner(): lax.ppermute(block, ('dp', 'space'), [(i, i ^ bit) for i in range(count)])]
  transfers between devices with their start and end apart: 9 -> 10, of which waited for: 7 -> 7; matrix products, arithmetic and copies ran while one was open for 0% -> 0% of each run, Pallas kernels for 18% -> 18%
where the time goes in v4:
time: 52.5 us; the launch traced here: 52.2 us
  starting transfers between devices  20.4 us (39%)
  Pallas kernels  15.4 us (29%)
  waiting for transfers between devices  15.1 us (29%)
  between operations  0.88 us (2%)
    pallas_call x8, Pallas kernels, call(): pl.pallas_call(kernel, name=name, in_specs=[pl.BlockSpec(memory_space=plt...  15.4 us
    ppermute x7, waiting for transfers between devices, with_partner(): lax.ppermute(block, ('dp', 'space'), [(i, i ^ bit) for i in range(count)])  12.8 us
    ppermute x7, starting transfers between devices, with_partner(): lax.ppermute(block, ('dp', 'space'), [(i, i ^ bit) for i in range(count)])  9.34 us
    all_to_all x1, starting transfers between devices, local(): cot_here = lax.all_to_all(cot_rows, 'space', 0, 0, tiled=True)  7.21 us
    ppermute x2, starting transfers between devices, passed_along(): lax.ppermute(block, 'space', [(i - distance, i) for i in devices if i - d...  3.86 us
    all_to_all x1, waiting for transfers between devices, local(): cot_here = lax.all_to_all(cot_rows, 'space', 0, 0, tiled=True)  2.27 us
  transfers between devices with their start and end apart: 10, of which 7 were waited for; matrix products, arithmetic and copies ran while one was open for 0% of the time, Pallas kernels for 18%

profile of v4, /device:TPU:0, one launch (start us, length us, event | category | flops | bytes accessed | tf_op | source)
XLA Modules:
  0.0 52.2 jit_solution(16673349093037848516)
XLA Ops:
  0.6 2.6 %gather.1 = (bf16[4,8,128,128]{3,2,1,0:T(8,128)(2,1)S(1)}, bf16[16,4,1024]{2,1,0:T(4,128)(2,1)}, bf16[27,4,16]{2,1,0:T(4,128)(2,1)S(1)}, bf16[432,32]{1,0:T(8,128)(2,1)S(1)}) custom-call(bf16[4,8,128,128]{3,2,1,0:T(8,128)(2,1)} %bitcast.46, bf16[32,32,64]{2,1,0:T(8,128)(2,1)} %bitcast.49, bf16[27,4,16]{2,1,0:T(4,128)(2,1)} %bitcast.61, bf16[432,32]{1,0:T(8,128)(2,1)} %bitcast.60), custom_call_target="tpu_custom_call" | custom-call | tf_op jit(solution)/shard_map/gather/pallas_call | solution.py:418
  3.2 2.4 %collective-permute-start = (bf16[4,3,128,128]{3,2,1,0:T(8,128)(2,1)S(1)}, bf16[4,3,128,128]{3,2,1,0:T(8,128)(2,1)S(1)}, u32[]{:S(2)}, u32[]{:S(2)}) collective-permute-start(bf16[4,3,128,128]{3,2,1,0:T(8,128)(2,1)S(1)} %last_planes.1), channel_id=1, source_target_pairs={{0,1},{1,2},{2,3},{3,4},{4,5},{5,6},{6,7},{7,8},{8,9},{9,10},{10,1... | collective-permute-start | bytes 1179656 | tf_op jit(solution)/shard_map/ppermute | solution.py:436
  5.6 7.2 %all-to-all-start = ((bf16[16,4,1024]{2,1,0:T(4,128)(2,1)}), bf16[16,4,1024]{2,1,0:T(4,128)(2,1)S(1)}, u32[]{:S(2)}, u32[]{:S(2)}) async-start(bf16[16,4,1024]{2,1,0:T(4,128)(2,1)} %get-tuple-element.21), calls=%async_computation | async-start | bytes 262144 | tf_op jit(solution)/shard_map/all_to_all | solution.py:510
  12.9 0.0 collective-permute-done.low_ref
  12.9 5.6 %forward.1 = (bf16[11,5,160,128]{3,2,1,0:T(8,128)(2,1)}, bf16[5,3,128,256]{3,2,1,0:T(8,128)(2,1)S(1)}, bf16[512,128]{1,0:T(8,128)(2,1)S(1)}, bf16[2,128,256]{2,1,0:T(8,128)(2,1)S(1)}) custom-call(bf16[4,8,128,128]{3,2,1,0:T(8,128)(2,1)S(1)} %get-tuple-element.16.vol_ref, bf16[4,3,128,128]{3,2,1,0:T(8,128)(2,1)S(1)} %collective-permute-done.low_ref, ...), custom_call_target="tpu_custom_call" | custom-call | tf_op jit(solution)/shard_map/forward/pallas_call | solution.py:418
  18.5 2.3 %all-to-all-done.cot_ref = bf16[16,4,1024]{2,1,0:T(4,128)(2,1)S(1)} async-done(((bf16[16,4,1024]{2,1,0:T(4,128)(2,1)}), bf16[16,4,1024]{2,1,0:T(4,128)(2,1)S(1)}, u32[]{:S(2)}, u32[]{:S(2)}) %all-to-all-start) | async-done | bytes 131104 | tf_op jit(solution)/shard_map/all_to_all | solution.py:510
  20.8 0.2 delta.1.delta_ref
  21.0 1.5 %collective-permute-start.1 = (bf16[128,256]{1,0:T(8,128)(2,1)S(1)}, bf16[128,256]{1,0:T(8,128)(2,1)S(1)}, u32[]{:S(2)}, u32[]{:S(2)}) collective-permute-start(bf16[128,256]{1,0:T(8,128)(2,1)S(1)} %slice_bitcast_fusion), channel_id=1, source_target_pairs={{1,0},{2,1},{3,2},{4,3},{5,4},{6,5},{7,6},{8,7},{9,8},{10,9},{11,1... | collective-permute-start | bytes 196616 | tf_op jit(solution)/shard_map/ppermute | solution.py:436
  22.5 2.1 %second_gradient.1 = (f32[48,384]{1,0:T(8,128)S(1)}, bf16[4608,256]{1,0:T(8,128)(2,1)S(1)}, bf16[11,5,160,128]{3,2,1,0:T(8,128)(2,1)S(1)}) custom-call(bf16[5,3,128,256]{3,2,1,0:T(8,128)(2,1)S(1)} %get-tuple-element.20.hh_ref, bf16[2,128,256]{2,1,0:T(8,128)(2,1)S(1)} %delta.1.delta_ref, bf16[432,32]{1,0:T(8,128)(2,1)S(1)} %get-tuple-element.18.k2_ref, ...), custom_call_target="tpu_custom_call" | custom-call | tf_op jit(solution)/shard_map/second_gradient/pallas_call | solution.py:418
  24.6 0.0 collective-permute-done.1.next_ref
  24.6 2.4 %first_gradient.1 = f32[144,128]{1,0:T(8,128)S(1)} custom-call(bf16[5,3,128,256]{3,2,1,0:T(8,128)(2,1)S(1)} %get-tuple-element.20.hh_ref, bf16[2,128,256]{2,1,0:T(8,128)(2,1)S(1)} %delta.1.delta_ref, bf16[128,256]{1,0:T(8,128)(2,1)S(1)} %collective-permute-done.1.next_ref, bf16[4608,256]{1,0:T(8,128)(2,1)S(1)} %get-tuple-element.24.t2b_ref, ...), custom_call_target="tpu_custom_call" | custom-call | tf_op jit(solution)/shard_map/first_gradient/pallas_call | solution.py:418
  27.0 1.4 %collective-permute-start.2 = (bf16[400,128]{1,0:T(8,128)(2,1)S(1)}, bf16[400,128]{1,0:T(8,128)(2,1)S(1)}, u32[]{:S(2)}, u32[]{:S(2)}) collective-permute-start(bf16[400,128]{1,0:T(8,128)(2,1)S(1)} %pad_maximum_fusion), channel_id=1, source_target_pairs={{0,1},{1,0},{2,3},{3,2},{4,5},{5,4},{6,7},{7,6},{8,9},{9,8},{10,11... | collective-permute-start | bytes 307208 | tf_op jit(solution)/shard_map/ppermute | solution.py:441
  28.4 0.9 %collective-permute-done.2 = bf16[400,128]{1,0:T(8,128)(2,1)S(1)} collective-permute-done((bf16[400,128]{1,0:T(8,128)(2,1)S(1)}, bf16[400,128]{1,0:T(8,128)(2,1)S(1)}, u32[]{:S(2)}, u32[]{:S(2)}) %collective-permute-start.2) | collective-permute-done | bytes 102432 | tf_op jit(solution)/shard_map/ppermute | solution.py:441
  29.5 1.7 %collective-permute-start.3 = (bf16[400,128]{1,0:T(8,128)(2,1)S(1)}, bf16[400,128]{1,0:T(8,128)(2,1)S(1)}, u32[]{:S(2)}, u32[]{:S(2)}) collective-permute-start(bf16[400,128]{1,0:T(8,128)(2,1)S(1)} %pad_maximum_fusion.1), channel_id=1, source_target_pairs={{0,2},{1,3},{2,0},{3,1},{4,6},{5,7},{6,4},{7,5},{8,10},{9,11},{10,... | collective-permute-start | bytes 307208 | tf_op jit(solution)/shard_map/ppermute | solution.py:441
  31.2 3.5 %collective-permute-done.3 = bf16[400,128]{1,0:T(8,128)(2,1)S(1)} collective-permute-done((bf16[400,128]{1,0:T(8,128)(2,1)S(1)}, bf16[400,128]{1,0:T(8,128)(2,1)S(1)}, u32[]{:S(2)}, u32[]{:S(2)}) %collective-permute-start.3) | collective-permute-done | bytes 102432 | tf_op jit(solution)/shard_map/ppermute | solution.py:441
  34.8 1.5 %collective-permute-start.4 = (bf16[400,128]{1,0:T(8,128)(2,1)S(1)}, bf16[400,128]{1,0:T(8,128)(2,1)S(1)}, u32[]{:S(2)}, u32[]{:S(2)}) collective-permute-start(bf16[400,128]{1,0:T(8,128)(2,1)S(1)} %pad_maximum_fusion.2), channel_id=1, source_target_pairs={{0,4},{1,5},{2,6},{3,7},{4,0},{5,1},{6,2},{7,3},{8,12},{9,13},{10,... | collective-permute-start | bytes 307208 | tf_op jit(solution)/shard_map/ppermute | solution.py:441
  36.4 3.2 %collective-permute-done.4 = bf16[400,128]{1,0:T(8,128)(2,1)S(1)} collective-permute-done((bf16[400,128]{1,0:T(8,128)(2,1)S(1)}, bf16[400,128]{1,0:T(8,128)(2,1)S(1)}, u32[]{:S(2)}, u32[]{:S(2)}) %collective-permute-start.4) | collective-permute-done | bytes 102432 | tf_op jit(solution)/shard_map/ppermute | solution.py:441
  39.6 2.5 %collective-permute-start.5 = (bf16[400,128]{1,0:T(8,128)(2,1)S(1)}, bf16[400,128]{1,0:T(8,128)(2,1)S(1)}, u32[]{:S(2)}, u32[]{:S(2)}) collective-permute-start(bf16[400,128]{1,0:T(8,128)(2,1)S(1)} %pad_maximum_fusion.3), channel_id=1, source_target_pairs={{0,8},{1,9},{2,10},{3,11},{4,12},{5,13},{6,14},{7,15},{8,0},{9,1},... | collective-permute-start | bytes 307208 | tf_op jit(solution)/shard_map/ppermute | solution.py:441
  42.2 4.2 %collective-permute-done.5 = bf16[400,128]{1,0:T(8,128)(2,1)S(1)} collective-permute-done((bf16[400,128]{1,0:T(8,128)(2,1)S(1)}, bf16[400,128]{1,0:T(8,128)(2,1)S(1)}, u32[]{:S(2)}, u32[]{:S(2)}) %collective-permute-start.5) | collective-permute-done | bytes 102432 | tf_op jit(solution)/shard_map/ppermute | solution.py:441
  46.4 1.6 %collective-permute-start.6 = (f32[72,128]{1,0:T(8,128)S(1)}, f32[72,128]{1,0:T(8,128)S(1)}, u32[]{:S(2)}, u32[]{:S(2)}) collective-permute-start(f32[72,128]{1,0:T(8,128)S(1)} %fusion.8), channel_id=1, source_target_pairs={{0,16},{1,17},{2,18},{3,19},{4,20},{5,21},{6,22},{7,23},{8,24},{9,... | collective-permute-start | bytes 110600 | tf_op jit(solution)/shard_map/ppermute | solution.py:441
  48.0 0.0 collective-permute-start.7
  48.0 0.6 %collective-permute-start.8 = (f32[72,128]{1,0:T(8,128)S(1)}, f32[72,128]{1,0:T(8,128)S(1)}, u32[]{:S(2)}, u32[]{:S(2)}) collective-permute-start(f32[72,128]{1,0:T(8,128)S(1)} %fusion.8), channel_id=1, source_target_pairs={{0,17},{1,16},{2,19},{3,18},{4,21},{5,20},{6,23},{7,22},{8,25},{9,... | collective-permute-start | bytes 110600 | tf_op jit(solution)/shard_map/ppermute | solution.py:441
  48.6 1.7 %scatter.1 = bf16[32,32,64]{2,1,0:T(8,128)(2,1)} custom-call(bf16[512,128]{1,0:T(8,128)(2,1)S(1)} %bitcast.44), custom_call_target="tpu_custom_call" | custom-call | tf_op jit(solution)/shard_map/scatter/pallas_call | solution.py:418
  50.3 0.1 collective-permute-done.6
  50.4 0.0 collective-permute-done.7
  50.4 0.9 %collective-permute-done.8 = f32[72,128]{1,0:T(8,128)S(1)} collective-permute-done((f32[72,128]{1,0:T(8,128)S(1)}, f32[72,128]{1,0:T(8,128)S(1)}, u32[]{:S(2)}, u32[]{:S(2)}) %collective-permute-start.8) | collective-permute-done | bytes 36896 | tf_op jit(solution)/shard_map/ppermute | solution.py:441
  51.4 0.8 %scale.1 = (f32[27,4,16]{2,1,0:T(4,128)}, f32[27,16,32]{2,1,0:T(8,128)}) custom-call(f32[144,128]{1,0:T(8,128)S(1)} %maximum_select_fusion.4.sum_ref), custom_call_target="tpu_custom_call" | custom-call | tf_op jit(solution)/shard_map/scale/pallas_call | solution.py:418
  (31 shorter events, 0.4 us)
Async XLA Ops:
  3.2 9.6 %collective-permute-start = (bf16[4,3,128,128]{3,2,1,0:T(8,128)(2,1)S(1)}, bf16[4,3,128,128]{3,2,1,0:T(8,128)(2,1)S(1)}, u32[]{:S(2)}, u32[]{:S(2)}) collective-permute-start(bf16[4,3,128,128]{3,2,1,0:T(8,128)(2,1)S(1)} %last_planes.1), channel_id=1, source_target_pairs={{0,1},{1,2},{2,3},{3,4},{4,5},{5,6},{6,7},{7,8},{8,9},{9,10},{10,1... | collective-permute-start | bytes 1179656 | tf_op jit(solution)/shard_map/ppermute | solution.py:436
  5.6 15.2 %all-to-all-start = ((bf16[16,4,1024]{2,1,0:T(4,128)(2,1)}), bf16[16,4,1024]{2,1,0:T(4,128)(2,1)S(1)}, u32[]{:S(2)}, u32[]{:S(2)}) async-start(bf16[16,4,1024]{2,1,0:T(4,128)(2,1)} %get-tuple-element.21), calls=%async_computation | async-start | bytes 262144 | tf_op jit(solution)/shard_map/all_to_all | solution.py:510
  21.0 3.6 %collective-permute-start.1 = (bf16[128,256]{1,0:T(8,128)(2,1)S(1)}, bf16[128,256]{1,0:T(8,128)(2,1)S(1)}, u32[]{:S(2)}, u32[]{:S(2)}) collective-permute-start(bf16[128,256]{1,0:T(8,128)(2,1)S(1)} %slice_bitcast_fusion), channel_id=1, source_target_pairs={{1,0},{2,1},{3,2},{4,3},{5,4},{6,5},{7,6},{8,7},{9,8},{10,9},{11,1... | collective-permute-start | bytes 196616 | tf_op jit(solution)/shard_map/ppermute | solution.py:436
  27.0 2.3 %collective-permute-start.2 = (bf16[400,128]{1,0:T(8,128)(2,1)S(1)}, bf16[400,128]{1,0:T(8,128)(2,1)S(1)}, u32[]{:S(2)}, u32[]{:S(2)}) collective-permute-start(bf16[400,128]{1,0:T(8,128)(2,1)S(1)} %pad_maximum_fusion), channel_id=1, source_target_pairs={{0,1},{1,0},{2,3},{3,2},{4,5},{5,4},{6,7},{7,6},{8,9},{9,8},{10,11... | collective-permute-start | bytes 307208 | tf_op jit(solution)/shard_map/ppermute | solution.py:441
  29.5 5.2 %collective-permute-start.3 = (bf16[400,128]{1,0:T(8,128)(2,1)S(1)}, bf16[400,128]{1,0:T(8,128)(2,1)S(1)}, u32[]{:S(2)}, u32[]{:S(2)}) collective-permute-start(bf16[400,128]{1,0:T(8,128)(2,1)S(1)} %pad_maximum_fusion.1), channel_id=1, source_target_pairs={{0,2},{1,3},{2,0},{3,1},{4,6},{5,7},{6,4},{7,5},{8,10},{9,11},{10,... | collective-permute-start | bytes 307208 | tf_op jit(solution)/shard_map/ppermute | solution.py:441
  34.8 4.7 %collective-permute-start.4 = (bf16[400,128]{1,0:T(8,128)(2,1)S(1)}, bf16[400,128]{1,0:T(8,128)(2,1)S(1)}, u32[]{:S(2)}, u32[]{:S(2)}) collective-permute-start(bf16[400,128]{1,0:T(8,128)(2,1)S(1)} %pad_maximum_fusion.2), channel_id=1, source_target_pairs={{0,4},{1,5},{2,6},{3,7},{4,0},{5,1},{6,2},{7,3},{8,12},{9,13},{10,... | collective-permute-start | bytes 307208 | tf_op jit(solution)/shard_map/ppermute | solution.py:441
  39.6 6.7 %collective-permute-start.5 = (bf16[400,128]{1,0:T(8,128)(2,1)S(1)}, bf16[400,128]{1,0:T(8,128)(2,1)S(1)}, u32[]{:S(2)}, u32[]{:S(2)}) collective-permute-start(bf16[400,128]{1,0:T(8,128)(2,1)S(1)} %pad_maximum_fusion.3), channel_id=1, source_target_pairs={{0,8},{1,9},{2,10},{3,11},{4,12},{5,13},{6,14},{7,15},{8,0},{9,1},... | collective-permute-start | bytes 307208 | tf_op jit(solution)/shard_map/ppermute | solution.py:441
  46.4 4.0 %collective-permute-start.6 = (f32[72,128]{1,0:T(8,128)S(1)}, f32[72,128]{1,0:T(8,128)S(1)}, u32[]{:S(2)}, u32[]{:S(2)}) collective-permute-start(f32[72,128]{1,0:T(8,128)S(1)} %fusion.8), channel_id=1, source_target_pairs={{0,16},{1,17},{2,18},{3,19},{4,20},{5,21},{6,22},{7,23},{8,24},{9,... | collective-permute-start | bytes 110600 | tf_op jit(solution)/shard_map/ppermute | solution.py:441
  48.0 2.5 %collective-permute-start.7 = (f32[72,128]{1,0:T(8,128)S(1)}, f32[72,128]{1,0:T(8,128)S(1)}, u32[]{:S(2)}, u32[]{:S(2)}) collective-permute-start(f32[72,128]{1,0:T(8,128)S(1)} %fusion.8), channel_id=1, source_target_pairs={{0,1},{1,0},{2,3},{3,2},{4,5},{5,4},{6,7},{7,6},{8,9},{9,8},{10,11... | collective-permute-start | bytes 110600 | tf_op jit(solution)/shard_map/ppermute | solution.py:441
  48.0 3.4 %collective-permute-start.8 = (f32[72,128]{1,0:T(8,128)S(1)}, f32[72,128]{1,0:T(8,128)S(1)}, u32[]{:S(2)}, u32[]{:S(2)}) collective-permute-start(f32[72,128]{1,0:T(8,128)S(1)} %fusion.8), channel_id=1, source_target_pairs={{0,17},{1,16},{2,19},{3,18},{4,21},{5,20},{6,23},{7,22},{8,25},{9,... | collective-permute-start | bytes 110600 | tf_op jit(solution)/shard_map/ppermute | solution.py:441

commit v5 on v4

--- a/solution.py
+++ b/solution.py
@@ -37,9 +37,13 @@
 
 
 def exact_nt(a, b):
-    return lax.dot_general(
-        a, b, (((1,), (1,)), ((), ())), precision=lax.Precision.HIGHEST, preferred_element_type=f32
-    )
+    a = a.astype(bf16)
+    total = None
+    for _ in range(3):
+        part = b.astype(bf16)
+        b = b - part.astype(f32)
+        total = dot_nt(a, part) if total is None else total + dot_nt(a, part)
+    return total
 
 
 def iotas(shape):

time: 52.5 us -> 52.4 us (level)
  no operation moved by 1% of the time
where the time goes in v5:
time: 52.4 us; the launch traced here: 52.1 us
  starting transfers between devices  20.6 us (39%)
  Pallas kernels  15.1 us (29%)
  waiting for transfers between devices  15.1 us (29%)
  between operations  0.88 us (2%)
    pallas_call x8, Pallas kernels, call(): pl.pallas_call(kernel, name=name, in_specs=[pl.BlockSpec(memory_space=plt...  15.1 us
    ppermute x7, waiting for transfers between devices, with_partner(): lax.ppermute(block, ('dp', 'space'), [(i, i ^ bit) for i in range(count)])  12.8 us
    ppermute x7, starting transfers between devices, with_partner(): lax.ppermute(block, ('dp', 'space'), [(i, i ^ bit) for i in range(count)])  9.73 us
    all_to_all x1, starting transfers between devices, local(): cot_here = lax.all_to_all(cot_rows, 'space', 0, 0, tiled=True)  7.21 us
    ppermute x2, starting transfers between devices, passed_along(): lax.ppermute(block, 'space', [(i - distance, i) for i in devices if i - d...  3.67 us
    all_to_all x1, waiting for transfers between devices, local(): cot_here = lax.all_to_all(cot_rows, 'space', 0, 0, tiled=True)  2.27 us
  transfers between devices with their start and end apart: 10, of which 7 were waited for; matrix products, arithmetic and copies ran while one was open for 0% of the time, Pallas kernels for 18%

profile of v5, /device:TPU:0, one launch (start us, length us, event | category | flops | bytes accessed | tf_op | source)
XLA Modules:
  0.0 52.1 jit_solution(6088304577801963468)
XLA Ops:
  0.6 2.6 %gather.1 = (bf16[4,8,128,128]{3,2,1,0:T(8,128)(2,1)S(1)}, bf16[16,4,1024]{2,1,0:T(4,128)(2,1)}, bf16[27,4,16]{2,1,0:T(4,128)(2,1)S(1)}, bf16[432,32]{1,0:T(8,128)(2,1)S(1)}) custom-call(bf16[4,8,128,128]{3,2,1,0:T(8,128)(2,1)} %bitcast.46, bf16[32,32,64]{2,1,0:T(8,128)(2,1)} %bitcast.49, bf16[27,4,16]{2,1,0:T(4,128)(2,1)} %bitcast.61, bf16[432,32]{1,0:T(8,128)(2,1)} %bitcast.60), custom_call_target="tpu_custom_call" | custom-call | tf_op jit(solution)/shard_map/gather/pallas_call | solution.py:422
  3.2 2.4 %collective-permute-start = (bf16[4,3,128,128]{3,2,1,0:T(8,128)(2,1)S(1)}, bf16[4,3,128,128]{3,2,1,0:T(8,128)(2,1)S(1)}, u32[]{:S(2)}, u32[]{:S(2)}) collective-permute-start(bf16[4,3,128,128]{3,2,1,0:T(8,128)(2,1)S(1)} %last_planes.1), channel_id=1, source_target_pairs={{0,1},{1,2},{2,3},{3,4},{4,5},{5,6},{6,7},{7,8},{8,9},{9,10},{10,1... | collective-permute-start | bytes 1179656 | tf_op jit(solution)/shard_map/ppermute | solution.py:440
  5.6 7.2 %all-to-all-start = ((bf16[16,4,1024]{2,1,0:T(4,128)(2,1)}), bf16[16,4,1024]{2,1,0:T(4,128)(2,1)S(1)}, u32[]{:S(2)}, u32[]{:S(2)}) async-start(bf16[16,4,1024]{2,1,0:T(4,128)(2,1)} %get-tuple-element.21), calls=%async_computation | async-start | bytes 262144 | tf_op jit(solution)/shard_map/all_to_all | solution.py:514
  12.9 0.0 collective-permute-done.low_ref
  12.9 5.6 %forward.1 = (bf16[11,5,160,128]{3,2,1,0:T(8,128)(2,1)}, bf16[5,3,128,256]{3,2,1,0:T(8,128)(2,1)S(1)}, bf16[512,128]{1,0:T(8,128)(2,1)S(1)}, bf16[2,128,256]{2,1,0:T(8,128)(2,1)S(1)}) custom-call(bf16[4,8,128,128]{3,2,1,0:T(8,128)(2,1)S(1)} %get-tuple-element.16.vol_ref, bf16[4,3,128,128]{3,2,1,0:T(8,128)(2,1)S(1)} %collective-permute-done.low_ref, ...), custom_call_target="tpu_custom_call" | custom-call | tf_op jit(solution)/shard_map/forward/pallas_call | solution.py:422
  18.5 2.3 %all-to-all-done.cot_ref = bf16[16,4,1024]{2,1,0:T(4,128)(2,1)S(1)} async-done(((bf16[16,4,1024]{2,1,0:T(4,128)(2,1)}), bf16[16,4,1024]{2,1,0:T(4,128)(2,1)S(1)}, u32[]{:S(2)}, u32[]{:S(2)}) %all-to-all-start) | async-done | bytes 131104 | tf_op jit(solution)/shard_map/all_to_all | solution.py:514
  20.8 0.2 delta.1.delta_ref
  21.0 1.3 %collective-permute-start.1 = (bf16[128,256]{1,0:T(8,128)(2,1)S(1)}, bf16[128,256]{1,0:T(8,128)(2,1)S(1)}, u32[]{:S(2)}, u32[]{:S(2)}) collective-permute-start(bf16[128,256]{1,0:T(8,128)(2,1)S(1)} %slice_bitcast_fusion), channel_id=1, source_target_pairs={{1,0},{2,1},{3,2},{4,3},{5,4},{6,5},{7,6},{8,7},{9,8},{10,9},{11,1... | collective-permute-start | bytes 196616 | tf_op jit(solution)/shard_map/ppermute | solution.py:440
  22.3 1.9 %second_gradient.1 = (f32[48,384]{1,0:T(8,128)S(1)}, bf16[4608,256]{1,0:T(8,128)(2,1)S(1)}, bf16[11,5,160,128]{3,2,1,0:T(8,128)(2,1)S(1)}) custom-call(bf16[5,3,128,256]{3,2,1,0:T(8,128)(2,1)S(1)} %get-tuple-element.20.hh_ref, bf16[2,128,256]{2,1,0:T(8,128)(2,1)S(1)} %delta.1.delta_ref, bf16[432,32]{1,0:T(8,128)(2,1)S(1)} %get-tuple-element.18.k2_ref, ...), custom_call_target="tpu_custom_call" | custom-call | tf_op jit(solution)/shard_map/second_gradient/pallas_call | solution.py:422
  24.2 0.0 collective-permute-done.1.next_ref
  24.2 2.2 %first_gradient.1 = f32[144,128]{1,0:T(8,128)S(1)} custom-call(bf16[5,3,128,256]{3,2,1,0:T(8,128)(2,1)S(1)} %get-tuple-element.20.hh_ref, bf16[2,128,256]{2,1,0:T(8,128)(2,1)S(1)} %delta.1.delta_ref, bf16[128,256]{1,0:T(8,128)(2,1)S(1)} %collective-permute-done.1.next_ref, bf16[4608,256]{1,0:T(8,128)(2,1)S(1)} %get-tuple-element.24.t2b_ref, ...), custom_call_target="tpu_custom_call" | custom-call | tf_op jit(solution)/shard_map/first_gradient/pallas_call | solution.py:422
  26.5 1.7 %collective-permute-start.2 = (bf16[400,128]{1,0:T(8,128)(2,1)S(1)}, bf16[400,128]{1,0:T(8,128)(2,1)S(1)}, u32[]{:S(2)}, u32[]{:S(2)}) collective-permute-start(bf16[400,128]{1,0:T(8,128)(2,1)S(1)} %pad_maximum_fusion), channel_id=1, source_target_pairs={{0,1},{1,0},{2,3},{3,2},{4,5},{5,4},{6,7},{7,6},{8,9},{9,8},{10,11... | collective-permute-start | bytes 307208 | tf_op jit(solution)/shard_map/ppermute | solution.py:445
  28.3 0.9 %collective-permute-done.2 = bf16[400,128]{1,0:T(8,128)(2,1)S(1)} collective-permute-done((bf16[400,128]{1,0:T(8,128)(2,1)S(1)}, bf16[400,128]{1,0:T(8,128)(2,1)S(1)}, u32[]{:S(2)}, u32[]{:S(2)}) %collective-permute-start.2) | collective-permute-done | bytes 102432 | tf_op jit(solution)/shard_map/ppermute | solution.py:445
  29.4 1.7 %collective-permute-start.3 = (bf16[400,128]{1,0:T(8,128)(2,1)S(1)}, bf16[400,128]{1,0:T(8,128)(2,1)S(1)}, u32[]{:S(2)}, u32[]{:S(2)}) collective-permute-start(bf16[400,128]{1,0:T(8,128)(2,1)S(1)} %pad_maximum_fusion.1), channel_id=1, source_target_pairs={{0,2},{1,3},{2,0},{3,1},{4,6},{5,7},{6,4},{7,5},{8,10},{9,11},{10,... | collective-permute-start | bytes 307208 | tf_op jit(solution)/shard_map/ppermute | solution.py:445
  31.1 3.5 %collective-permute-done.3 = bf16[400,128]{1,0:T(8,128)(2,1)S(1)} collective-permute-done((bf16[400,128]{1,0:T(8,128)(2,1)S(1)}, bf16[400,128]{1,0:T(8,128)(2,1)S(1)}, u32[]{:S(2)}, u32[]{:S(2)}) %collective-permute-start.3) | collective-permute-done | bytes 102432 | tf_op jit(solution)/shard_map/ppermute | solution.py:445
  34.7 1.5 %collective-permute-start.4 = (bf16[400,128]{1,0:T(8,128)(2,1)S(1)}, bf16[400,128]{1,0:T(8,128)(2,1)S(1)}, u32[]{:S(2)}, u32[]{:S(2)}) collective-permute-start(bf16[400,128]{1,0:T(8,128)(2,1)S(1)} %pad_maximum_fusion.2), channel_id=1, source_target_pairs={{0,4},{1,5},{2,6},{3,7},{4,0},{5,1},{6,2},{7,3},{8,12},{9,13},{10,... | collective-permute-start | bytes 307208 | tf_op jit(solution)/shard_map/ppermute | solution.py:445
  36.2 3.2 %collective-permute-done.4 = bf16[400,128]{1,0:T(8,128)(2,1)S(1)} collective-permute-done((bf16[400,128]{1,0:T(8,128)(2,1)S(1)}, bf16[400,128]{1,0:T(8,128)(2,1)S(1)}, u32[]{:S(2)}, u32[]{:S(2)}) %collective-permute-start.4) | collective-permute-done | bytes 102432 | tf_op jit(solution)/shard_map/ppermute | solution.py:445
  39.5 2.5 %collective-permute-start.5 = (bf16[400,128]{1,0:T(8,128)(2,1)S(1)}, bf16[400,128]{1,0:T(8,128)(2,1)S(1)}, u32[]{:S(2)}, u32[]{:S(2)}) collective-permute-start(bf16[400,128]{1,0:T(8,128)(2,1)S(1)} %pad_maximum_fusion.3), channel_id=1, source_target_pairs={{0,8},{1,9},{2,10},{3,11},{4,12},{5,13},{6,14},{7,15},{8,0},{9,1},... | collective-permute-start | bytes 307208 | tf_op jit(solution)/shard_map/ppermute | solution.py:445
  42.1 4.2 %collective-permute-done.5 = bf16[400,128]{1,0:T(8,128)(2,1)S(1)} collective-permute-done((bf16[400,128]{1,0:T(8,128)(2,1)S(1)}, bf16[400,128]{1,0:T(8,128)(2,1)S(1)}, u32[]{:S(2)}, u32[]{:S(2)}) %collective-permute-start.5) | collective-permute-done | bytes 102432 | tf_op jit(solution)/shard_map/ppermute | solution.py:445
  46.3 1.6 %collective-permute-start.6 = (f32[72,128]{1,0:T(8,128)S(1)}, f32[72,128]{1,0:T(8,128)S(1)}, u32[]{:S(2)}, u32[]{:S(2)}) collective-permute-start(f32[72,128]{1,0:T(8,128)S(1)} %fusion.8), channel_id=1, source_target_pairs={{0,16},{1,17},{2,18},{3,19},{4,20},{5,21},{6,22},{7,23},{8,24},{9,... | collective-permute-start | bytes 110600 | tf_op jit(solution)/shard_map/ppermute | solution.py:445
  47.8 0.0 collective-permute-start.7
  47.8 0.6 %collective-permute-start.8 = (f32[72,128]{1,0:T(8,128)S(1)}, f32[72,128]{1,0:T(8,128)S(1)}, u32[]{:S(2)}, u32[]{:S(2)}) collective-permute-start(f32[72,128]{1,0:T(8,128)S(1)} %fusion.8), channel_id=1, source_target_pairs={{0,17},{1,16},{2,19},{3,18},{4,21},{5,20},{6,23},{7,22},{8,25},{9,... | collective-permute-start | bytes 110600 | tf_op jit(solution)/shard_map/ppermute | solution.py:445
  48.5 1.7 %scatter.1 = bf16[32,32,64]{2,1,0:T(8,128)(2,1)} custom-call(bf16[512,128]{1,0:T(8,128)(2,1)S(1)} %bitcast.44), custom_call_target="tpu_custom_call" | custom-call | tf_op jit(solution)/shard_map/scatter/pallas_call | solution.py:422
  50.2 0.1 collective-permute-done.6
  50.3 0.0 collective-permute-done.7
  50.3 0.9 %collective-permute-done.8 = f32[72,128]{1,0:T(8,128)S(1)} collective-permute-done((f32[72,128]{1,0:T(8,128)S(1)}, f32[72,128]{1,0:T(8,128)S(1)}, u32[]{:S(2)}, u32[]{:S(2)}) %collective-permute-start.8) | collective-permute-done | bytes 36896 | tf_op jit(solution)/shard_map/ppermute | solution.py:445
  51.2 0.8 %scale.1 = (f32[27,4,16]{2,1,0:T(4,128)}, f32[27,16,32]{2,1,0:T(8,128)}) custom-call(f32[144,128]{1,0:T(8,128)S(1)} %maximum_select_fusion.4.sum_ref), custom_call_target="tpu_custom_call" | custom-call | tf_op jit(solution)/shard_map/scale/pallas_call | solution.py:422
  (31 shorter events, 0.4 us)
Async XLA Ops:
  3.2 9.6 %collective-permute-start = (bf16[4,3,128,128]{3,2,1,0:T(8,128)(2,1)S(1)}, bf16[4,3,128,128]{3,2,1,0:T(8,128)(2,1)S(1)}, u32[]{:S(2)}, u32[]{:S(2)}) collective-permute-start(bf16[4,3,128,128]{3,2,1,0:T(8,128)(2,1)S(1)} %last_planes.1), channel_id=1, source_target_pairs={{0,1},{1,2},{2,3},{3,4},{4,5},{5,6},{6,7},{7,8},{8,9},{9,10},{10,1... | collective-permute-start | bytes 1179656 | tf_op jit(solution)/shard_map/ppermute | solution.py:440
  5.6 15.2 %all-to-all-start = ((bf16[16,4,1024]{2,1,0:T(4,128)(2,1)}), bf16[16,4,1024]{2,1,0:T(4,128)(2,1)S(1)}, u32[]{:S(2)}, u32[]{:S(2)}) async-start(bf16[16,4,1024]{2,1,0:T(4,128)(2,1)} %get-tuple-element.21), calls=%async_computation | async-start | bytes 262144 | tf_op jit(solution)/shard_map/all_to_all | solution.py:514
  21.0 3.2 %collective-permute-start.1 = (bf16[128,256]{1,0:T(8,128)(2,1)S(1)}, bf16[128,256]{1,0:T(8,128)(2,1)S(1)}, u32[]{:S(2)}, u32[]{:S(2)}) collective-permute-start(bf16[128,256]{1,0:T(8,128)(2,1)S(1)} %slice_bitcast_fusion), channel_id=1, source_target_pairs={{1,0},{2,1},{3,2},{4,3},{5,4},{6,5},{7,6},{8,7},{9,8},{10,9},{11,1... | collective-permute-start | bytes 196616 | tf_op jit(solution)/shard_map/ppermute | solution.py:440
  26.5 2.7 %collective-permute-start.2 = (bf16[400,128]{1,0:T(8,128)(2,1)S(1)}, bf16[400,128]{1,0:T(8,128)(2,1)S(1)}, u32[]{:S(2)}, u32[]{:S(2)}) collective-permute-start(bf16[400,128]{1,0:T(8,128)(2,1)S(1)} %pad_maximum_fusion), channel_id=1, source_target_pairs={{0,1},{1,0},{2,3},{3,2},{4,5},{5,4},{6,7},{7,6},{8,9},{9,8},{10,11... | collective-permute-start | bytes 307208 | tf_op jit(solution)/shard_map/ppermute | solution.py:445
  29.4 5.2 %collective-permute-start.3 = (bf16[400,128]{1,0:T(8,128)(2,1)S(1)}, bf16[400,128]{1,0:T(8,128)(2,1)S(1)}, u32[]{:S(2)}, u32[]{:S(2)}) collective-permute-start(bf16[400,128]{1,0:T(8,128)(2,1)S(1)} %pad_maximum_fusion.1), channel_id=1, source_target_pairs={{0,2},{1,3},{2,0},{3,1},{4,6},{5,7},{6,4},{7,5},{8,10},{9,11},{10,... | collective-permute-start | bytes 307208 | tf_op jit(solution)/shard_map/ppermute | solution.py:445
  34.7 4.7 %collective-permute-start.4 = (bf16[400,128]{1,0:T(8,128)(2,1)S(1)}, bf16[400,128]{1,0:T(8,128)(2,1)S(1)}, u32[]{:S(2)}, u32[]{:S(2)}) collective-permute-start(bf16[400,128]{1,0:T(8,128)(2,1)S(1)} %pad_maximum_fusion.2), channel_id=1, source_target_pairs={{0,4},{1,5},{2,6},{3,7},{4,0},{5,1},{6,2},{7,3},{8,12},{9,13},{10,... | collective-permute-start | bytes 307208 | tf_op jit(solution)/shard_map/ppermute | solution.py:445
  39.5 6.7 %collective-permute-start.5 = (bf16[400,128]{1,0:T(8,128)(2,1)S(1)}, bf16[400,128]{1,0:T(8,128)(2,1)S(1)}, u32[]{:S(2)}, u32[]{:S(2)}) collective-permute-start(bf16[400,128]{1,0:T(8,128)(2,1)S(1)} %pad_maximum_fusion.3), channel_id=1, source_target_pairs={{0,8},{1,9},{2,10},{3,11},{4,12},{5,13},{6,14},{7,15},{8,0},{9,1},... | collective-permute-start | bytes 307208 | tf_op jit(solution)/shard_map/ppermute | solution.py:445
  46.3 4.0 %collective-permute-start.6 = (f32[72,128]{1,0:T(8,128)S(1)}, f32[72,128]{1,0:T(8,128)S(1)}, u32[]{:S(2)}, u32[]{:S(2)}) collective-permute-start(f32[72,128]{1,0:T(8,128)S(1)} %fusion.8), channel_id=1, source_target_pairs={{0,16},{1,17},{2,18},{3,19},{4,20},{5,21},{6,22},{7,23},{8,24},{9,... | collective-permute-start | bytes 110600 | tf_op jit(solution)/shard_map/ppermute | solution.py:445
  47.8 2.5 %collective-permute-start.7 = (f32[72,128]{1,0:T(8,128)S(1)}, f32[72,128]{1,0:T(8,128)S(1)}, u32[]{:S(2)}, u32[]{:S(2)}) collective-permute-start(f32[72,128]{1,0:T(8,128)S(1)} %fusion.8), channel_id=1, source_target_pairs={{0,1},{1,0},{2,3},{3,2},{4,5},{5,4},{6,7},{7,6},{8,9},{9,8},{10,11... | collective-permute-start | bytes 110600 | tf_op jit(solution)/shard_map/ppermute | solution.py:445
  47.8 3.4 %collective-permute-start.8 = (f32[72,128]{1,0:T(8,128)S(1)}, f32[72,128]{1,0:T(8,128)S(1)}, u32[]{:S(2)}, u32[]{:S(2)}) collective-permute-start(f32[72,128]{1,0:T(8,128)S(1)} %fusion.8), channel_id=1, source_target_pairs={{0,17},{1,16},{2,19},{3,18},{4,21},{5,20},{6,23},{7,22},{8,25},{9,... | collective-permute-start | bytes 110600 | tf_op jit(solution)/shard_map/ppermute | solution.py:445

commit v6 on v5

--- a/solution.py
+++ b/solution.py
@@ -87,13 +87,13 @@
     return jnp.concatenate([x, jnp.concatenate([jnp.zeros_like(x[:HB]), x[:-HB]], axis=0)], axis=1)
 
 
-def first_layer_columns(a_ref, planes):
+def first_layer_columns(a_ref, planes, skipped=0):
     _, q = iotas((HB, LA))
     times = [one_hot(q // CIN % 8 == t) for t in range(8)]
     blocks = [one_hot(q // EDGE == b) for b in range(BLOCKS)]
     cols = [[] for _ in range(11)]
     for p, j in planes:
-        x = [a_ref[2 * j + kd, INPUT_ROWS[p, kh]] for kd, kh in TAPS]
+        x = [a_ref[2 * j + kd - skipped, INPUT_ROWS[p, kh]] for kd, kh in TAPS]
         edges = [y[ROWS:] for y in x]
         eight = edges[0] * times[0]
         for t in range(1, 8):
@@ -175,7 +175,7 @@
     count = vol_ref.shape[1]
     planes = hh_ref.shape[0]
     d2n = slope_ref.shape[0]
-    copy = pltpu.make_async_copy(a_ref, a_hbm, sem)
+    copy = pltpu.make_async_copy(a_ref.at[2:], a_hbm, sem)
 
     def put_from(first):
         def put(d, v, blocks):
@@ -328,7 +328,7 @@
             hidden = jnp.concatenate([hh_ref[j, 2 if p else 1] for _, j in here], axis=0)
             deltas.append((back * jnp.where(hidden.astype(f32) > 0, 1.0, SLOPE)).astype(bf16))
             planes += here
-    g = dot_tn(jnp.concatenate(deltas, axis=0), first_layer_columns(a_ref, planes))
+    g = dot_tn(jnp.concatenate(deltas, axis=0), first_layer_columns(a_ref, planes, 2))
     before, after = [jnp.zeros((C2, LA), f32)], [jnp.zeros((128 - C2 - 3 * C1, LA), f32)]
 
     def place(taps):
@@ -517,7 +517,7 @@
         forward_kernel,
         "forward",
         [
-            ((planes + 3, 5, ROWS + HB, LA), bf16),
+            ((planes + 1, 5, ROWS + HB, LA), bf16),
             ((d1n + 1, 3, ROWS, LH), bf16),
             ((travelling, 128), bf16),
             ((d2n, ROWS, LZ), bf16),

time: 52.4 us -> 52.4 us (level)
  no operation moved by 1% of the time
where the time goes in v6:
time: 52.4 us; the launch traced here: 52.1 us
  starting transfers between devices  20.6 us (39%)
  Pallas kernels  15.1 us (29%)
  waiting for transfers between devices  15.1 us (29%)
  between operations  0.88 us (2%)
    pallas_call x8, Pallas kernels, call(): pl.pallas_call(kernel, name=name, in_specs=[pl.BlockSpec(memory_space=plt...  15.1 us
    ppermute x7, waiting for transfers between devices, with_partner(): lax.ppermute(block, ('dp', 'space'), [(i, i ^ bit) for i in range(count)])  12.8 us
    ppermute x7, starting transfers between devices, with_partner(): lax.ppermute(block, ('dp', 'space'), [(i, i ^ bit) for i in range(count)])  9.73 us
    all_to_all x1, starting transfers between devices, local(): cot_here = lax.all_to_all(cot_rows, 'space', 0, 0, tiled=True)  7.21 us
    ppermute x2, starting transfers between devices, passed_along(): lax.ppermute(block, 'space', [(i - distance, i) for i in devices if i - d...  3.67 us
    all_to_all x1, waiting for transfers between devices, local(): cot_here = lax.all_to_all(cot_rows, 'space', 0, 0, tiled=True)  2.27 us
  transfers between devices with their start and end apart: 10, of which 7 were waited for; matrix products, arithmetic and copies ran while one was open for 0% of the time, Pallas kernels for 18%

profile of v6, /device:TPU:0, one launch (start us, length us, event | category | flops | bytes accessed | tf_op | source)
XLA Modules:
  0.0 52.1 jit_solution(5535163132172585806)
XLA Ops:
  0.6 2.6 %gather.1 = (bf16[4,8,128,128]{3,2,1,0:T(8,128)(2,1)S(1)}, bf16[16,4,1024]{2,1,0:T(4,128)(2,1)}, bf16[27,4,16]{2,1,0:T(4,128)(2,1)S(1)}, bf16[432,32]{1,0:T(8,128)(2,1)S(1)}) custom-call(bf16[4,8,128,128]{3,2,1,0:T(8,128)(2,1)} %bitcast.46, bf16[32,32,64]{2,1,0:T(8,128)(2,1)} %bitcast.49, bf16[27,4,16]{2,1,0:T(4,128)(2,1)} %bitcast.61, bf16[432,32]{1,0:T(8,128)(2,1)} %bitcast.60), custom_call_target="tpu_custom_call" | custom-call | tf_op jit(solution)/shard_map/gather/pallas_call | solution.py:422
  3.2 2.4 %collective-permute-start = (bf16[4,3,128,128]{3,2,1,0:T(8,128)(2,1)S(1)}, bf16[4,3,128,128]{3,2,1,0:T(8,128)(2,1)S(1)}, u32[]{:S(2)}, u32[]{:S(2)}) collective-permute-start(bf16[4,3,128,128]{3,2,1,0:T(8,128)(2,1)S(1)} %last_planes.1), channel_id=1, source_target_pairs={{0,1},{1,2},{2,3},{3,4},{4,5},{5,6},{6,7},{7,8},{8,9},{9,10},{10,1... | collective-permute-start | bytes 1179656 | tf_op jit(solution)/shard_map/ppermute | solution.py:440
  5.6 7.2 %all-to-all-start = ((bf16[16,4,1024]{2,1,0:T(4,128)(2,1)}), bf16[16,4,1024]{2,1,0:T(4,128)(2,1)S(1)}, u32[]{:S(2)}, u32[]{:S(2)}) async-start(bf16[16,4,1024]{2,1,0:T(4,128)(2,1)} %get-tuple-element.21), calls=%async_computation | async-start | bytes 262144 | tf_op jit(solution)/shard_map/all_to_all | solution.py:514
  12.9 0.0 collective-permute-done.low_ref
  12.9 5.6 %forward.1 = (bf16[9,5,160,128]{3,2,1,0:T(8,128)(2,1)}, bf16[5,3,128,256]{3,2,1,0:T(8,128)(2,1)S(1)}, bf16[512,128]{1,0:T(8,128)(2,1)S(1)}, bf16[2,128,256]{2,1,0:T(8,128)(2,1)S(1)}) custom-call(bf16[4,8,128,128]{3,2,1,0:T(8,128)(2,1)S(1)} %get-tuple-element.16.vol_ref, bf16[4,3,128,128]{3,2,1,0:T(8,128)(2,1)S(1)} %collective-permute-done.low_ref, ...), custom_call_target="tpu_custom_call" | custom-call | tf_op jit(solution)/shard_map/forward/pallas_call | solution.py:422
  18.5 2.3 %all-to-all-done.cot_ref = bf16[16,4,1024]{2,1,0:T(4,128)(2,1)S(1)} async-done(((bf16[16,4,1024]{2,1,0:T(4,128)(2,1)}), bf16[16,4,1024]{2,1,0:T(4,128)(2,1)S(1)}, u32[]{:S(2)}, u32[]{:S(2)}) %all-to-all-start) | async-done | bytes 131104 | tf_op jit(solution)/shard_map/all_to_all | solution.py:514
  20.8 0.2 delta.1.delta_ref
  21.0 1.3 %collective-permute-start.1 = (bf16[128,256]{1,0:T(8,128)(2,1)S(1)}, bf16[128,256]{1,0:T(8,128)(2,1)S(1)}, u32[]{:S(2)}, u32[]{:S(2)}) collective-permute-start(bf16[128,256]{1,0:T(8,128)(2,1)S(1)} %slice_bitcast_fusion), channel_id=1, source_target_pairs={{1,0},{2,1},{3,2},{4,3},{5,4},{6,5},{7,6},{8,7},{9,8},{10,9},{11,1... | collective-permute-start | bytes 196616 | tf_op jit(solution)/shard_map/ppermute | solution.py:440
  22.3 1.9 %second_gradient.1 = (f32[48,384]{1,0:T(8,128)S(1)}, bf16[4608,256]{1,0:T(8,128)(2,1)S(1)}, bf16[9,5,160,128]{3,2,1,0:T(8,128)(2,1)S(1)}) custom-call(bf16[5,3,128,256]{3,2,1,0:T(8,128)(2,1)S(1)} %get-tuple-element.20.hh_ref, bf16[2,128,256]{2,1,0:T(8,128)(2,1)S(1)} %delta.1.delta_ref, bf16[432,32]{1,0:T(8,128)(2,1)S(1)} %get-tuple-element.18.k2_ref, ...), custom_call_target="tpu_custom_call" | custom-call | tf_op jit(solution)/shard_map/second_gradient/pallas_call | solution.py:422
  24.2 0.0 collective-permute-done.1.next_ref
  24.2 2.2 %first_gradient.1 = f32[144,128]{1,0:T(8,128)S(1)} custom-call(bf16[5,3,128,256]{3,2,1,0:T(8,128)(2,1)S(1)} %get-tuple-element.20.hh_ref, bf16[2,128,256]{2,1,0:T(8,128)(2,1)S(1)} %delta.1.delta_ref, bf16[128,256]{1,0:T(8,128)(2,1)S(1)} %collective-permute-done.1.next_ref, bf16[4608,256]{1,0:T(8,128)(2,1)S(1)} %get-tuple-element.24.t2b_ref, ...), custom_call_target="tpu_custom_call" | custom-call | tf_op jit(solution)/shard_map/first_gradient/pallas_call | solution.py:422
  26.5 1.7 %collective-permute-start.2 = (bf16[400,128]{1,0:T(8,128)(2,1)S(1)}, bf16[400,128]{1,0:T(8,128)(2,1)S(1)}, u32[]{:S(2)}, u32[]{:S(2)}) collective-permute-start(bf16[400,128]{1,0:T(8,128)(2,1)S(1)} %pad_maximum_fusion), channel_id=1, source_target_pairs={{0,1},{1,0},{2,3},{3,2},{4,5},{5,4},{6,7},{7,6},{8,9},{9,8},{10,11... | collective-permute-start | bytes 307208 | tf_op jit(solution)/shard_map/ppermute | solution.py:445
  28.3 0.9 %collective-permute-done.2 = bf16[400,128]{1,0:T(8,128)(2,1)S(1)} collective-permute-done((bf16[400,128]{1,0:T(8,128)(2,1)S(1)}, bf16[400,128]{1,0:T(8,128)(2,1)S(1)}, u32[]{:S(2)}, u32[]{:S(2)}) %collective-permute-start.2) | collective-permute-done | bytes 102432 | tf_op jit(solution)/shard_map/ppermute | solution.py:445
  29.4 1.7 %collective-permute-start.3 = (bf16[400,128]{1,0:T(8,128)(2,1)S(1)}, bf16[400,128]{1,0:T(8,128)(2,1)S(1)}, u32[]{:S(2)}, u32[]{:S(2)}) collective-permute-start(bf16[400,128]{1,0:T(8,128)(2,1)S(1)} %pad_maximum_fusion.1), channel_id=1, source_target_pairs={{0,2},{1,3},{2,0},{3,1},{4,6},{5,7},{6,4},{7,5},{8,10},{9,11},{10,... | collective-permute-start | bytes 307208 | tf_op jit(solution)/shard_map/ppermute | solution.py:445
  31.1 3.5 %collective-permute-done.3 = bf16[400,128]{1,0:T(8,128)(2,1)S(1)} collective-permute-done((bf16[400,128]{1,0:T(8,128)(2,1)S(1)}, bf16[400,128]{1,0:T(8,128)(2,1)S(1)}, u32[]{:S(2)}, u32[]{:S(2)}) %collective-permute-start.3) | collective-permute-done | bytes 102432 | tf_op jit(solution)/shard_map/ppermute | solution.py:445
  34.7 1.5 %collective-permute-start.4 = (bf16[400,128]{1,0:T(8,128)(2,1)S(1)}, bf16[400,128]{1,0:T(8,128)(2,1)S(1)}, u32[]{:S(2)}, u32[]{:S(2)}) collective-permute-start(bf16[400,128]{1,0:T(8,128)(2,1)S(1)} %pad_maximum_fusion.2), channel_id=1, source_target_pairs={{0,4},{1,5},{2,6},{3,7},{4,0},{5,1},{6,2},{7,3},{8,12},{9,13},{10,... | collective-permute-start | bytes 307208 | tf_op jit(solution)/shard_map/ppermute | solution.py:445
  36.2 3.2 %collective-permute-done.4 = bf16[400,128]{1,0:T(8,128)(2,1)S(1)} collective-permute-done((bf16[400,128]{1,0:T(8,128)(2,1)S(1)}, bf16[400,128]{1,0:T(8,128)(2,1)S(1)}, u32[]{:S(2)}, u32[]{:S(2)}) %collective-permute-start.4) | collective-permute-done | bytes 102432 | tf_op jit(solution)/shard_map/ppermute | solution.py:445
  39.5 2.5 %collective-permute-start.5 = (bf16[400,128]{1,0:T(8,128)(2,1)S(1)}, bf16[400,128]{1,0:T(8,128)(2,1)S(1)}, u32[]{:S(2)}, u32[]{:S(2)}) collective-permute-start(bf16[400,128]{1,0:T(8,128)(2,1)S(1)} %pad_maximum_fusion.3), channel_id=1, source_target_pairs={{0,8},{1,9},{2,10},{3,11},{4,12},{5,13},{6,14},{7,15},{8,0},{9,1},... | collective-permute-start | bytes 307208 | tf_op jit(solution)/shard_map/ppermute | solution.py:445
  42.1 4.2 %collective-permute-done.5 = bf16[400,128]{1,0:T(8,128)(2,1)S(1)} collective-permute-done((bf16[400,128]{1,0:T(8,128)(2,1)S(1)}, bf16[400,128]{1,0:T(8,128)(2,1)S(1)}, u32[]{:S(2)}, u32[]{:S(2)}) %collective-permute-start.5) | collective-permute-done | bytes 102432 | tf_op jit(solution)/shard_map/ppermute | solution.py:445
  46.3 1.6 %collective-permute-start.6 = (f32[72,128]{1,0:T(8,128)S(1)}, f32[72,128]{1,0:T(8,128)S(1)}, u32[]{:S(2)}, u32[]{:S(2)}) collective-permute-start(f32[72,128]{1,0:T(8,128)S(1)} %fusion.8), channel_id=1, source_target_pairs={{0,16},{1,17},{2,18},{3,19},{4,20},{5,21},{6,22},{7,23},{8,24},{9,... | collective-permute-start | bytes 110600 | tf_op jit(solution)/shard_map/ppermute | solution.py:445
  47.8 0.0 collective-permute-start.7
  47.8 0.6 %collective-permute-start.8 = (f32[72,128]{1,0:T(8,128)S(1)}, f32[72,128]{1,0:T(8,128)S(1)}, u32[]{:S(2)}, u32[]{:S(2)}) collective-permute-start(f32[72,128]{1,0:T(8,128)S(1)} %fusion.8), channel_id=1, source_target_pairs={{0,17},{1,16},{2,19},{3,18},{4,21},{5,20},{6,23},{7,22},{8,25},{9,... | collective-permute-start | bytes 110600 | tf_op jit(solution)/shard_map/ppermute | solution.py:445
  48.5 1.7 %scatter.1 = bf16[32,32,64]{2,1,0:T(8,128)(2,1)} custom-call(bf16[512,128]{1,0:T(8,128)(2,1)S(1)} %bitcast.44), custom_call_target="tpu_custom_call" | custom-call | tf_op jit(solution)/shard_map/scatter/pallas_call | solution.py:422
  50.2 0.1 collective-permute-done.6
  50.3 0.0 collective-permute-done.7
  50.3 0.9 %collective-permute-done.8 = f32[72,128]{1,0:T(8,128)S(1)} collective-permute-done((f32[72,128]{1,0:T(8,128)S(1)}, f32[72,128]{1,0:T(8,128)S(1)}, u32[]{:S(2)}, u32[]{:S(2)}) %collective-permute-start.8) | collective-permute-done | bytes 36896 | tf_op jit(solution)/shard_map/ppermute | solution.py:445
  51.2 0.8 %scale.1 = (f32[27,4,16]{2,1,0:T(4,128)}, f32[27,16,32]{2,1,0:T(8,128)}) custom-call(f32[144,128]{1,0:T(8,128)S(1)} %maximum_select_fusion.4.sum_ref), custom_call_target="tpu_custom_call" | custom-call | tf_op jit(solution)/shard_map/scale/pallas_call | solution.py:422
  (31 shorter events, 0.4 us)
Async XLA Ops:
  3.2 9.6 %collective-permute-start = (bf16[4,3,128,128]{3,2,1,0:T(8,128)(2,1)S(1)}, bf16[4,3,128,128]{3,2,1,0:T(8,128)(2,1)S(1)}, u32[]{:S(2)}, u32[]{:S(2)}) collective-permute-start(bf16[4,3,128,128]{3,2,1,0:T(8,128)(2,1)S(1)} %last_planes.1), channel_id=1, source_target_pairs={{0,1},{1,2},{2,3},{3,4},{4,5},{5,6},{6,7},{7,8},{8,9},{9,10},{10,1... | collective-permute-start | bytes 1179656 | tf_op jit(solution)/shard_map/ppermute | solution.py:440
  5.6 15.2 %all-to-all-start = ((bf16[16,4,1024]{2,1,0:T(4,128)(2,1)}), bf16[16,4,1024]{2,1,0:T(4,128)(2,1)S(1)}, u32[]{:S(2)}, u32[]{:S(2)}) async-start(bf16[16,4,1024]{2,1,0:T(4,128)(2,1)} %get-tuple-element.21), calls=%async_computation | async-start | bytes 262144 | tf_op jit(solution)/shard_map/all_to_all | solution.py:514
  21.0 3.2 %collective-permute-start.1 = (bf16[128,256]{1,0:T(8,128)(2,1)S(1)}, bf16[128,256]{1,0:T(8,128)(2,1)S(1)}, u32[]{:S(2)}, u32[]{:S(2)}) collective-permute-start(bf16[128,256]{1,0:T(8,128)(2,1)S(1)} %slice_bitcast_fusion), channel_id=1, source_target_pairs={{1,0},{2,1},{3,2},{4,3},{5,4},{6,5},{7,6},{8,7},{9,8},{10,9},{11,1... | collective-permute-start | bytes 196616 | tf_op jit(solution)/shard_map/ppermute | solution.py:440
  26.5 2.7 %collective-permute-start.2 = (bf16[400,128]{1,0:T(8,128)(2,1)S(1)}, bf16[400,128]{1,0:T(8,128)(2,1)S(1)}, u32[]{:S(2)}, u32[]{:S(2)}) collective-permute-start(bf16[400,128]{1,0:T(8,128)(2,1)S(1)} %pad_maximum_fusion), channel_id=1, source_target_pairs={{0,1},{1,0},{2,3},{3,2},{4,5},{5,4},{6,7},{7,6},{8,9},{9,8},{10,11... | collective-permute-start | bytes 307208 | tf_op jit(solution)/shard_map/ppermute | solution.py:445
  29.4 5.2 %collective-permute-start.3 = (bf16[400,128]{1,0:T(8,128)(2,1)S(1)}, bf16[400,128]{1,0:T(8,128)(2,1)S(1)}, u32[]{:S(2)}, u32[]{:S(2)}) collective-permute-start(bf16[400,128]{1,0:T(8,128)(2,1)S(1)} %pad_maximum_fusion.1), channel_id=1, source_target_pairs={{0,2},{1,3},{2,0},{3,1},{4,6},{5,7},{6,4},{7,5},{8,10},{9,11},{10,... | collective-permute-start | bytes 307208 | tf_op jit(solution)/shard_map/ppermute | solution.py:445
  34.7 4.7 %collective-permute-start.4 = (bf16[400,128]{1,0:T(8,128)(2,1)S(1)}, bf16[400,128]{1,0:T(8,128)(2,1)S(1)}, u32[]{:S(2)}, u32[]{:S(2)}) collective-permute-start(bf16[400,128]{1,0:T(8,128)(2,1)S(1)} %pad_maximum_fusion.2), channel_id=1, source_target_pairs={{0,4},{1,5},{2,6},{3,7},{4,0},{5,1},{6,2},{7,3},{8,12},{9,13},{10,... | collective-permute-start | bytes 307208 | tf_op jit(solution)/shard_map/ppermute | solution.py:445
  39.5 6.7 %collective-permute-start.5 = (bf16[400,128]{1,0:T(8,128)(2,1)S(1)}, bf16[400,128]{1,0:T(8,128)(2,1)S(1)}, u32[]{:S(2)}, u32[]{:S(2)}) collective-permute-start(bf16[400,128]{1,0:T(8,128)(2,1)S(1)} %pad_maximum_fusion.3), channel_id=1, source_target_pairs={{0,8},{1,9},{2,10},{3,11},{4,12},{5,13},{6,14},{7,15},{8,0},{9,1},... | collective-permute-start | bytes 307208 | tf_op jit(solution)/shard_map/ppermute | solution.py:445
  46.3 4.0 %collective-permute-start.6 = (f32[72,128]{1,0:T(8,128)S(1)}, f32[72,128]{1,0:T(8,128)S(1)}, u32[]{:S(2)}, u32[]{:S(2)}) collective-permute-start(f32[72,128]{1,0:T(8,128)S(1)} %fusion.8), channel_id=1, source_target_pairs={{0,16},{1,17},{2,18},{3,19},{4,20},{5,21},{6,22},{7,23},{8,24},{9,... | collective-permute-start | bytes 110600 | tf_op jit(solution)/shard_map/ppermute | solution.py:445
  47.8 2.5 %collective-permute-start.7 = (f32[72,128]{1,0:T(8,128)S(1)}, f32[72,128]{1,0:T(8,128)S(1)}, u32[]{:S(2)}, u32[]{:S(2)}) collective-permute-start(f32[72,128]{1,0:T(8,128)S(1)} %fusion.8), channel_id=1, source_target_pairs={{0,1},{1,0},{2,3},{3,2},{4,5},{5,4},{6,7},{7,6},{8,9},{9,8},{10,11... | collective-permute-start | bytes 110600 | tf_op jit(solution)/shard_map/ppermute | solution.py:445
  47.8 3.4 %collective-permute-start.8 = (f32[72,128]{1,0:T(8,128)S(1)}, f32[72,128]{1,0:T(8,128)S(1)}, u32[]{:S(2)}, u32[]{:S(2)}) collective-permute-start(f32[72,128]{1,0:T(8,128)S(1)} %fusion.8), channel_id=1, source_target_pairs={{0,17},{1,16},{2,19},{3,18},{4,21},{5,20},{6,23},{7,22},{8,25},{9,... | collective-permute-start | bytes 110600 | tf_op jit(solution)/shard_map/ppermute | solution.py:445

commit v7 on v5

--- a/solution.py
+++ b/solution.py
@@ -39,7 +39,7 @@
 def exact_nt(a, b):
     a = a.astype(bf16)
     total = None
-    for _ in range(3):
+    for _ in range(2):
         part = b.astype(bf16)
         b = b - part.astype(f32)
         total = dot_nt(a, part) if total is None else total + dot_nt(a, part)

time: 52.4 us -> 52.3 us (level)
  no operation moved by 1% of the time
where the time goes in v7:
time: 52.3 us; the launch traced here: 52 us
  starting transfers between devices  20.7 us (40%)
  waiting for transfers between devices  15.1 us (29%)
  Pallas kernels  14.9 us (28%)
  between operations  0.88 us (2%)
    pallas_call x8, Pallas kernels, call(): pl.pallas_call(kernel, name=name, in_specs=[pl.BlockSpec(memory_space=plt...  14.9 us
    ppermute x7, waiting for transfers between devices, with_partner(): lax.ppermute(block, ('dp', 'space'), [(i, i ^ bit) for i in range(count)])  12.8 us
    ppermute x7, starting transfers between devices, with_partner(): lax.ppermute(block, ('dp', 'space'), [(i, i ^ bit) for i in range(count)])  9.78 us
    all_to_all x1, starting transfers between devices, local(): cot_here = lax.all_to_all(cot_rows, 'space', 0, 0, tiled=True)  7.21 us
    ppermute x2, starting transfers between devices, passed_along(): lax.ppermute(block, 'space', [(i - distance, i) for i in devices if i - d...  3.67 us
    all_to_all x1, waiting for transfers between devices, local(): cot_here = lax.all_to_all(cot_rows, 'space', 0, 0, tiled=True)  2.27 us
  transfers between devices with their start and end apart: 10, of which 7 were waited for; matrix products, arithmetic and copies ran while one was open for 0% of the time, Pallas kernels for 18%

profile of v7, /device:TPU:0, one launch (start us, length us, event | category | flops | bytes accessed | tf_op | source)
XLA Modules:
  0.0 52.0 jit_solution(18230253632183664399)
XLA Ops:
  0.6 2.6 %gather.1 = (bf16[4,8,128,128]{3,2,1,0:T(8,128)(2,1)S(1)}, bf16[16,4,1024]{2,1,0:T(4,128)(2,1)}, bf16[27,4,16]{2,1,0:T(4,128)(2,1)S(1)}, bf16[432,32]{1,0:T(8,128)(2,1)S(1)}) custom-call(bf16[4,8,128,128]{3,2,1,0:T(8,128)(2,1)} %bitcast.46, bf16[32,32,64]{2,1,0:T(8,128)(2,1)} %bitcast.49, bf16[27,4,16]{2,1,0:T(4,128)(2,1)} %bitcast.61, bf16[432,32]{1,0:T(8,128)(2,1)} %bitcast.60), custom_call_target="tpu_custom_call" | custom-call | tf_op jit(solution)/shard_map/gather/pallas_call | solution.py:422
  3.2 2.4 %collective-permute-start = (bf16[4,3,128,128]{3,2,1,0:T(8,128)(2,1)S(1)}, bf16[4,3,128,128]{3,2,1,0:T(8,128)(2,1)S(1)}, u32[]{:S(2)}, u32[]{:S(2)}) collective-permute-start(bf16[4,3,128,128]{3,2,1,0:T(8,128)(2,1)S(1)} %last_planes.1), channel_id=1, source_target_pairs={{0,1},{1,2},{2,3},{3,4},{4,5},{5,6},{6,7},{7,8},{8,9},{9,10},{10,1... | collective-permute-start | bytes 1179656 | tf_op jit(solution)/shard_map/ppermute | solution.py:440
  5.6 7.2 %all-to-all-start = ((bf16[16,4,1024]{2,1,0:T(4,128)(2,1)}), bf16[16,4,1024]{2,1,0:T(4,128)(2,1)S(1)}, u32[]{:S(2)}, u32[]{:S(2)}) async-start(bf16[16,4,1024]{2,1,0:T(4,128)(2,1)} %get-tuple-element.21), calls=%async_computation | async-start | bytes 262144 | tf_op jit(solution)/shard_map/all_to_all | solution.py:514
  12.9 0.0 collective-permute-done.low_ref
  12.9 5.6 %forward.1 = (bf16[11,5,160,128]{3,2,1,0:T(8,128)(2,1)}, bf16[5,3,128,256]{3,2,1,0:T(8,128)(2,1)S(1)}, bf16[512,128]{1,0:T(8,128)(2,1)S(1)}, bf16[2,128,256]{2,1,0:T(8,128)(2,1)S(1)}) custom-call(bf16[4,8,128,128]{3,2,1,0:T(8,128)(2,1)S(1)} %get-tuple-element.16.vol_ref, bf16[4,3,128,128]{3,2,1,0:T(8,128)(2,1)S(1)} %collective-permute-done.low_ref, ...), custom_call_target="tpu_custom_call" | custom-call | tf_op jit(solution)/shard_map/forward/pallas_call | solution.py:422
  18.5 2.3 %all-to-all-done.cot_ref = bf16[16,4,1024]{2,1,0:T(4,128)(2,1)S(1)} async-done(((bf16[16,4,1024]{2,1,0:T(4,128)(2,1)}), bf16[16,4,1024]{2,1,0:T(4,128)(2,1)S(1)}, u32[]{:S(2)}, u32[]{:S(2)}) %all-to-all-start) | async-done | bytes 131104 | tf_op jit(solution)/shard_map/all_to_all | solution.py:514
  20.8 0.2 delta.1.delta_ref
  21.0 1.3 %collective-permute-start.1 = (bf16[128,256]{1,0:T(8,128)(2,1)S(1)}, bf16[128,256]{1,0:T(8,128)(2,1)S(1)}, u32[]{:S(2)}, u32[]{:S(2)}) collective-permute-start(bf16[128,256]{1,0:T(8,128)(2,1)S(1)} %slice_bitcast_fusion), channel_id=1, source_target_pairs={{1,0},{2,1},{3,2},{4,3},{5,4},{6,5},{7,6},{8,7},{9,8},{10,9},{11,1... | collective-permute-start | bytes 196616 | tf_op jit(solution)/shard_map/ppermute | solution.py:440
  22.3 1.9 %second_gradient.1 = (f32[48,384]{1,0:T(8,128)S(1)}, bf16[4608,256]{1,0:T(8,128)(2,1)S(1)}, bf16[11,5,160,128]{3,2,1,0:T(8,128)(2,1)S(1)}) custom-call(bf16[5,3,128,256]{3,2,1,0:T(8,128)(2,1)S(1)} %get-tuple-element.20.hh_ref, bf16[2,128,256]{2,1,0:T(8,128)(2,1)S(1)} %delta.1.delta_ref, bf16[432,32]{1,0:T(8,128)(2,1)S(1)} %get-tuple-element.18.k2_ref, ...), custom_call_target="tpu_custom_call" | custom-call | tf_op jit(solution)/shard_map/second_gradient/pallas_call | solution.py:422
  24.2 0.0 collective-permute-done.1.next_ref
  24.2 2.1 %first_gradient.1 = f32[144,128]{1,0:T(8,128)S(1)} custom-call(bf16[5,3,128,256]{3,2,1,0:T(8,128)(2,1)S(1)} %get-tuple-element.20.hh_ref, bf16[2,128,256]{2,1,0:T(8,128)(2,1)S(1)} %delta.1.delta_ref, bf16[128,256]{1,0:T(8,128)(2,1)S(1)} %collective-permute-done.1.next_ref, bf16[4608,256]{1,0:T(8,128)(2,1)S(1)} %get-tuple-element.24.t2b_ref, ...), custom_call_target="tpu_custom_call" | custom-call | tf_op jit(solution)/shard_map/first_gradient/pallas_call | solution.py:422
  26.4 1.8 %collective-permute-start.2 = (bf16[400,128]{1,0:T(8,128)(2,1)S(1)}, bf16[400,128]{1,0:T(8,128)(2,1)S(1)}, u32[]{:S(2)}, u32[]{:S(2)}) collective-permute-start(bf16[400,128]{1,0:T(8,128)(2,1)S(1)} %pad_maximum_fusion), channel_id=1, source_target_pairs={{0,1},{1,0},{2,3},{3,2},{4,5},{5,4},{6,7},{7,6},{8,9},{9,8},{10,11... | collective-permute-start | bytes 307208 | tf_op jit(solution)/shard_map/ppermute | solution.py:445
  28.2 0.9 %collective-permute-done.2 = bf16[400,128]{1,0:T(8,128)(2,1)S(1)} collective-permute-done((bf16[400,128]{1,0:T(8,128)(2,1)S(1)}, bf16[400,128]{1,0:T(8,128)(2,1)S(1)}, u32[]{:S(2)}, u32[]{:S(2)}) %collective-permute-start.2) | collective-permute-done | bytes 102432 | tf_op jit(solution)/shard_map/ppermute | solution.py:445
  29.3 1.7 %collective-permute-start.3 = (bf16[400,128]{1,0:T(8,128)(2,1)S(1)}, bf16[400,128]{1,0:T(8,128)(2,1)S(1)}, u32[]{:S(2)}, u32[]{:S(2)}) collective-permute-start(bf16[400,128]{1,0:T(8,128)(2,1)S(1)} %pad_maximum_fusion.1), channel_id=1, source_target_pairs={{0,2},{1,3},{2,0},{3,1},{4,6},{5,7},{6,4},{7,5},{8,10},{9,11},{10,... | collective-permute-start | bytes 307208 | tf_op jit(solution)/shard_map/ppermute | solution.py:445
  31.0 3.5 %collective-permute-done.3 = bf16[400,128]{1,0:T(8,128)(2,1)S(1)} collective-permute-done((bf16[400,128]{1,0:T(8,128)(2,1)S(1)}, bf16[400,128]{1,0:T(8,128)(2,1)S(1)}, u32[]{:S(2)}, u32[]{:S(2)}) %collective-permute-start.3) | collective-permute-done | bytes 102432 | tf_op jit(solution)/shard_map/ppermute | solution.py:445
  34.6 1.5 %collective-permute-start.4 = (bf16[400,128]{1,0:T(8,128)(2,1)S(1)}, bf16[400,128]{1,0:T(8,128)(2,1)S(1)}, u32[]{:S(2)}, u32[]{:S(2)}) collective-permute-start(bf16[400,128]{1,0:T(8,128)(2,1)S(1)} %pad_maximum_fusion.2), channel_id=1, source_target_pairs={{0,4},{1,5},{2,6},{3,7},{4,0},{5,1},{6,2},{7,3},{8,12},{9,13},{10,... | collective-permute-start | bytes 307208 | tf_op jit(solution)/shard_map/ppermute | solution.py:445
  36.2 3.2 %collective-permute-done.4 = bf16[400,128]{1,0:T(8,128)(2,1)S(1)} collective-permute-done((bf16[400,128]{1,0:T(8,128)(2,1)S(1)}, bf16[400,128]{1,0:T(8,128)(2,1)S(1)}, u32[]{:S(2)}, u32[]{:S(2)}) %collective-permute-start.4) | collective-permute-done | bytes 102432 | tf_op jit(solution)/shard_map/ppermute | solution.py:445
  39.4 2.5 %collective-permute-start.5 = (bf16[400,128]{1,0:T(8,128)(2,1)S(1)}, bf16[400,128]{1,0:T(8,128)(2,1)S(1)}, u32[]{:S(2)}, u32[]{:S(2)}) collective-permute-start(bf16[400,128]{1,0:T(8,128)(2,1)S(1)} %pad_maximum_fusion.3), channel_id=1, source_target_pairs={{0,8},{1,9},{2,10},{3,11},{4,12},{5,13},{6,14},{7,15},{8,0},{9,1},... | collective-permute-start | bytes 307208 | tf_op jit(solution)/shard_map/ppermute | solution.py:445
  42.0 4.2 %collective-permute-done.5 = bf16[400,128]{1,0:T(8,128)(2,1)S(1)} collective-permute-done((bf16[400,128]{1,0:T(8,128)(2,1)S(1)}, bf16[400,128]{1,0:T(8,128)(2,1)S(1)}, u32[]{:S(2)}, u32[]{:S(2)}) %collective-permute-start.5) | collective-permute-done | bytes 102432 | tf_op jit(solution)/shard_map/ppermute | solution.py:445
  46.2 1.6 %collective-permute-start.6 = (f32[72,128]{1,0:T(8,128)S(1)}, f32[72,128]{1,0:T(8,128)S(1)}, u32[]{:S(2)}, u32[]{:S(2)}) collective-permute-start(f32[72,128]{1,0:T(8,128)S(1)} %fusion.8), channel_id=1, source_target_pairs={{0,16},{1,17},{2,18},{3,19},{4,20},{5,21},{6,22},{7,23},{8,24},{9,... | collective-permute-start | bytes 110600 | tf_op jit(solution)/shard_map/ppermute | solution.py:445
  47.7 0.0 collective-permute-start.7
  47.7 0.6 %collective-permute-start.8 = (f32[72,128]{1,0:T(8,128)S(1)}, f32[72,128]{1,0:T(8,128)S(1)}, u32[]{:S(2)}, u32[]{:S(2)}) collective-permute-start(f32[72,128]{1,0:T(8,128)S(1)} %fusion.8), channel_id=1, source_target_pairs={{0,17},{1,16},{2,19},{3,18},{4,21},{5,20},{6,23},{7,22},{8,25},{9,... | collective-permute-start | bytes 110600 | tf_op jit(solution)/shard_map/ppermute | solution.py:445
  48.4 1.7 %scatter.1 = bf16[32,32,64]{2,1,0:T(8,128)(2,1)} custom-call(bf16[512,128]{1,0:T(8,128)(2,1)S(1)} %bitcast.44), custom_call_target="tpu_custom_call" | custom-call | tf_op jit(solution)/shard_map/scatter/pallas_call | solution.py:422
  50.1 0.1 collective-permute-done.6
  50.2 0.0 collective-permute-done.7
  50.2 0.9 %collective-permute-done.8 = f32[72,128]{1,0:T(8,128)S(1)} collective-permute-done((f32[72,128]{1,0:T(8,128)S(1)}, f32[72,128]{1,0:T(8,128)S(1)}, u32[]{:S(2)}, u32[]{:S(2)}) %collective-permute-start.8) | collective-permute-done | bytes 36896 | tf_op jit(solution)/shard_map/ppermute | solution.py:445
  51.1 0.8 %scale.1 = (f32[27,4,16]{2,1,0:T(4,128)}, f32[27,16,32]{2,1,0:T(8,128)}) custom-call(f32[144,128]{1,0:T(8,128)S(1)} %maximum_select_fusion.4.sum_ref), custom_call_target="tpu_custom_call" | custom-call | tf_op jit(solution)/shard_map/scale/pallas_call | solution.py:422
  (31 shorter events, 0.4 us)
Async XLA Ops:
  3.2 9.6 %collective-permute-start = (bf16[4,3,128,128]{3,2,1,0:T(8,128)(2,1)S(1)}, bf16[4,3,128,128]{3,2,1,0:T(8,128)(2,1)S(1)}, u32[]{:S(2)}, u32[]{:S(2)}) collective-permute-start(bf16[4,3,128,128]{3,2,1,0:T(8,128)(2,1)S(1)} %last_planes.1), channel_id=1, source_target_pairs={{0,1},{1,2},{2,3},{3,4},{4,5},{5,6},{6,7},{7,8},{8,9},{9,10},{10,1... | collective-permute-start | bytes 1179656 | tf_op jit(solution)/shard_map/ppermute | solution.py:440
  5.6 15.2 %all-to-all-start = ((bf16[16,4,1024]{2,1,0:T(4,128)(2,1)}), bf16[16,4,1024]{2,1,0:T(4,128)(2,1)S(1)}, u32[]{:S(2)}, u32[]{:S(2)}) async-start(bf16[16,4,1024]{2,1,0:T(4,128)(2,1)} %get-tuple-element.21), calls=%async_computation | async-start | bytes 262144 | tf_op jit(solution)/shard_map/all_to_all | solution.py:514
  21.0 3.2 %collective-permute-start.1 = (bf16[128,256]{1,0:T(8,128)(2,1)S(1)}, bf16[128,256]{1,0:T(8,128)(2,1)S(1)}, u32[]{:S(2)}, u32[]{:S(2)}) collective-permute-start(bf16[128,256]{1,0:T(8,128)(2,1)S(1)} %slice_bitcast_fusion), channel_id=1, source_target_pairs={{1,0},{2,1},{3,2},{4,3},{5,4},{6,5},{7,6},{8,7},{9,8},{10,9},{11,1... | collective-permute-start | bytes 196616 | tf_op jit(solution)/shard_map/ppermute | solution.py:440
  26.4 2.7 %collective-permute-start.2 = (bf16[400,128]{1,0:T(8,128)(2,1)S(1)}, bf16[400,128]{1,0:T(8,128)(2,1)S(1)}, u32[]{:S(2)}, u32[]{:S(2)}) collective-permute-start(bf16[400,128]{1,0:T(8,128)(2,1)S(1)} %pad_maximum_fusion), channel_id=1, source_target_pairs={{0,1},{1,0},{2,3},{3,2},{4,5},{5,4},{6,7},{7,6},{8,9},{9,8},{10,11... | collective-permute-start | bytes 307208 | tf_op jit(solution)/shard_map/ppermute | solution.py:445
  29.3 5.2 %collective-permute-start.3 = (bf16[400,128]{1,0:T(8,128)(2,1)S(1)}, bf16[400,128]{1,0:T(8,128)(2,1)S(1)}, u32[]{:S(2)}, u32[]{:S(2)}) collective-permute-start(bf16[400,128]{1,0:T(8,128)(2,1)S(1)} %pad_maximum_fusion.1), channel_id=1, source_target_pairs={{0,2},{1,3},{2,0},{3,1},{4,6},{5,7},{6,4},{7,5},{8,10},{9,11},{10,... | collective-permute-start | bytes 307208 | tf_op jit(solution)/shard_map/ppermute | solution.py:445
  34.6 4.7 %collective-permute-start.4 = (bf16[400,128]{1,0:T(8,128)(2,1)S(1)}, bf16[400,128]{1,0:T(8,128)(2,1)S(1)}, u32[]{:S(2)}, u32[]{:S(2)}) collective-permute-start(bf16[400,128]{1,0:T(8,128)(2,1)S(1)} %pad_maximum_fusion.2), channel_id=1, source_target_pairs={{0,4},{1,5},{2,6},{3,7},{4,0},{5,1},{6,2},{7,3},{8,12},{9,13},{10,... | collective-permute-start | bytes 307208 | tf_op jit(solution)/shard_map/ppermute | solution.py:445
  39.4 6.7 %collective-permute-start.5 = (bf16[400,128]{1,0:T(8,128)(2,1)S(1)}, bf16[400,128]{1,0:T(8,128)(2,1)S(1)}, u32[]{:S(2)}, u32[]{:S(2)}) collective-permute-start(bf16[400,128]{1,0:T(8,128)(2,1)S(1)} %pad_maximum_fusion.3), channel_id=1, source_target_pairs={{0,8},{1,9},{2,10},{3,11},{4,12},{5,13},{6,14},{7,15},{8,0},{9,1},... | collective-permute-start | bytes 307208 | tf_op jit(solution)/shard_map/ppermute | solution.py:445
  46.2 4.0 %collective-permute-start.6 = (f32[72,128]{1,0:T(8,128)S(1)}, f32[72,128]{1,0:T(8,128)S(1)}, u32[]{:S(2)}, u32[]{:S(2)}) collective-permute-start(f32[72,128]{1,0:T(8,128)S(1)} %fusion.8), channel_id=1, source_target_pairs={{0,16},{1,17},{2,18},{3,19},{4,20},{5,21},{6,22},{7,23},{8,24},{9,... | collective-permute-start | bytes 110600 | tf_op jit(solution)/shard_map/ppermute | solution.py:445
  47.7 2.5 %collective-permute-start.7 = (f32[72,128]{1,0:T(8,128)S(1)}, f32[72,128]{1,0:T(8,128)S(1)}, u32[]{:S(2)}, u32[]{:S(2)}) collective-permute-start(f32[72,128]{1,0:T(8,128)S(1)} %fusion.8), channel_id=1, source_target_pairs={{0,1},{1,0},{2,3},{3,2},{4,5},{5,4},{6,7},{7,6},{8,9},{9,8},{10,11... | collective-permute-start | bytes 110600 | tf_op jit(solution)/shard_map/ppermute | solution.py:445
  47.7 3.4 %collective-permute-start.8 = (f32[72,128]{1,0:T(8,128)S(1)}, f32[72,128]{1,0:T(8,128)S(1)}, u32[]{:S(2)}, u32[]{:S(2)}) collective-permute-start(f32[72,128]{1,0:T(8,128)S(1)} %fusion.8), channel_id=1, source_target_pairs={{0,17},{1,16},{2,19},{3,18},{4,21},{5,20},{6,23},{7,22},{8,25},{9,... | collective-permute-start | bytes 110600 | tf_op jit(solution)/shard_map/ppermute | solution.py:445
